TPU v7x, 128 devices: a whole 4x4x4 slice. The times are simulated.
128 devices in a mesh: sample: 8 (over x, core), gene: 4 (over y), cohort: 4 (over z).
Axes of the slice: x: 4, y: 4, z: 4, core: 2. Of those that a mesh axis runs over, the one named last changes fastest.
Arguments:
- dosage: bfloat16 [16384, 32768], P(('sample', 'cohort'), 'gene'), may hold values from 0 to 2
- covariates: bfloat16 [16384, 32], P(('sample', 'cohort')), may hold values from 0 to 2
- phenotype: bfloat16 [16384], P(('sample', 'cohort')), may hold values from -6 to 6
- sample_mask: int32 [16384], P(('sample', 'cohort')), may hold values 0 or 1
- variant_weight: float32 [32768], replicated, may hold values from 0.1 to 1
- bucket_owner: int32 [256], replicated, may hold values from 0 to 15, as said below
- variant_gene: int32 [32768], replicated, may hold values from -1 to 127, as said below
Outputs:
- gram_tiles: float32 [16, 16, 128, 128], P(('gene', 'cohort'), 'sample')
- rho_stats: float32 [8, 128], P(None, ('gene', 'cohort'))
- gene_trace: float32 [128], P(('gene', 'cohort'))
Inputs may be any that keep to these rules, and one draw needn't show every extreme that they name: `bucket_owner`: every owner holds exactly 16 buckets, at most 8 of them among the 64 buckets of one index of gene, and some owner exactly 8; of the buckets of one index of gene, exactly 16 belong to owners whose index leaves a given remainder on division by the size of the cohort axis. `variant_gene`: genes o * 8 to (o + 1) * 8 - 1 lie in the buckets of owner o, each in one or more whole buckets that are consecutive among that owner's buckets; all its buckets are full but its last, whose first 10 to 128 columns are live and the rest -1.
All inputs are finite; a program needn't handle non-finite values. No bound on the sum of `sample_mask` on one device may be relied on, other than what follows from the above.
Results may differ from a plain program's by a relative error of at most 0.0003.
Values may be sent and summed in bfloat16 or wider, within the bound.
No kernel may reach another device: no remote copies, remote signals or barrier semaphores. Data moves between devices by JAX's collectives and lax.ppermute only.
A program may use at most 128 MiB of HBM per device.

v0:
```python
import math

import jax
import jax.numpy as jnp
from jax import lax
from jax.sharding import PartitionSpec as P

BUCKET_WIDTH = 128
GENES_OWN = 8


RHO_GRID = (0.0, 0.01, 0.04, 0.09, 0.16, 0.25, 0.5, 1.0)


def solve_moments(factor, rhs):
    half = lax.linalg.triangular_solve(factor, rhs, left_side=True, lower=True)
    return lax.linalg.triangular_solve(factor, half, left_side=True, lower=True, transpose_a=True)


def inner_rows(first, second):
    return lax.dot_general(
        first, second, (((0,), (0,)), ((), ())), preferred_element_type=jnp.float32
    )


def block_rank(labels, group_count, label_count):
    onehot = (labels[:, None] == jnp.arange(label_count, dtype=jnp.int32)[None, :]).astype(
        jnp.int32
    )
    blocks = onehot.reshape(group_count, labels.shape[0] // group_count, label_count)
    return jnp.sum((jnp.cumsum(blocks, axis=1) - blocks) * blocks, axis=2).reshape(labels.shape[0])


def finish_slots(
    gram, cross, slot_bucket, moments, variant_weight, variant_gene, owner_here, sample_total
):
    cov_count = moments.shape[0]
    slot_count = gram.shape[0]
    span_width = gram.shape[1]
    factor = jnp.linalg.cholesky(moments[:, :cov_count])
    beta_hat = solve_moments(factor, moments[:, cov_count:])[:, 0]
    cov_cross = cross[:, :cov_count, :]
    raw_score = cross[:, cov_count, :]
    stacked = jnp.transpose(cov_cross, (1, 0, 2)).reshape(cov_count, slot_count * span_width)
    solved = solve_moments(factor, stacked).reshape(cov_count, slot_count, span_width)
    projected = jnp.einsum("bcj,cbk->bjk", cov_cross, solved, precision=lax.Precision.HIGHEST)
    scores = raw_score - jnp.einsum(
        "bcj,c->bj", cov_cross, beta_hat, precision=lax.Precision.HIGHEST
    )
    bucket_total = variant_gene.shape[0] // span_width
    weight_rows = jnp.where(variant_gene >= 0, variant_weight, 0.0).reshape(
        bucket_total, span_width
    )
    live_weight = jnp.take(weight_rows, slot_bucket, axis=0)
    tiles = live_weight[:, :, None] * live_weight[:, None, :] * (gram - projected) / sample_total
    zscore = (live_weight * scores / math.sqrt(sample_total)).reshape(slot_count * span_width)
    gene_rows = (
        jnp.take(variant_gene.reshape(bucket_total, span_width), slot_bucket, axis=0)
        - owner_here * GENES_OWN
    )
    member = (
        gene_rows.reshape(slot_count * span_width)[:, None]
        == jnp.arange(GENES_OWN, dtype=jnp.int32)[None, :]
    ).astype(jnp.float32)
    squares = jnp.dot(zscore * zscore, member, precision=lax.Precision.HIGHEST)
    burden_sum = jnp.dot(zscore, member, precision=lax.Precision.HIGHEST)
    diagonal = jnp.diagonal(tiles, axis1=1, axis2=2).reshape(slot_count * span_width)
    trace_sum = jnp.dot(diagonal, member, precision=lax.Precision.HIGHEST)
    return (tiles, squares, burden_sum, trace_sum)


def shards(dosage, covariates, phenotype, sample_mask, variant_weight, bucket_owner, variant_gene):
    gene_count = lax.axis_size("gene")
    cohort_count = lax.axis_size("cohort")
    sample_count = lax.axis_size("sample")
    owner_count = gene_count * cohort_count
    span_width = BUCKET_WIDTH
    sample_rows = dosage.shape[0]
    src_buckets = dosage.shape[1] // span_width
    total_buckets = bucket_owner.shape[0]
    held_slots = total_buckets // owner_count
    cap_slots = held_slots // 2
    share = held_slots // sample_count
    sample_total = sample_rows * sample_count * cohort_count
    cohort_here = lax.axis_index("cohort")
    owner_here = lax.axis_index("gene") * cohort_count + cohort_here
    sample_keep = sample_mask.astype(jnp.bfloat16)
    masked_cov = covariates * sample_keep[:, None]
    left_cols = jnp.concatenate([masked_cov, (phenotype * sample_keep)[:, None]], axis=1)
    moments = lax.psum(
        inner_rows(masked_cov, jnp.concatenate([covariates, phenotype[:, None]], axis=1)),
        ("sample", "cohort"),
    )
    masked_dosage = (dosage * sample_keep[:, None]).reshape(sample_rows, src_buckets, span_width)
    owner_ids = jnp.arange(owner_count, dtype=jnp.int32)
    onehot = (bucket_owner[:, None] == owner_ids[None, :]).astype(jnp.int32)
    owner_rank = jnp.sum((jnp.cumsum(onehot, axis=0) - onehot) * onehot, axis=1)
    pair_rank = block_rank(bucket_owner, gene_count, owner_count)
    source_start = lax.axis_index("gene") * src_buckets
    mine_owner = lax.dynamic_slice_in_dim(bucket_owner, source_start, src_buckets)
    mine_rank = lax.dynamic_slice_in_dim(pair_rank, source_start, src_buckets)
    own_key = jnp.where(bucket_owner == owner_here, owner_rank, held_slots)
    own_bucket = (
        jnp.zeros((held_slots,), jnp.int32)
        .at[own_key]
        .set(jnp.arange(total_buckets, dtype=jnp.int32), mode="drop")
    )
    own_source = own_bucket // src_buckets
    own_pair = jnp.take(pair_rank, own_bucket)
    cohort_ids = jnp.arange(cohort_count, dtype=jnp.int32)
    flat_index = (
        (own_source[None, :] * cohort_count + cohort_ids[:, None]) * cap_slots + own_pair[None, :]
    ).reshape(cohort_count * held_slots)
    send_from = (
        jnp.full((owner_count * cap_slots,), -1, jnp.int32)
        .at[mine_owner * cap_slots + mine_rank]
        .set(jnp.arange(src_buckets, dtype=jnp.int32))
    )
    send_pick = jnp.maximum(send_from, 0)
    cohort_left = lax.all_gather(left_cols[:, None, :], "cohort", axis=1, tiled=True)
    packed = (
        jnp.take(masked_dosage, send_pick, axis=1)
        * (send_from >= 0).astype(jnp.bfloat16)[None, :, None]
    )
    packed = packed.reshape(sample_rows, owner_count, cap_slots, span_width)
    arrived = lax.all_to_all(packed, ("gene", "cohort"), split_axis=1, concat_axis=1, tiled=True)
    arrived = arrived.reshape(sample_rows, owner_count * cap_slots, span_width)
    owned = jnp.take(arrived, flat_index, axis=1).reshape(
        sample_rows, cohort_count, held_slots, span_width
    )
    gram = jnp.einsum("schj,schk->hjk", owned, owned, preferred_element_type=jnp.float32)
    cross = jnp.einsum("sci,schk->hik", cohort_left, owned, preferred_element_type=jnp.float32)
    slot_start = lax.axis_index("sample") * share
    gram, cross = lax.psum((gram, cross), "sample")
    tiles, squares, burden_sum, trace_sum = finish_slots(
        gram, cross, own_bucket, moments, variant_weight, variant_gene, owner_here, sample_total
    )
    tiles = lax.dynamic_slice_in_dim(tiles, slot_start, share)
    rho_col = jnp.array(RHO_GRID, dtype=jnp.float32)[:, None]
    rho_stats = (
        (1.0 - rho_col) * squares[None, :] + rho_col * (burden_sum * burden_sum)[None, :]
    ) / span_width
    gene_trace = trace_sum / span_width
    return (tiles[None], rho_stats, gene_trace)


def solution(mesh):
    placed = (
        P(("sample", "cohort"), "gene"),
        P(("sample", "cohort"), None),
        P(("sample", "cohort")),
        P(("sample", "cohort")),
        P(),
        P(),
        P(),
    )
    return jax.shard_map(
        shards,
        mesh=mesh,
        in_specs=placed,
        out_specs=(
            P(("gene", "cohort"), "sample", None, None),
            P(None, ("gene", "cohort")),
            P(("gene", "cohort")),
        ),
        check_vma=False,
    )
```

profile of v0, /device:TPU:1, one launch (start us, length us, event | category | flops | bytes accessed | tf_op | source)
XLA Modules:
  0.0 635.4 jit_solution(13550545437215399836)
XLA Ops:
  7.2 0.8 eq.67
  8.5 0.8 compare_select_fusion.3
  9.3 0.8 scatter_custom_fusion.1
  10.1 12.0 %copy.54 = bf16[512,8192]{0,1:T(8,128)(2,1)} copy(bf16[512,8192]{1,0:T(8,128)(2,1)} %param.8) | data formatting | bytes 16777216 | tf_op args[0]
  22.1 7.1 %broadcast_multiply_fusion = bf16[512,8192]{0,1:T(8,128)(2,1)} fusion(bf16[512,8192]{0,1:T(8,128)(2,1)} %copy.54, bf16[512]{0:T(512)(128)(2,1)S(1)} %get-tuple-element.9), kind=kLoop, calls=%fused_computation.14 | loop fusion | flops 4194304 | bytes 16778240 | tf_op jit(solution)/shard_map/mul | solution.py:94
  29.2 11.9 %copy.55 = bf16[512,64,128]{2,0,1:T(8,128)(2,1)} copy(bf16[512,64,128]{0,2,1:T(8,128)(2,1)} %bitcast.130) | data formatting | bytes 16777216 | tf_op jit(solution)/shard_map/reshape | solution.py:94
  41.3 11.5 %gather_fusion.2 = bf16[128,512,128]{2,1,0:T(8,128)(2,1)} fusion(bf16[512,64,128]{2,0,1:T(8,128)(2,1)} %copy.55, s32[1024]{0:T(1024)S(1)} %pad_clamp_fusion.1), kind=kCustom, calls=%fused_computation.2 | custom fusion | bytes 33554944 | tf_op jit(solution)/shard_map/jit(_take)/gather | solution.py:122
  52.9 14.2 %select_multiply_fusion = bf16[512,16,8,128]{3,0,2,1:T(8,128)(2,1)} fusion(bf16[512,16,8,128]{3,0,2,1:T(8,128)(2,1)} %bitcast.127, pred[16,8]{1,0:T(8,128)(4,1)S(1)} %broadcast_in_dim.106, bf16[16,8]{1,0:T(8,128)(2,1)S(1)} %reshape.226), kind=kLoop, calls=%fused_computation.8 | loop fusion | flops 16777216 | bytes 33554816 | tf_op jit(solution)/shard_map/mul | solution.py:122
  67.0 8.8 %all-to-all-start = ((bf16[512,16,8,128]{3,0,2,1:T(8,128)(2,1)}), bf16[512,16,8,128]{3,0,2,1:T(8,128)(2,1)}, u32[]{:S(2)}, u32[]{:S(2)}) async-start(bf16[512,16,8,128]{3,0,2,1:T(8,128)(2,1)} %select_multiply_fusion), calls=%async_computation | async-start | bytes 33554432 | tf_op jit(solution)/shard_map/all_to_all | solution.py:126
  76.8 1.4 scatter_custom_fusion
  78.3 0.7 gather_fusion.1
  79.1 160.4 %all-gather.1 = bf16[4,33,512]{2,1,0:T(8,128)(2,1)S(1)} all-gather(bf16[1,33,512]{2,1,0:T(8,128)(2,1)S(1)} %maximum_bitcast_fusion), channel_id=2, replica_groups=mesh['sample'=8,'gene'=4,'cohort'=4] {'cohort'}, dimensions={0}, use_global_device_ids=true | all-gather | bytes 168960 | tf_op jit(solution)/shard_map/all_gather | solution.py:120
  239.7 192.9 %psum.23 = f32[32,33]{0,1:T(8,128)S(1)} all-reduce(f32[32,33]{0,1:T(8,128)S(1)} %fusion.24), channel_id=1, replica_groups=mesh['sample'=8,'gene'=4,'cohort'=4] {'sample','cohort'}, use_global_device_ids=true, to_apply=%region_9.10 | all-reduce | flops 1056 | bytes 8448 | tf_op jit(solution)/shard_map/psum | solution.py:90
  432.7 2.9 cholesky.16
  435.7 0.6 compare_reduce_fusion
  436.3 0.7 fusion.28
  437.0 2.4 custom-call.12
  440.6 11.7 %gather_fusion.3 = bf16[64,512,128]{2,1,0:T(8,128)(2,1)} fusion(bf16[512,128,128]{2,0,1:T(8,128)(2,1)} %bitcast.6, s32[1024]{0:T(1024)S(1)} %pad_clamp_fusion), kind=kCustom, calls=%fused_computation.3 | custom fusion | bytes 16777472 | tf_op jit(solution)/shard_map/jit(_take)/gather | solution.py:128
  452.4 12.0 %copy.56 = bf16[512,64,128]{2,1,0:T(8,128)(2,1)} copy(bf16[512,64,128]{2,0,1:T(8,128)(2,1)} %bitcast.128) | data formatting | bytes 16777216 | tf_op jit(solution)/shard_map/jit(_take)/gather | solution.py:128
  464.4 7.4 %broadcast_select_fusion = bf16[512,4,16,128]{3,2,1,0:T(8,128)(2,1)} fusion(bf16[512,4,16,128]{3,2,1,0:T(8,128)(2,1)} %bitcast.129, pred[4,16]{1,0:T(4,128)(4,1)S(1)} %compare_and_fusion), kind=kLoop, calls=%fused_computation.9 | loop fusion | flops 4194304 | bytes 16777280 | tf_op jit(solution)/shard_map/jit(_take)/select_n | solution.py:128
  471.8 25.9 %fusion.4 = f32[16,128,128]{2,1,0:T(8,128)} fusion(bf16[512,4,16,128]{3,2,1,0:T(8,128)(2,1)} %broadcast_select_fusion), kind=kOutput, calls=%fused_computation.15 | convolution fusion | flops 1073741824 | bytes 9437184 | tf_op jit(solution)/shard_map/schj,schk->hjk/dot_general | solution.py:131
  497.7 8.8 %fusion.9 = f32[16,33,128]{2,1,0:T(8,128)} fusion(bf16[512,4,33,1]{0,2,1,3:T(8,128)(2,1)S(1)} %reshape.299, bf16[512,4,16,128]{3,2,1,0:T(8,128)(2,1)} %broadcast_select_fusion), kind=kOutput, calls=%fused_computation.19 | convolution fusion | flops 276824064 | bytes 8794112 | tf_op jit(solution)/shard_map/sci,schk->hik/dot_general | solution.py:132
  506.8 104.2 %all-reduce.3.cloned.1.call-done = (f32[16,128,128]{2,1,0:T(8,128)}, f32[16,33,128]{2,1,0:T(8,128)}) async-done(((f32[16,128,128]{2,1,0:T(8,128)}, f32[16,33,128]{2,1,0:T(8,128)}), (f32[16,128,128]{2,1,0:T(8,128)}, f32[16,33,128]{2,1,0:T(8,128)})) %all-reduce.3.cloned.1.call-update) | async-done | bytes 1318928 | tf_op jit(solution)/shard_map/psum | solution.py:134
  611.1 0.8 slice.59
  611.9 1.4 fusion.17
  613.3 1.2 fusion.20
  614.9 3.3 fusion.8
  618.2 4.6 copy.65
  622.9 1.8 gather_fusion.5
  624.7 1.1 fusion.12
  627.0 0.7 dynamic-slice_bitcast_fusion
  627.7 0.7 add_multiply_fusion
  (69 shorter events, 5.4 us)
Async XLA Ops:
  10.1 12.0 %copy-start.4 = (bf16[512]{0:T(512)(128)(2,1)S(1)}, bf16[512]{0:T(512)(128)(2,1)}, u32[]{:S(2)}) copy-start(bf16[512]{0:T(512)(128)(2,1)} %param.10) | copy-start | bytes 3076
  10.1 12.0 %copy-start.5 = (s32[512]{0:T(512)S(1)}, s32[512]{0:T(512)}, u32[]{:S(2)}) copy-start(s32[512]{0:T(512)} %param.11) | copy-start | bytes 6148
  67.0 8.9 %copy-start.3 = (s32[256]{0:T(256)S(1)}, s32[256]{0:T(256)}, u32[]{:S(2)}) copy-start(s32[256]{0:T(256)} %param.13) | copy-start | bytes 3076
  67.0 12.0 %copy-start.2 = (bf16[512,32]{0,1:T(8,128)(2,1)S(1)}, bf16[512,32]{0,1:T(8,128)(2,1)}, u32[]{:S(2)}) copy-start(bf16[512,32]{0,1:T(8,128)(2,1)} %param.9) | copy-start | bytes 98308
  67.0 372.4 %copy-start = (s32[32768]{0:T(1024)S(1)}, s32[32768]{0:T(1024)}, u32[]{:S(2)}) copy-start(s32[32768]{0:T(1024)} %param.14) | copy-start | bytes 393220
  67.0 372.4 %copy-start.1 = (f32[32768]{0:T(1024)S(1)}, f32[32768]{0:T(1024)}, u32[]{:S(2)}) copy-start(f32[32768]{0:T(1024)} %param.12) | copy-start | bytes 393220
  67.0 373.6 %all-to-all-start = ((bf16[512,16,8,128]{3,0,2,1:T(8,128)(2,1)}), bf16[512,16,8,128]{3,0,2,1:T(8,128)(2,1)}, u32[]{:S(2)}, u32[]{:S(2)}) async-start(bf16[512,16,8,128]{3,0,2,1:T(8,128)(2,1)} %select_multiply_fusion), calls=%async_computation | async-start | bytes 33554432 | tf_op jit(solution)/shard_map/all_to_all | solution.py:126
  75.8 535.2 %all-reduce.3.cloned.1.call-start = ((), (), s32[]{:S(2)}) async-start(), calls=%async_computation.1 | async-start | bytes 2752512 | tf_op jit(solution)/shard_map/psum | solution.py:134
  506.4 121.3 %copy-start.6 = (f32[8]{0:T(128)S(1)}, f32[8]{0:T(128)}, u32[]{:S(2)}) copy-start(f32[8]{0:T(128)} %constant.200.clone) | copy-start | bytes 100
  506.4 121.3 %copy-start.7 = (f32[8]{0:T(128)S(1)}, f32[8]{0:T(128)}, u32[]{:S(2)}) copy-start(f32[8]{0:T(128)} %constant.202) | copy-start | bytes 100
Sparse Core Ops, SparseCore 0:
  506.6 104.4 all-reduce.2
where the time goes:
time: 643 us; the launch traced here: 635 us
  blocking collectives  353 us (55%)
  waiting for transfers between devices  104 us (16%)
  local copies, waits for them, and re-layouts  72.6 us (11%)
  matrix products  43.6 us (7%)
  other arithmetic  38.3 us (6%)
  between operations  14.6 us (2%)
  starting transfers between devices  8.82 us (1%)
    psum x1, blocking collectives, shards(): lax.psum(inner_rows(masked_cov, jnp.concatenate([covariates, phenotype[:,...  193 us
    all_gather x1, blocking collectives, shards(): lax.all_gather(left_cols[:, None, :], 'cohort', axis=1, tiled=True)  160 us
    psum x1, waiting for transfers between devices, shards(): gram, cross = lax.psum((gram, cross), 'sample')  104 us
    dot_general x1, matrix products, shards(): jnp.einsum('schj,schk->hjk', owned, owned, preferred_element_type=jnp.flo...  25.9 us
    gather x2, local copies, waits for them, and re-layouts, shards(): jnp.take(arrived, flat_index, axis=1)  23.7 us
    mul x2, other arithmetic, shards(): jnp.take(masked_dosage, send_pick, axis=1)  14.2 us
  transfers between devices with their start and end apart: 2, of which 1 were waited for; matrix products, arithmetic and copies ran while one was open for 2% of the time, Pallas kernels for 0%

commit v1 on v0

v1 whole, which is shorter than its diff:
```python
import jax
import jax.numpy as jnp
from jax import lax
from jax.experimental import pallas as pl
from jax.experimental.pallas import tpu as pltpu
from jax.sharding import Mesh, PartitionSpec as P

AXES = ("x", "k", "g", "c")
RHO_GRID = (0.0, 0.01, 0.04, 0.09, 0.16, 0.25, 0.5, 1.0)
SAMPLES = 16384
WIDTH = 128
COVS = 32
LOCAL = 64
STEP = 4
CHUNK = 208
ROUTED = 112
FINAL = 48
F32 = jnp.float32
HIGHEST = lax.Precision.HIGHEST


def params(**kwargs):
    return pltpu.CompilerParams(vmem_limit_bytes=48 * 1024 * 1024, **kwargs)


def iota(shape, dim):
    return lax.broadcasted_iota(jnp.int32, shape, dim)


def products_kernel(owner_ref, dosage_ref, cov_ref, pheno_ref, mask_ref, keep_ref, send_ref,
                    left_ref, packed_ref, cross_ref, rest_ref, moment_ref, count_ref):
    step = pl.program_id(0)
    x, k, g, c = (lax.axis_index(a) for a in AXES)

    def place(core, xd, cd):
        first = core == 0
        d = jnp.where(first, (xd - x) & 3, (cd - c) & 3)
        j = jnp.where(first, cd, xd)
        return d, j

    @pl.when(step == 0)
    def _():
        rest_ref[...] = jnp.zeros_like(rest_ref)
        for i in range(4):
            count_ref[i] = 0
        cov_rows = cov_ref[...].T
        pheno = pheno_ref[...]
        right = jnp.concatenate(
            [cov_rows, pheno, jnp.zeros((WIDTH - COVS - 1, cov_rows.shape[1]), jnp.bfloat16)], 0)
        keep = mask_ref[...].astype(F32).astype(jnp.bfloat16)
        masked = right[:48] * keep
        left_ref[...] = masked
        m = lax.dot_general(masked[:COVS], right, (((1,), (1,)), ((), ())),
                            preferred_element_type=F32)
        moment_ref[...] = pltpu.roll(m[:16], 32, 1) + pltpu.roll(m[16:32], 65, 1)

    keep_row = mask_ref[...].astype(F32).astype(jnp.bfloat16)
    row, lane = iota((64, WIDTH), 0), iota((64, WIDTH), 1)
    take_low = (lane < 64) & (row > lane)
    eye = iota((WIDTH, WIDTH), 0) == iota((WIDTH, WIDTH), 1)
    for pair in range(STEP // 2):
        panel = dosage_ref[:, pair * 256:(pair + 1) * 256]
        left = jnp.concatenate([panel.T * keep_row, left_ref[...]], 0)
        out = jnp.dot(left, panel, preferred_element_type=F32)
        for half in range(2):
            lo = half * WIDTH
            block = out[lo:lo + WIDTH, lo:lo + WIDTH]
            bucket = step * STEP + pair * 2 + half
            cd = owner_ref[g * LOCAL + bucket] & 3
            pos = count_ref[cd]
            count_ref[cd] = pos + 1
            slot = pair * 2 + half
            packed_ref[slot] = jnp.where(take_low, pltpu.roll(block[64:], 64, 1), block[:64])
            rows = pl.ds(pl.multiple_of(pos * 8, 8), 8)
            for xd in range(4):
                d, j = place(k, xd, cd)
                keep_ref[d, j, rows, :] = packed_ref[
                    slot, pl.ds(pl.multiple_of((2 * xd + k) * 8, 8), 8), :]
                d, j = place(1 - k, xd, cd)
                send_ref[d, j, rows, :] = packed_ref[
                    slot, pl.ds(pl.multiple_of((2 * xd + 1 - k) * 8, 8), 8), :]
            cross_ref[cd, pl.ds(pl.multiple_of(pos * COVS, 8), COVS), :] = out[
                256:256 + COVS, lo:lo + WIDTH]
            rest_ref[cd, pl.ds(pos, 1), :] = out[256 + COVS:257 + COVS, lo:lo + WIDTH]
            rest_ref[cd, pl.ds(pos + 16, 1), :] = jnp.sum(
                jnp.where(eye, block, 0.0), axis=0, keepdims=True)

    @pl.when(step == pl.num_programs(0) - 1)
    def _():
        for cd in range(4):
            for q in range(5):
                if q < 4:
                    turned = cross_ref[cd, q * WIDTH:(q + 1) * WIDTH, :].T
                else:
                    turned = rest_ref[cd].T
                for t in range(8):
                    tile = turned[16 * t:16 * t + 16]
                    if q == 4:
                        tile = tile + moment_ref[...]
                    rows = slice(128 + 16 * q, 144 + 16 * q)
                    d, j = place(t & 1, t >> 1, cd)

                    @pl.when(k == (t & 1))
                    def _():
                        keep_ref[d, j, rows, :] = tile

                    @pl.when(k != (t & 1))
                    def _():
                        send_ref[d, j, rows, :] = tile


def products(owner, dosage, cov, pheno, mask):
    samples = dosage.shape[0]
    out = jax.ShapeDtypeStruct((4, 4, CHUNK, WIDTH), F32)
    whole = lambda shape: pl.BlockSpec(shape, lambda i, o: (0,) * len(shape))
    return pl.pallas_call(
        products_kernel,
        out_shape=(out, out),
        grid_spec=pltpu.PrefetchScalarGridSpec(
            num_scalar_prefetch=1,
            grid=(LOCAL // STEP,),
            in_specs=[
                pl.BlockSpec((samples, STEP * WIDTH), lambda i, o: (0, i)),
                whole(cov.shape), whole(pheno.shape), whole(mask.shape),
            ],
            out_specs=[whole(out.shape), whole(out.shape)],
            scratch_shapes=[
                pltpu.VMEM((48, samples), jnp.bfloat16),
                pltpu.VMEM((STEP, 64, WIDTH), F32),
                pltpu.VMEM((4, 16 * COVS, WIDTH), F32),
                pltpu.VMEM((4, WIDTH, WIDTH), F32),
                pltpu.VMEM((16, WIDTH), F32),
                pltpu.SMEM((4,), jnp.int32),
            ],
        ),
        compiler_params=params(dimension_semantics=("arbitrary",)),
        name="products",
    )(owner, dosage, cov, pheno, mask)


def first_sum_kernel(keep_ref, recv_ref, *outs):
    for d in range(4):
        outs[d][...] = keep_ref[d] + recv_ref[d]


def second_sum_kernel(a0, r1, r2, r3, *outs):
    x, k, g, c = (lax.axis_index(a) for a in AXES)
    base = jnp.where(k == 0, c, x)
    for d in range(4):
        j = (base + d) & 3
        outs[d][...] = (a0[j] + r1[j]) + (r2[j] + r3[j])


def vmem_call(kernel, shapes, name, n_in, scratch=(), smem_in=0, smem_out=()):
    specs = [pl.BlockSpec(memory_space=pltpu.SMEM)] * smem_in + [
        pl.BlockSpec(memory_space=pltpu.VMEM)] * (n_in - smem_in)
    return pl.pallas_call(
        kernel,
        out_shape=tuple(shapes),
        in_specs=specs,
        out_specs=tuple(
            pl.BlockSpec(memory_space=pltpu.SMEM if i in smem_out else pltpu.VMEM)
            for i in range(len(shapes))),
        scratch_shapes=scratch,
        compiler_params=params(),
        name=name,
    )


def route_kernel(owner_ref, b0, q1, q2, q3, e0, e1, e2, e3, moment_ref, total_ref, slot_ref,
                 count_ref):
    x, k, g, c = (lax.axis_index(a) for a in AXES)
    total_ref[...] = (b0[...] + q1[...]) + (q2[...] + q3[...])
    moment_ref[...] = total_ref[192:208, :]
    slot_ref[...] = jnp.zeros_like(slot_ref)
    for i in range(5):
        count_ref[i] = 0
    lane = iota((16, WIDTH), 1)

    def body(bucket, _):
        owner = owner_ref[g * LOCAL + bucket]

        @pl.when((owner & 3) == c)
        def _():
            pos = count_ref[4]
            count_ref[4] = pos + 1
            gd = owner >> 2
            pr = count_ref[gd]
            count_ref[gd] = pr + 1
            d = (gd - g) & 3
            slot_ref[d, pl.ds(pl.multiple_of(pr * 8, 8), 8), :] = total_ref[
                pl.ds(pl.multiple_of(pos * 8, 8), 8), :]
            tile = total_ref[pl.ds(pl.multiple_of(128 + 16 * (pos >> 2), 16), 16), :]
            tile = pltpu.roll(tile, (32 * (pr - pos)) & 127, 1)
            at = pl.ds(pl.multiple_of(64 + 16 * (pr >> 2), 16), 16)
            slot_ref[d, at, :] = jnp.where((lane >> 5) == (pr & 3), tile, slot_ref[d, at, :])
            rest = pltpu.roll(total_ref[192:208, :], (pr - pos) & 127, 1)
            slot_ref[d, 96:112, :] = jnp.where(
                (lane == pr) | (lane == pr + 16), rest, slot_ref[d, 96:112, :])

        return 0

    lax.fori_loop(0, LOCAL, body, 0)
    for d, out in enumerate((e0, e1, e2, e3)):
        out[...] = slot_ref[d]


def prepare_kernel(owner_ref, moment_ref, weight_ref, gene_ref,
                   source_ref, rank_ref, local_gene_ref, whiten_ref, half_ref, scale_ref,
                   weights_ref, pad_ref, system_ref, count_ref):
    x, k, g, c = (lax.axis_index(a) for a in AXES)
    me = g * 4 + c
    count_ref[0] = 0
    pad_ref[...] = jnp.zeros_like(pad_ref)
    lane1 = iota((1, WIDTH), 1)

    for source in range(4):
        count_ref[1] = 0

        def body(i, _):
            bucket = source * LOCAL + i

            @pl.when(owner_ref[bucket] == me)
            def _():
                r = count_ref[0]
                count_ref[0] = r + 1
                pr = count_ref[1]
                count_ref[1] = pr + 1
                source_ref[r] = (g - source) & 3
                rank_ref[r] = pr
                genes = gene_ref[pl.ds(bucket, 1), :]
                local_gene_ref[r] = jnp.max(genes) - me * 8
                pad_ref[pl.ds(r, 1), :] = jnp.where(genes >= 0, weight_ref[pl.ds(bucket, 1), :], 0.0)

            return 0

        lax.fori_loop(0, LOCAL, body, 0)

    weights_ref[...] = pad_ref[:16, :]
    turned = pad_ref[...].T
    pad_ref[...] = turned
    part = 2 * x + k
    mine = pad_ref[pl.ds(pl.multiple_of(part * 16, 16), 16), :]
    lane = iota((16, WIDTH), 1)
    by16 = pltpu.roll(mine, 16, 1)
    scale_ref[...] = (mine * (1.0 / 128.0) + by16 * by16 * (1.0 / SAMPLES)
                      + pltpu.roll(mine, 32, 1))

    m = moment_ref[...]
    high = pltpu.roll(m, WIDTH - 32, 1)
    low = pltpu.roll(m, WIDTH - 65, 1)
    m = jnp.concatenate([high, low], 0)
    row, lane = iota((COVS, WIDTH), 0), iota((COVS, WIDTH), 1)
    unit = jnp.where(lane == row + 64, 1.0, 0.0)
    m = jnp.where(lane <= COVS, m, 0.0) + unit
    scales = jnp.zeros((COVS, WIDTH), F32)
    for i in range(COVS):
        pivot_row = m[i:i + 1, :]
        col = jnp.sum(jnp.where(lane == i, m, 0.0), axis=1, keepdims=True)
        inv = 1.0 / col[i:i + 1, :]
        scales = jnp.where(row == i, jnp.broadcast_to(inv, (COVS, WIDTH)), scales)
        factor = jnp.where(row[:, :1] > i, col * inv, 0.0)
        m = m - factor * pivot_row
    m = m * jnp.sqrt(scales)
    linv = jnp.where(lane < COVS, pltpu.roll(m, 64, 1), 0.0)
    blocks = linv
    wide = jnp.concatenate([pltpu.roll(linv, 32 * q, 1) for q in range(4)], 0)
    whiten_ref[...] = wide
    half_col = jnp.sum(jnp.where(lane == COVS, m, 0.0), axis=1, keepdims=True)
    half_wide = jnp.concatenate([half_col] * 4, 0)
    row, lane = iota((WIDTH, WIDTH), 0), iota((WIDTH, WIDTH), 1)
    half_ref[...] = jnp.where(lane == (row >> 5), half_wide, 0.0)


def scores_kernel(source_ref, rank_ref, w0, w1, w2, w3, whiten_ref, half_ref, scale_ref,
                  out_ref, slot_ref, cross_ref):
    for d, ref in enumerate((w0, w1, w2, w3)):
        slot_ref[d] = ref[...]
    lane = iota((16, WIDTH), 1)
    rest = jnp.zeros((16, WIDTH), F32)
    for group in range(4):
        tile = jnp.zeros((16, WIDTH), F32)
        for q in range(4):
            r = group * 4 + q
            d, pr = source_ref[r], rank_ref[r]
            out_ref[r >> 1, 8 * (r & 1):8 * (r & 1) + 8, :] = slot_ref[
                d, pl.ds(pl.multiple_of(pr * 8, 8), 8), :]
            part = slot_ref[d, pl.ds(pl.multiple_of(64 + 16 * (pr >> 2), 16), 16), :]
            part = pltpu.roll(part, (32 * (q - pr)) & 127, 1)
            tile = jnp.where((lane >> 5) == q, part, tile)
            more = pltpu.roll(slot_ref[d, 96:112, :], (r - pr) & 127, 1)
            rest = jnp.where((lane == r) | (lane == r + 16), more, rest)
        cross_ref[group * 16:group * 16 + 16, :] = tile
    whitened = lax.dot_general(cross_ref[...], whiten_ref[...], (((1,), (1,)), ((), ())),
                               precision=HIGHEST, preferred_element_type=F32)
    row, col = iota((WIDTH, WIDTH), 0), iota((WIDTH, WIDTH), 1)
    ones = jnp.where(col == (row >> 5) + 16, 1.0, 0.0)
    taken = (jnp.dot(whitened, half_ref[...], precision=HIGHEST, preferred_element_type=F32)
             + jnp.dot(whitened * whitened, ones, precision=HIGHEST, preferred_element_type=F32))
    for group in range(4):
        rest = rest - pltpu.roll(taken[group * 16:group * 16 + 16], 4 * group, 1)
    scale = scale_ref[...]
    rest = jnp.where(lane < 32, rest * scale, jnp.where(lane < 48, scale, 0.0))
    for t in range(8):
        out_ref[t, 16:32, :] = whitened[(t >> 1) * 16:(t >> 1) * 16 + 16]
        out_ref[t, 32:48, :] = rest


def finish_kernel(local_gene_ref, parts_ref, weights_ref, tiles_ref, rho_ref, trace_ref):
    x, k, g, c = (lax.axis_index(a) for a in AXES)
    part = 2 * x + k
    row, lane = iota((WIDTH, WIDTH), 0), iota((WIDTH, WIDTH), 1)
    whitened = jnp.concatenate([parts_ref[t, 16:32, :] for t in range(8)], 0)
    rest = jnp.concatenate([parts_ref[t, 32:48, :] for t in range(8)], 0)
    direct = ((row < 64) & ((lane >= 64) | (row <= lane))) | ((row >= 64) & (lane >= 64) & (row > lane))
    for q in range(2):
        rank = 2 * part + q
        packed = jnp.concatenate([parts_ref[t, 8 * q:8 * q + 8, :] for t in range(8)], 0)
        full = jnp.concatenate([packed, pltpu.roll(packed, 64, 1)], 0)
        gram = jnp.where(direct, full, full.T)
        w = jnp.where((lane >> 5) == 2 * (part & 1) + q, whitened, 0.0)
        projected = lax.dot_general(w, w, (((1,), (1,)), ((), ())), precision=HIGHEST,
                                    preferred_element_type=F32)
        weight_col = jnp.sum(jnp.where(lane == 32 + rank, rest, 0.0), axis=1, keepdims=True)
        diag_col = jnp.sum(jnp.where(lane == 16 + rank, rest, 0.0), axis=1, keepdims=True)
        weight_row = weights_ref[pl.ds(rank, 1), :]
        tile = weight_col * weight_row * (gram - projected) * (1.0 / SAMPLES)
        tiles_ref[q] = jnp.where(row == lane, diag_col, tile)

    row8, lane8 = iota((8, WIDTH), 0), iota((8, WIDTH), 1)
    member = jnp.zeros((8, WIDTH), F32)
    for r in range(16):
        member = jnp.where((lane8 == r) & (row8 == local_gene_ref[r]), 1.0, member)
    squares = jnp.sum(rest * rest, axis=0, keepdims=True)
    sums = jnp.sum(rest, axis=0, keepdims=True)
    table = jnp.where(row8 == 0, squares, sums)
    nt = (((1,), (1,)), ((), ()))
    by_gene = lax.dot_general(table, member, nt, precision=HIGHEST, preferred_element_type=F32)
    traces = lax.dot_general(table, pltpu.roll(member, 16, 1), nt, precision=HIGHEST,
                             preferred_element_type=F32)
    level = iota((8, 8), 0)
    rho = jnp.zeros((8, 8), F32)
    for i, value in enumerate(RHO_GRID):
        rho = jnp.where(level == i, value, rho)
    burden = by_gene[1:2, :]
    rho_ref[...] = ((1.0 - rho) * by_gene[0:1, :] + rho * (burden * burden)) * (1.0 / WIDTH)
    trace_ref[...] = traces[1:2, :] * (1.0 / WIDTH)


def turns(d, first):
    pairs = []
    for x in range(4):
        for k in range(2):
            for g in range(4):
                for c in range(4):
                    along_x = (k == 0) == first
                    xd, cd = ((x + d) % 4, c) if along_x else (x, (c + d) % 4)
                    pairs.append((((x * 2 + k) * 4 + g) * 4 + c, ((xd * 2 + k) * 4 + g) * 4 + cd))
    return pairs


def shards(dosage, covariates, phenotype, sample_mask, variant_weight, bucket_owner, variant_gene):
    samples = dosage.shape[0]
    keep, send = products(bucket_owner, dosage, covariates, phenotype.reshape(1, samples),
                          sample_mask.reshape(1, samples))
    recv = lax.ppermute(send, "k", [(0, 1), (1, 0)])
    chunk = jax.ShapeDtypeStruct((4, CHUNK, WIDTH), F32)
    a = vmem_call(first_sum_kernel, [chunk] * 4, "first_sum", 2)(keep, recv)
    r = {d: lax.ppermute(a[d], AXES, turns(d, True)) for d in (2, 1, 3)}
    part = jax.ShapeDtypeStruct((CHUNK, WIDTH), F32)
    b = vmem_call(second_sum_kernel, [part] * 4, "second_sum", 4)(a[0], r[1], r[2], r[3])
    q = {d: lax.ppermute(b[d], AXES, turns(d, False)) for d in (2, 1, 3)}
    routed = jax.ShapeDtypeStruct((ROUTED, WIDTH), F32)
    tile16 = jax.ShapeDtypeStruct((16, WIDTH), F32)
    *e, moment = vmem_call(
        route_kernel, [routed] * 4 + [tile16], "route", 5, smem_in=1,
        scratch=[pltpu.VMEM((CHUNK, WIDTH), F32), pltpu.VMEM((4, ROUTED, WIDTH), F32),
                 pltpu.SMEM((5,), jnp.int32)],
    )(bucket_owner, b[0], q[1], q[2], q[3])
    w = {d: lax.ppermute(e[d], "g", [(i, (i + d) % 4) for i in range(4)]) for d in (2, 1, 3)}
    list16 = jax.ShapeDtypeStruct((16,), jnp.int32)
    square = jax.ShapeDtypeStruct((WIDTH, WIDTH), F32)
    source, rank, local_gene, whiten, half, scale, weights = vmem_call(
        prepare_kernel, [list16] * 3 + [square] * 2 + [tile16] * 2, "prepare", 4, smem_in=1,
        smem_out=(0, 1, 2),
        scratch=[pltpu.VMEM((WIDTH, WIDTH), F32), pltpu.VMEM((COVS, WIDTH), F32),
                 pltpu.SMEM((2,), jnp.int32)],
    )(bucket_owner, moment, variant_weight.reshape(-1, WIDTH), variant_gene.reshape(-1, WIDTH))
    (parts,) = vmem_call(
        scores_kernel, [jax.ShapeDtypeStruct((8, FINAL, WIDTH), F32)], "scores", 9, smem_in=2,
        scratch=[pltpu.VMEM((4, ROUTED, WIDTH), F32), pltpu.VMEM((64, WIDTH), F32)],
    )(source, rank, e[0], w[1], w[2], w[3], whiten, half, scale)
    parts = lax.all_to_all(parts, ("x", "k"), split_axis=0, concat_axis=0, tiled=True)
    tiles, rho, trace = vmem_call(
        finish_kernel,
        [jax.ShapeDtypeStruct((2, WIDTH, WIDTH), F32), jax.ShapeDtypeStruct((8, 8), F32),
         jax.ShapeDtypeStruct((1, 8), F32)], "finish", 3, smem_in=1,
    )(local_gene, parts, weights)
    return tiles[None], rho, trace.reshape(8)


def solution(mesh):
    grid = Mesh(mesh.devices.reshape(4, 2, 4, 4), AXES)
    rows = ("x", "k", "c")
    owners = ("g", "c")
    return jax.shard_map(
        shards,
        mesh=grid,
        in_specs=(P(rows, "g"), P(rows, None), P(rows), P(rows), P(), P(), P()),
        out_specs=(P(owners, ("x", "k"), None, None), P(None, owners), P(owners)),
        check_vma=False,
    )
```

time: 643 us -> 82.8 us (0.13); the launches traced: 635 us -> 82.3 us
  blocking collectives: 353 us -> 14 us
  waiting for transfers between devices: 104 us -> 15 us
  local copies, waits for them, and re-layouts: 72.6 us -> 2.94 us
  matrix products: 43.6 us -> 0 us
  other arithmetic: 38.3 us -> 0 us
  Pallas kernels: 0 us -> 32.3 us
  between operations: 14.6 us -> 0.74 us
  starting transfers between devices: 8.82 us -> 17.4 us
    psum x1 -> x0, blocking collectives: 193 us -> none  [shards(): lax.psum(inner_rows(masked_cov, jnp.concatenate([covariates, phenotype[:,...]
    all_gather x1 -> x0, blocking collectives: 160 us -> none  [shards(): lax.all_gather(left_cols[:, None, :], 'cohort', axis=1, tiled=True)]
    psum x1 -> x0, waiting for transfers between devices: 104 us -> none  [shards(): gram, cross = lax.psum((gram, cross), 'sample')]
    dot_general x8 -> x0, matrix products: 41.6 us -> none  [the longest x1 25.9 us: shards(): jnp.einsum('schj,schk->hjk', owned, owned, preferred_element_type=jnp.flo...]
    gather x8 -> x0, local copies, waits for them, and re-layouts: 38.9 us -> none  [the longest x2 23.7 us: shards(): jnp.take(arrived, flat_index, axis=1)]
    pallas_call x0 -> x7, Pallas kernels: none -> 32.3 us  [the longest x1 16.2 us: products(): pl.pallas_call(products_kernel, out_shape=(out, out), grid_spec=pltpu.Pre...]
    mul x6 -> x0, other arithmetic: 21.4 us -> none  [the longest x2 14.2 us: shards(): jnp.take(masked_dosage, send_pick, axis=1)]
    ppermute x0 -> x10, starting transfers between devices: none -> 17.4 us  [the longest x3 5.82 us: shards(): r = {d: lax.ppermute(a[d], AXES, turns(d, True)) for d in (2, 1, 3)}]
  transfers between devices with their start and end apart: 2 -> 10, of which waited for: 1 -> 5; matrix products, arithmetic and copies ran while one was open for 2% -> 0% of each run, Pallas kernels for 0% -> 13%
where the time goes in v1:
time: 82.8 us; the launch traced here: 82.3 us
  Pallas kernels  32.3 us (39%)
  starting transfers between devices  17.4 us (21%)
  waiting for transfers between devices  15 us (18%)
  blocking collectives  14 us (17%)
  local copies, waits for them, and re-layouts  2.94 us (4%)
    pallas_call x1, Pallas kernels, products(): pl.pallas_call(products_kernel, out_shape=(out, out), grid_spec=pltpu.Pre...  16.2 us
    all_to_all x1, blocking collectives, shards(): lax.all_to_all(parts, ('x', 'k'), split_axis=0, concat_axis=0, tiled=True)  14 us
    pallas_call x1, Pallas kernels, shards(): vmem_call(prepare_kernel, [list16] * 3 + [square] * 2 + [tile16] * 2, 'pr...  10.8 us
    ppermute x3, waiting for transfers between devices, shards(): r = {d: lax.ppermute(a[d], AXES, turns(d, True)) for d in (2, 1, 3)}  9.35 us
    ppermute x3, starting transfers between devices, shards(): r = {d: lax.ppermute(a[d], AXES, turns(d, True)) for d in (2, 1, 3)}  5.82 us
    ppermute x3, starting transfers between devices, shards(): lax.ppermute(e[d], 'g', [(i, (i + d) % 4) for i in range(4)])  5.11 us
    ppermute x3, starting transfers between devices, shards(): q = {d: lax.ppermute(b[d], AXES, turns(d, False)) for d in (2, 1, 3)}  4.88 us
    ppermute x1, waiting for transfers between devices, shards(): recv = lax.ppermute(send, 'k', [(0, 1), (1, 0)])  3.22 us
  transfers between devices with their start and end apart: 10, of which 5 were waited for; matrix products, arithmetic and copies ran while one was open for 0% of the time, Pallas kernels for 13%

profile of v1, /device:TPU:1, one launch (start us, length us, event | category | flops | bytes accessed | tf_op | source)
XLA Modules:
  0.0 82.3 jit_solution(10022373566439675163)
XLA Ops:
  0.6 0.7 reshape.21.pheno_ref
  1.3 0.9 %copy.10.cov_ref = bf16[512,32]{1,0:T(8,128)(2,1)S(1)} copy(bf16[512,32]{0,1:T(8,128)(2,1)} %param.8) | data formatting | bytes 65536 | tf_op args[1]
  2.2 0.0 copy-start.2
  2.2 0.7 copy-done.2
  2.9 0.7 copy-done.4
  3.6 16.2 %products.1 = (f32[4,4,208,128]{3,2,1,0:T(8,128)S(1)}, f32[4,4,208,128]{3,2,1,0:T(8,128)S(1)}) custom-call(s32[256]{0:T(256)S(1)} %copy-done.2, bf16[512,8192]{1,0:T(8,128)(2,1)} %dosage_ref.1, bf16[512,32]{1,0:T(8,128)(2,1)S(1)} %copy.10.cov_ref, bf16[1,512]{1,0:T(2,128)(2,1)S(1)} %reshape.21.pheno_ref, s32[1,512]{1,0:T(1,128)S(1)} %bitcast.7), custom_call_target="tpu_custom_call" | custom-call | tf_op jit(solution)/shard_map/products/pallas_call | solution.py:116
  19.7 1.6 %collective-permute-start = (f32[4,4,208,128]{3,2,1,0:T(8,128)S(1)}, f32[4,4,208,128]{3,2,1,0:T(8,128)S(1)}, u32[]{:S(2)}, u32[]{:S(2)}) collective-permute-start(f32[4,4,208,128]{3,2,1,0:T(8,128)S(1)} %get-tuple-element.29), channel_id=1, source_target_pairs={{0,16},{16,0},{1,17},{17,1},{2,18},{18,2},{3,19},{19,3},{4,20},{20... | collective-permute-start | bytes 5111816 | tf_op jit(solution)/shard_map/ppermute | solution.py:366
  21.3 3.2 %collective-permute-done.recv_ref = f32[4,4,208,128]{3,2,1,0:T(8,128)S(1)} collective-permute-done((f32[4,4,208,128]{3,2,1,0:T(8,128)S(1)}, f32[4,4,208,128]{3,2,1,0:T(8,128)S(1)}, u32[]{:S(2)}, u32[]{:S(2)}) %collective-permute-start) | collective-permute-done | bytes 1703968 | tf_op jit(solution)/shard_map/ppermute | solution.py:366
  24.6 0.2 first_sum.1
  24.7 0.0 copy-start.3
  24.7 0.0 copy-start
  24.8 0.0 copy-start.1
  24.8 1.8 %collective-permute-start.1 = (f32[4,208,128]{2,1,0:T(8,128)S(1)}, f32[4,208,128]{2,1,0:T(8,128)S(1)}, u32[]{:S(2)}, u32[]{:S(2)}) collective-permute-start(f32[4,208,128]{2,1,0:T(8,128)S(1)} %get-tuple-element.31), channel_id=1, source_target_pairs={{0,32},{1,33},{2,34},{3,35},{4,36},{5,37},{6,38},{7,39},{8,40},{9,... | collective-permute-start | bytes 1277960 | tf_op jit(solution)/shard_map/ppermute | solution.py:369
  26.6 3.3 %collective-permute-start.2 = (f32[4,208,128]{2,1,0:T(8,128)S(1)}, f32[4,208,128]{2,1,0:T(8,128)S(1)}, u32[]{:S(2)}, u32[]{:S(2)}) collective-permute-start(f32[4,208,128]{2,1,0:T(8,128)S(1)} %get-tuple-element.32), channel_id=1, source_target_pairs={{0,64},{1,65},{2,66},{3,67},{4,68},{5,69},{6,70},{7,71},{8,72},{9,... | collective-permute-start | bytes 1277960 | tf_op jit(solution)/shard_map/ppermute | solution.py:369
  29.9 0.7 collective-permute-start.3
  30.6 3.6 %collective-permute-done.1.r1 = f32[4,208,128]{2,1,0:T(8,128)S(1)} collective-permute-done((f32[4,208,128]{2,1,0:T(8,128)S(1)}, f32[4,208,128]{2,1,0:T(8,128)S(1)}, u32[]{:S(2)}, u32[]{:S(2)}) %collective-permute-start.1) | collective-permute-done | bytes 426016 | tf_op jit(solution)/shard_map/ppermute | solution.py:369
  34.2 5.7 %collective-permute-done.2.r2 = f32[4,208,128]{2,1,0:T(8,128)S(1)} collective-permute-done((f32[4,208,128]{2,1,0:T(8,128)S(1)}, f32[4,208,128]{2,1,0:T(8,128)S(1)}, u32[]{:S(2)}, u32[]{:S(2)}) %collective-permute-start.2) | collective-permute-done | bytes 426016 | tf_op jit(solution)/shard_map/ppermute | solution.py:369
  39.9 0.1 second_sum.1
  40.0 1.3 %collective-permute-start.4 = (f32[208,128]{1,0:T(8,128)S(1)}, f32[208,128]{1,0:T(8,128)S(1)}, u32[]{:S(2)}, u32[]{:S(2)}) collective-permute-start(f32[208,128]{1,0:T(8,128)S(1)} %get-tuple-element.35), channel_id=1, source_target_pairs={{0,1},{1,2},{2,3},{3,0},{4,5},{5,6},{6,7},{7,4},{8,9},{9,10},{10,1... | collective-permute-start | bytes 319496 | tf_op jit(solution)/shard_map/ppermute | solution.py:372
  41.3 2.4 %collective-permute-start.5 = (f32[208,128]{1,0:T(8,128)S(1)}, f32[208,128]{1,0:T(8,128)S(1)}, u32[]{:S(2)}, u32[]{:S(2)}) collective-permute-start(f32[208,128]{1,0:T(8,128)S(1)} %get-tuple-element.36), channel_id=1, source_target_pairs={{0,2},{1,3},{2,0},{3,1},{4,6},{5,7},{6,4},{7,5},{8,10},{9,11},{10,... | collective-permute-start | bytes 319496 | tf_op jit(solution)/shard_map/ppermute | solution.py:372
  43.8 1.2 %collective-permute-start.6 = (f32[208,128]{1,0:T(8,128)S(1)}, f32[208,128]{1,0:T(8,128)S(1)}, u32[]{:S(2)}, u32[]{:S(2)}) collective-permute-start(f32[208,128]{1,0:T(8,128)S(1)} %get-tuple-element.37), channel_id=1, source_target_pairs={{0,3},{1,0},{2,1},{3,2},{4,7},{5,4},{6,5},{7,6},{8,11},{9,8},{10,9... | collective-permute-start | bytes 319496 | tf_op jit(solution)/shard_map/ppermute | solution.py:372
  44.9 2.1 %collective-permute-done.5.q2 = f32[208,128]{1,0:T(8,128)S(1)} collective-permute-done((f32[208,128]{1,0:T(8,128)S(1)}, f32[208,128]{1,0:T(8,128)S(1)}, u32[]{:S(2)}, u32[]{:S(2)}) %collective-permute-start.5) | collective-permute-done | bytes 106528 | tf_op jit(solution)/shard_map/ppermute | solution.py:372
  47.0 0.3 collective-permute-done.6.q3
  47.3 2.1 %route.1 = (f32[112,128]{1,0:T(8,128)S(1)}, f32[112,128]{1,0:T(8,128)S(1)}, f32[112,128]{1,0:T(8,128)S(1)}, f32[112,128]{1,0:T(8,128)S(1)}, f32[16,128]{1,0:T(8,128)S(1)}) custom-call(s32[256]{0:T(256)S(1)} %copy-done.3, f32[208,128]{1,0:T(8,128)S(1)} %get-tuple-element.34.b0, f32[208,128]{1,0:T(8,128)S(1)} %collective-permute-done.4.q1, ...), custom_call_target="tpu_custom_call" | custom-call | tf_op jit(solution)/shard_map/route/pallas_call | solution.py:375
  49.4 1.5 %collective-permute-start.7 = (f32[112,128]{1,0:T(8,128)S(1)}, f32[112,128]{1,0:T(8,128)S(1)}, u32[]{:S(2)}, u32[]{:S(2)}) collective-permute-start(f32[112,128]{1,0:T(8,128)S(1)} %get-tuple-element.43), channel_id=1, source_target_pairs={{0,4},{4,8},{8,12},{12,0},{1,5},{5,9},{9,13},{13,1},{2,6},{6,10},{... | collective-permute-start | bytes 172040 | tf_op jit(solution)/shard_map/ppermute | solution.py:380
  50.9 2.5 %collective-permute-start.8 = (f32[112,128]{1,0:T(8,128)S(1)}, f32[112,128]{1,0:T(8,128)S(1)}, u32[]{:S(2)}, u32[]{:S(2)}) collective-permute-start(f32[112,128]{1,0:T(8,128)S(1)} %get-tuple-element.44), channel_id=1, source_target_pairs={{0,8},{4,12},{8,0},{12,4},{1,9},{5,13},{9,1},{13,5},{2,10},{6,14},... | collective-permute-start | bytes 172040 | tf_op jit(solution)/shard_map/ppermute | solution.py:380
  53.4 1.1 %collective-permute-start.9 = (f32[112,128]{1,0:T(8,128)S(1)}, f32[112,128]{1,0:T(8,128)S(1)}, u32[]{:S(2)}, u32[]{:S(2)}) collective-permute-start(f32[112,128]{1,0:T(8,128)S(1)} %get-tuple-element.45), channel_id=1, source_target_pairs={{0,12},{4,0},{8,4},{12,8},{1,13},{5,1},{9,5},{13,9},{2,14},{6,2},{... | collective-permute-start | bytes 172040 | tf_op jit(solution)/shard_map/ppermute | solution.py:380
  54.5 10.8 %prepare.1 = (s32[16]{0:T(128)S(1)}, s32[16]{0:T(128)S(1)}, s32[16]{0:T(128)S(1)}, f32[128,128]{1,0:T(8,128)S(1)}, f32[128,128]{1,0:T(8,128)S(1)}, /*index=5*/f32[16,128]{1,0:T(8,128)S(1)}, f32[16,128]{1,0:T(8,128)S(1)}) custom-call(s32[256]{0:T(256)S(1)} %copy-done.3, f32[16,128]{1,0:T(8,128)S(1)} %get-tuple-element.38.moment_ref, f32[256,128]{1,0:T(8,128)S(1)} %bitcast.5, ...), custom_call_target="tpu_custom_call" | custom-call | tf_op jit(solution)/shard_map/prepare/pallas_call | solution.py:383
  65.4 0.0 collective-permute-done.7.w1
  65.4 1.3 %scores.1 = f32[8,48,128]{2,1,0:T(8,128)S(1)} custom-call(s32[16]{0:T(128)S(1)} %get-tuple-element.40.source_ref, s32[16]{0:T(128)S(1)} %get-tuple-element.41.rank_ref, f32[112,128]{1,0:T(8,128)S(1)} %get-tuple-element.42.w0, f32[112,128]{1,0:T(8,128)S(1)} %collective-permute-done.7.w1, f32[112,128]{1,0:T(8,128)S(1)} %collective-permute-done.8.w2, ...), custom_call_target="tpu_custom_call" | custom-call | tf_op jit(solution)/shard_map/scores/pallas_call | solution.py:389
  66.7 14.0 %all_to_all.5.parts_ref = f32[8,48,128]{2,1,0:T(8,128)S(1)} all-to-all(f32[8,48,128]{2,1,0:T(8,128)S(1)} %scores.1), channel_id=1, replica_groups=mesh['x'=4,'k'=2,'g'=4,'c'=4] {'x','k'}, dimensions={0} | all-to-all | bytes 393216 | tf_op jit(solution)/shard_map/all_to_all | solution.py:393
  80.7 1.6 %finish.1 = (f32[2,128,128]{2,1,0:T(8,128)}, f32[8,8]{1,0:T(8,128)}, f32[1,8]{1,0:T(1,128)}) custom-call(s32[16]{0:T(128)S(1)} %get-tuple-element.39.local_gene_ref, f32[8,48,128]{2,1,0:T(8,128)S(1)} %all_to_all.5.parts_ref, f32[16,128]{1,0:T(8,128)S(1)} %get-tuple-element.49.weights_ref), custom_call_target="tpu_custom_call" | custom-call | tf_op jit(solution)/shard_map/finish/pallas_call | solution.py:394
  (8 shorter events, 0.0 us)
Async XLA Ops:
  2.2 0.7 copy-start.2
  2.9 0.7 copy-start.4
  19.7 4.8 %collective-permute-start = (f32[4,4,208,128]{3,2,1,0:T(8,128)S(1)}, f32[4,4,208,128]{3,2,1,0:T(8,128)S(1)}, u32[]{:S(2)}, u32[]{:S(2)}) collective-permute-start(f32[4,4,208,128]{3,2,1,0:T(8,128)S(1)} %get-tuple-element.29), channel_id=1, source_target_pairs={{0,16},{16,0},{1,17},{17,1},{2,18},{18,2},{3,19},{19,3},{4,20},{20... | collective-permute-start | bytes 5111816 | tf_op jit(solution)/shard_map/ppermute | solution.py:366
  24.7 22.6 %copy-start.3 = (s32[256]{0:T(256)S(1)}, s32[256]{0:T(256)}, u32[]{:S(2)}) copy-start(s32[256]{0:T(256)} %owner_ref.5) | copy-start | bytes 3076
  24.7 29.8 %copy-start = (f32[32768]{0:T(1024)S(1)}, f32[32768]{0:T(1024)}, u32[]{:S(2)}) copy-start(f32[32768]{0:T(1024)} %param.11) | copy-start | bytes 393220
  24.8 29.8 %copy-start.1 = (s32[32768]{0:T(1024)S(1)}, s32[32768]{0:T(1024)}, u32[]{:S(2)}) copy-start(s32[32768]{0:T(1024)} %param.13) | copy-start | bytes 393220
  24.8 9.4 %collective-permute-start.1 = (f32[4,208,128]{2,1,0:T(8,128)S(1)}, f32[4,208,128]{2,1,0:T(8,128)S(1)}, u32[]{:S(2)}, u32[]{:S(2)}) collective-permute-start(f32[4,208,128]{2,1,0:T(8,128)S(1)} %get-tuple-element.31), channel_id=1, source_target_pairs={{0,32},{1,33},{2,34},{3,35},{4,36},{5,37},{6,38},{7,39},{8,40},{9,... | collective-permute-start | bytes 1277960 | tf_op jit(solution)/shard_map/ppermute | solution.py:369
  26.6 13.4 %collective-permute-start.2 = (f32[4,208,128]{2,1,0:T(8,128)S(1)}, f32[4,208,128]{2,1,0:T(8,128)S(1)}, u32[]{:S(2)}, u32[]{:S(2)}) collective-permute-start(f32[4,208,128]{2,1,0:T(8,128)S(1)} %get-tuple-element.32), channel_id=1, source_target_pairs={{0,64},{1,65},{2,66},{3,67},{4,68},{5,69},{6,70},{7,71},{8,72},{9,... | collective-permute-start | bytes 1277960 | tf_op jit(solution)/shard_map/ppermute | solution.py:369
  29.9 10.1 %collective-permute-start.3 = (f32[4,208,128]{2,1,0:T(8,128)S(1)}, f32[4,208,128]{2,1,0:T(8,128)S(1)}, u32[]{:S(2)}, u32[]{:S(2)}) collective-permute-start(f32[4,208,128]{2,1,0:T(8,128)S(1)} %get-tuple-element.33), channel_id=1, source_target_pairs={{0,96},{1,97},{2,98},{3,99},{4,100},{5,101},{6,102},{7,103},{8,104... | collective-permute-start | bytes 1277960 | tf_op jit(solution)/shard_map/ppermute | solution.py:369
  40.0 4.9 %collective-permute-start.4 = (f32[208,128]{1,0:T(8,128)S(1)}, f32[208,128]{1,0:T(8,128)S(1)}, u32[]{:S(2)}, u32[]{:S(2)}) collective-permute-start(f32[208,128]{1,0:T(8,128)S(1)} %get-tuple-element.35), channel_id=1, source_target_pairs={{0,1},{1,2},{2,3},{3,0},{4,5},{5,6},{6,7},{7,4},{8,9},{9,10},{10,1... | collective-permute-start | bytes 319496 | tf_op jit(solution)/shard_map/ppermute | solution.py:372
  41.3 5.7 %collective-permute-start.5 = (f32[208,128]{1,0:T(8,128)S(1)}, f32[208,128]{1,0:T(8,128)S(1)}, u32[]{:S(2)}, u32[]{:S(2)}) collective-permute-start(f32[208,128]{1,0:T(8,128)S(1)} %get-tuple-element.36), channel_id=1, source_target_pairs={{0,2},{1,3},{2,0},{3,1},{4,6},{5,7},{6,4},{7,5},{8,10},{9,11},{10,... | collective-permute-start | bytes 319496 | tf_op jit(solution)/shard_map/ppermute | solution.py:372
  43.8 3.6 %collective-permute-start.6 = (f32[208,128]{1,0:T(8,128)S(1)}, f32[208,128]{1,0:T(8,128)S(1)}, u32[]{:S(2)}, u32[]{:S(2)}) collective-permute-start(f32[208,128]{1,0:T(8,128)S(1)} %get-tuple-element.37), channel_id=1, source_target_pairs={{0,3},{1,0},{2,1},{3,2},{4,7},{5,4},{6,5},{7,6},{8,11},{9,8},{10,9... | collective-permute-start | bytes 319496 | tf_op jit(solution)/shard_map/ppermute | solution.py:372
  49.4 16.0 %collective-permute-start.7 = (f32[112,128]{1,0:T(8,128)S(1)}, f32[112,128]{1,0:T(8,128)S(1)}, u32[]{:S(2)}, u32[]{:S(2)}) collective-permute-start(f32[112,128]{1,0:T(8,128)S(1)} %get-tuple-element.43), channel_id=1, source_target_pairs={{0,4},{4,8},{8,12},{12,0},{1,5},{5,9},{9,13},{13,1},{2,6},{6,10},{... | collective-permute-start | bytes 172040 | tf_op jit(solution)/shard_map/ppermute | solution.py:380
  50.9 14.5 %collective-permute-start.8 = (f32[112,128]{1,0:T(8,128)S(1)}, f32[112,128]{1,0:T(8,128)S(1)}, u32[]{:S(2)}, u32[]{:S(2)}) collective-permute-start(f32[112,128]{1,0:T(8,128)S(1)} %get-tuple-element.44), channel_id=1, source_target_pairs={{0,8},{4,12},{8,0},{12,4},{1,9},{5,13},{9,1},{13,5},{2,10},{6,14},... | collective-permute-start | bytes 172040 | tf_op jit(solution)/shard_map/ppermute | solution.py:380
  53.4 12.0 %collective-permute-start.9 = (f32[112,128]{1,0:T(8,128)S(1)}, f32[112,128]{1,0:T(8,128)S(1)}, u32[]{:S(2)}, u32[]{:S(2)}) collective-permute-start(f32[112,128]{1,0:T(8,128)S(1)} %get-tuple-element.45), channel_id=1, source_target_pairs={{0,12},{4,0},{8,4},{12,8},{1,13},{5,1},{9,5},{13,9},{2,14},{6,2},{... | collective-permute-start | bytes 172040 | tf_op jit(solution)/shard_map/ppermute | solution.py:380

commit v2 on v1

v2 whole, which is shorter than its diff:
```python
import jax
import jax.numpy as jnp
from jax import lax
from jax.experimental import pallas as pl
from jax.experimental.pallas import tpu as pltpu
from jax.sharding import Mesh, PartitionSpec as P

AXES = ("x", "k", "g", "c")
RHO_GRID = (0.0, 0.01, 0.04, 0.09, 0.16, 0.25, 0.5, 1.0)
SAMPLES = 16384
WIDTH = 128
COVS = 32
LOCAL = 64
STEP = 16
LOAD = 16
CHUNK = 208
ROUTED = 112
FINAL = 48
F32 = jnp.float32
HIGHEST = lax.Precision.HIGHEST


def params(**kwargs):
    return pltpu.CompilerParams(vmem_limit_bytes=48 * 1024 * 1024, **kwargs)


def iota(shape, dim):
    return lax.broadcasted_iota(jnp.int32, shape, dim)


def products_kernel(owner_hbm, dosage_ref, cov_hbm, pheno_hbm, mask_hbm, keep_ref, send_ref,
                    owner_ref, cov_ref, pheno_ref, mask_ref,
                    panel_ref, left_ref, packed_ref, cross_ref, rest_ref, moment_ref, count_ref,
                    sems, small_sems):
    x, k, g, c = (lax.axis_index(a) for a in AXES)
    samples = dosage_ref.shape[0]

    def fetch(i):
        at = pl.ds(pl.multiple_of(i * LOAD * WIDTH, WIDTH), LOAD * WIDTH)
        return pltpu.make_async_copy(dosage_ref.at[:, at], panel_ref.at[i], sems.at[i])

    small = [
        pltpu.make_async_copy(src, dst, small_sems.at[i])
        for i, (src, dst) in enumerate([(cov_hbm, cov_ref), (pheno_hbm, pheno_ref),
                                        (mask_hbm, mask_ref), (owner_hbm, owner_ref)])]
    for copy in small:
        copy.start()
    for i in range(LOCAL // LOAD):
        fetch(i).start()

    def place(core, xd, cd):
        first = core == 0
        d = jnp.where(first, (xd - x) & 3, (cd - c) & 3)
        j = jnp.where(first, cd, xd)
        return d, j

    rest_ref[...] = jnp.zeros_like(rest_ref)
    for i in range(4):
        count_ref[i] = 0
    for copy in small:
        copy.wait()
    cov_rows = cov_ref[...]
    pheno = jnp.concatenate([pheno_ref[i:i + 1, :] for i in range(samples // WIDTH)], 1)
    right = jnp.concatenate(
        [cov_rows, pheno, jnp.zeros((WIDTH - COVS - 1, cov_rows.shape[1]), jnp.bfloat16)], 0)
    keep = mask_ref[...].astype(F32).astype(jnp.bfloat16)
    masked = right[:48] * keep
    left_ref[...] = masked
    m = lax.dot_general(masked[:COVS], right, (((1,), (1,)), ((), ())),
                        preferred_element_type=F32)
    moment_ref[...] = pltpu.roll(m[:16], 32, 1) + pltpu.roll(m[16:32], 65, 1)

    keep_row = mask_ref[...].astype(F32).astype(jnp.bfloat16)
    row, lane = iota((64, WIDTH), 0), iota((64, WIDTH), 1)
    take_low = (lane < 64) & (row > lane)
    eye = iota((WIDTH, WIDTH), 0) == iota((WIDTH, WIDTH), 1)
    def run(step, _):
        for pair in range(STEP // 2):
            load = step * (STEP // LOAD) + pair * 2 // LOAD
            if pair * 2 % LOAD == 0:
                fetch(load).wait()
            lo = pair * 256 % (LOAD * WIDTH)
            panel = panel_ref[load, :, lo:lo + 256]
            left = jnp.concatenate([panel.T * keep_row, left_ref[...]], 0)
            out = jnp.dot(left, panel, preferred_element_type=F32)
            for half in range(2):
                lo = half * WIDTH
                block = out[lo:lo + WIDTH, lo:lo + WIDTH]
                bucket = step * STEP + pair * 2 + half
                cd = owner_ref[g * LOCAL + bucket] & 3
                pos = count_ref[cd]
                count_ref[cd] = pos + 1
                slot = pair * 2 + half
                packed_ref[slot] = jnp.where(take_low, pltpu.roll(block[64:], 64, 1), block[:64])
                rows = pl.ds(pl.multiple_of(pos * 8, 8), 8)
                for xd in range(4):
                    d, j = place(k, xd, cd)
                    keep_ref[d, j, rows, :] = packed_ref[
                        slot, pl.ds(pl.multiple_of((2 * xd + k) * 8, 8), 8), :]
                    d, j = place(1 - k, xd, cd)
                    send_ref[d, j, rows, :] = packed_ref[
                        slot, pl.ds(pl.multiple_of((2 * xd + 1 - k) * 8, 8), 8), :]
                cross_ref[cd, pl.ds(pl.multiple_of(pos * COVS, 8), COVS), :] = out[
                    256:256 + COVS, lo:lo + WIDTH]
                rest_ref[cd, pl.ds(pos, 1), :] = out[256 + COVS:257 + COVS, lo:lo + WIDTH]
                rest_ref[cd, pl.ds(pos + 16, 1), :] = jnp.sum(
                    jnp.where(eye, block, 0.0), axis=0, keepdims=True)
        return 0

    lax.fori_loop(0, LOCAL // STEP, run, 0)

    for cd in range(4):
        for q in range(5):
            if q < 4:
                turned = cross_ref[cd, q * WIDTH:(q + 1) * WIDTH, :].T
            else:
                turned = rest_ref[cd].T
            for t in range(8):
                tile = turned[16 * t:16 * t + 16]
                if q == 4:
                    tile = tile + moment_ref[...]
                rows = slice(128 + 16 * q, 144 + 16 * q)
                d, j = place(t & 1, t >> 1, cd)

                @pl.when(k == (t & 1))
                def _():
                    keep_ref[d, j, rows, :] = tile

                @pl.when(k != (t & 1))
                def _():
                    send_ref[d, j, rows, :] = tile


def products(owner, dosage, cov, pheno, mask):
    samples = dosage.shape[0]
    out = jax.ShapeDtypeStruct((4, 4, CHUNK, WIDTH), F32)
    vmem = pl.BlockSpec(memory_space=pltpu.VMEM)
    return pl.pallas_call(
        products_kernel,
        out_shape=(out, out),
        in_specs=[pl.BlockSpec(memory_space=pltpu.HBM)] * 5,
        out_specs=(vmem, vmem),
        scratch_shapes=[
            pltpu.SMEM(owner.shape, jnp.int32),
            pltpu.VMEM(cov.shape, jnp.bfloat16),
            pltpu.VMEM(pheno.shape, jnp.bfloat16),
            pltpu.VMEM(mask.shape, jnp.int32),
            pltpu.VMEM((LOCAL // LOAD, samples, LOAD * WIDTH), jnp.bfloat16),
            pltpu.VMEM((48, samples), jnp.bfloat16),
            pltpu.VMEM((STEP, 64, WIDTH), F32),
            pltpu.VMEM((4, 16 * COVS, WIDTH), F32),
            pltpu.VMEM((4, WIDTH, WIDTH), F32),
            pltpu.VMEM((16, WIDTH), F32),
            pltpu.SMEM((4,), jnp.int32),
            pltpu.SemaphoreType.DMA((LOCAL // LOAD,)),
            pltpu.SemaphoreType.DMA((4,)),
        ],
        compiler_params=params(),
        name="products",
    )(*[pltpu.with_memory_space_constraint(a, pltpu.HBM)
        for a in (owner, dosage, cov, pheno, mask)])


def first_sum_kernel(keep_ref, recv_ref, *outs):
    for d in range(4):
        outs[d][...] = keep_ref[d] + recv_ref[d]


def second_sum_kernel(a0, r2, r1, r3, _, *outs):
    x, k, g, c = (lax.axis_index(a) for a in AXES)
    base = jnp.where(k == 0, c, x)
    for d in range(4):
        j = (base + d) & 3
        outs[d][...] = (a0[j] + r1[j]) + (r2[j] + r3[j])


def vmem_call(kernel, shapes, name, n_in, scratch=(), smem_in=0, smem_out=(), any_in=0):
    specs = [pl.BlockSpec(memory_space=pltpu.SMEM)] * smem_in + [
        pl.BlockSpec(memory_space=pltpu.VMEM)] * (n_in - smem_in - any_in) + [
        pl.BlockSpec(memory_space=pl.ANY)] * any_in
    return pl.pallas_call(
        kernel,
        out_shape=tuple(shapes),
        in_specs=specs,
        out_specs=tuple(
            pl.BlockSpec(memory_space=pltpu.SMEM if i in smem_out else pltpu.VMEM)
            for i in range(len(shapes))),
        scratch_shapes=scratch,
        compiler_params=params(),
        name=name,
    )


def route_kernel(turn_ref, slot_at_ref, b0, q2, q1, q3, e0, e1, e2, e3, moment_ref, total_ref,
                 slot_ref):
    total_ref[...] = (b0[...] + q1[...]) + (q2[...] + q3[...])
    rest = total_ref[192:208, :]
    moment_ref[...] = rest
    slot_ref[...] = jnp.zeros_like(slot_ref)
    lane = iota((16, WIDTH), 1)
    for pos in range(16):
        d, pr = turn_ref[pos], slot_at_ref[pos]
        slot_ref[d, pl.ds(pl.multiple_of(pr * 8, 8), 8), :] = total_ref[8 * pos:8 * pos + 8, :]
        tile = total_ref[128 + 16 * (pos >> 2):144 + 16 * (pos >> 2), :]
        tile = pltpu.roll(tile, (32 * (pr - pos)) & 127, 1)
        at = pl.ds(pl.multiple_of(64 + 16 * (pr >> 2), 16), 16)
        slot_ref[d, at, :] = jnp.where((lane >> 5) == (pr & 3), tile, slot_ref[d, at, :])
        slot_ref[d, 96:112, :] = jnp.where(
            (lane == pr) | (lane == pr + 16), pltpu.roll(rest, (pr - pos) & 127, 1),
            slot_ref[d, 96:112, :])
    for d, out in enumerate((e0, e1, e2, e3)):
        out[...] = slot_ref[d]


def layout_kernel(owner_ref, weight_ref, gene_ref, _, turn_ref, slot_at_ref, source_ref, rank_ref,
                  local_gene_ref, scale_ref, weights_ref, pad_ref, count_ref):
    x, k, g, c = (lax.axis_index(a) for a in AXES)
    me = g * 4 + c
    for i in range(6):
        count_ref[i] = 0
    pad_ref[...] = jnp.zeros_like(pad_ref)

    def outgoing(i, _):
        owner = owner_ref[g * LOCAL + i]

        @pl.when((owner & 3) == c)
        def _():
            pos = count_ref[4]
            count_ref[4] = pos + 1
            gd = owner >> 2
            pr = count_ref[gd]
            count_ref[gd] = pr + 1
            turn_ref[pos] = (gd - g) & 3
            slot_at_ref[pos] = pr

        return 0

    lax.fori_loop(0, LOCAL, outgoing, 0)
    count_ref[4] = 0

    for source in range(4):
        count_ref[5] = 0

        def owned(i, _):
            bucket = source * LOCAL + i

            @pl.when(owner_ref[bucket] == me)
            def _():
                r = count_ref[4]
                count_ref[4] = r + 1
                pr = count_ref[5]
                count_ref[5] = pr + 1
                source_ref[r] = (g - source) & 3
                rank_ref[r] = pr
                genes = gene_ref[pl.ds(bucket, 1), :]
                local_gene_ref[r] = jnp.max(genes) - me * 8
                pad_ref[pl.ds(r, 1), :] = jnp.where(
                    genes >= 0, weight_ref[pl.ds(bucket, 1), :], 0.0)

            return 0

        lax.fori_loop(0, LOCAL, owned, 0)

    weights_ref[...] = pad_ref[:16, :]
    pad_ref[...] = pad_ref[...].T
    mine = pad_ref[pl.ds(pl.multiple_of((2 * x + k) * 16, 16), 16), :]
    by16 = pltpu.roll(mine, 16, 1)
    scale_ref[...] = (mine * (1.0 / 128.0) + by16 * by16 * (1.0 / SAMPLES)
                      + pltpu.roll(mine, 32, 1))


def solve_kernel(moment_ref, whiten_ref, half_ref):
    m = moment_ref[...]
    m = jnp.concatenate([pltpu.roll(m, WIDTH - 32, 1), pltpu.roll(m, WIDTH - 65, 1)], 0)
    row, lane = iota((COVS, WIDTH), 0), iota((COVS, WIDTH), 1)
    m = jnp.where(lane <= COVS, m, jnp.where(lane == row + 64, 1.0, 0.0))
    scales = jnp.zeros((COVS, WIDTH), F32)
    for i in range(COVS):
        col = jnp.broadcast_to(m[:, i:i + 1], m.shape)
        inv = 1.0 / col[i:i + 1, :]
        scales = jnp.where(row == i, inv, scales)
        m = m - jnp.where(row > i, col * inv, 0.0) * m[i:i + 1, :]
    m = m * jnp.sqrt(scales)
    inverse = jnp.where(lane < COVS, pltpu.roll(m, 64, 1), 0.0)
    whiten_ref[...] = jnp.concatenate(
        [inverse] + [pltpu.roll(inverse, 32 * q, 1) for q in range(1, 4)], 0)
    half = jnp.concatenate([jnp.broadcast_to(m[:, COVS:COVS + 1], m.shape)] * 4, 0)
    row, lane = iota((WIDTH, WIDTH), 0), iota((WIDTH, WIDTH), 1)
    half_ref[...] = jnp.where(lane == (row >> 5), half, 0.0)


def scores_kernel(source_ref, rank_ref, w0, w2, w1, w3, whiten_ref, half_ref, scale_ref,
                  out_ref, slot_ref, cross_ref):
    for d, ref in enumerate((w0, w1, w2, w3)):
        slot_ref[d] = ref[...]
    lane = iota((16, WIDTH), 1)
    rest = jnp.zeros((16, WIDTH), F32)
    for group in range(4):
        tile = jnp.zeros((16, WIDTH), F32)
        for q in range(4):
            r = group * 4 + q
            d, pr = source_ref[r], rank_ref[r]
            out_ref[r >> 1, 8 * (r & 1):8 * (r & 1) + 8, :] = slot_ref[
                d, pl.ds(pl.multiple_of(pr * 8, 8), 8), :]
            part = slot_ref[d, pl.ds(pl.multiple_of(64 + 16 * (pr >> 2), 16), 16), :]
            part = pltpu.roll(part, (32 * (q - pr)) & 127, 1)
            tile = jnp.where((lane >> 5) == q, part, tile)
            more = pltpu.roll(slot_ref[d, 96:112, :], (r - pr) & 127, 1)
            rest = jnp.where((lane == r) | (lane == r + 16), more, rest)
        cross_ref[group * 16:group * 16 + 16, :] = tile
    whitened = lax.dot_general(cross_ref[...], whiten_ref[...], (((1,), (1,)), ((), ())),
                               precision=HIGHEST, preferred_element_type=F32)
    row, col = iota((WIDTH, WIDTH), 0), iota((WIDTH, WIDTH), 1)
    ones = jnp.where(col == (row >> 5) + 16, 1.0, 0.0)
    taken = (jnp.dot(whitened, half_ref[...], precision=HIGHEST, preferred_element_type=F32)
             + jnp.dot(whitened * whitened, ones, precision=HIGHEST, preferred_element_type=F32))
    for group in range(4):
        rest = rest - pltpu.roll(taken[group * 16:group * 16 + 16], 4 * group, 1)
    scale = scale_ref[...]
    rest = jnp.where(lane < 32, rest * scale, jnp.where(lane < 48, scale, 0.0))
    for t in range(8):
        out_ref[t, 16:32, :] = whitened[(t >> 1) * 16:(t >> 1) * 16 + 16]
        out_ref[t, 32:48, :] = rest


def finish_kernel(local_gene_ref, parts_ref, weights_ref, tiles_ref, rho_ref, trace_ref):
    x, k, g, c = (lax.axis_index(a) for a in AXES)
    part = 2 * x + k
    row, lane = iota((WIDTH, WIDTH), 0), iota((WIDTH, WIDTH), 1)
    whitened = jnp.concatenate([parts_ref[t, 16:32, :] for t in range(8)], 0)
    rest = jnp.concatenate([parts_ref[t, 32:48, :] for t in range(8)], 0)
    direct = ((row < 64) & ((lane >= 64) | (row <= lane))) | ((row >= 64) & (lane >= 64) & (row > lane))
    for q in range(2):
        rank = 2 * part + q
        packed = jnp.concatenate([parts_ref[t, 8 * q:8 * q + 8, :] for t in range(8)], 0)
        full = jnp.concatenate([packed, pltpu.roll(packed, 64, 1)], 0)
        gram = jnp.where(direct, full, full.T)
        w = jnp.where((lane >> 5) == 2 * (part & 1) + q, whitened, 0.0)
        projected = lax.dot_general(w, w, (((1,), (1,)), ((), ())), precision=HIGHEST,
                                    preferred_element_type=F32)
        weight_col = jnp.sum(jnp.where(lane == 32 + rank, rest, 0.0), axis=1, keepdims=True)
        diag_col = jnp.sum(jnp.where(lane == 16 + rank, rest, 0.0), axis=1, keepdims=True)
        weight_row = weights_ref[pl.ds(rank, 1), :]
        tile = weight_col * weight_row * (gram - projected) * (1.0 / SAMPLES)
        tiles_ref[q] = jnp.where(row == lane, diag_col, tile)

    row8, lane8 = iota((8, WIDTH), 0), iota((8, WIDTH), 1)
    member = jnp.zeros((8, WIDTH), F32)
    for r in range(16):
        member = jnp.where((lane8 == r) & (row8 == local_gene_ref[r]), 1.0, member)
    squares = jnp.sum(rest * rest, axis=0, keepdims=True)
    sums = jnp.sum(rest, axis=0, keepdims=True)
    table = jnp.where(row8 == 0, squares, sums)
    nt = (((1,), (1,)), ((), ()))
    by_gene = lax.dot_general(table, member, nt, precision=HIGHEST, preferred_element_type=F32)
    traces = lax.dot_general(table, pltpu.roll(member, 16, 1), nt, precision=HIGHEST,
                             preferred_element_type=F32)
    level = iota((8, 8), 0)
    rho = jnp.zeros((8, 8), F32)
    for i, value in enumerate(RHO_GRID):
        rho = jnp.where(level == i, value, rho)
    burden = by_gene[1:2, :]
    rho_ref[...] = ((1.0 - rho) * by_gene[0:1, :] + rho * (burden * burden)) * (1.0 / WIDTH)
    trace_ref[...] = traces[1:2, :] * (1.0 / WIDTH)


def turns(d, first):
    pairs = []
    for x in range(4):
        for k in range(2):
            for g in range(4):
                for c in range(4):
                    along_x = (k == 0) == first
                    xd, cd = ((x + d) % 4, c) if along_x else (x, (c + d) % 4)
                    pairs.append((((x * 2 + k) * 4 + g) * 4 + c, ((xd * 2 + k) * 4 + g) * 4 + cd))
    return pairs


def shards(dosage, covariates, phenotype, sample_mask, variant_weight, bucket_owner, variant_gene):
    samples = dosage.shape[0]
    keep, send = products(bucket_owner, dosage, covariates.T, phenotype.reshape(-1, WIDTH),
                          sample_mask.reshape(1, samples))
    recv = lax.ppermute(send, "k", [(0, 1), (1, 0)])
    chunk = jax.ShapeDtypeStruct((4, CHUNK, WIDTH), F32)
    a = vmem_call(first_sum_kernel, [chunk] * 4, "first_sum", 2)(keep, recv)
    r = {d: lax.ppermute(a[d], AXES, turns(d, True)) for d in (2, 1, 3)}
    list16 = jax.ShapeDtypeStruct((16,), jnp.int32)
    square = jax.ShapeDtypeStruct((WIDTH, WIDTH), F32)
    tile16 = jax.ShapeDtypeStruct((16, WIDTH), F32)
    turn, slot_at, source, rank, local_gene, scale, weights = vmem_call(
        layout_kernel, [list16] * 5 + [tile16] * 2, "layout", 4, smem_in=1,
        smem_out=(0, 1, 2, 3, 4), any_in=1,
        scratch=[pltpu.VMEM((WIDTH, WIDTH), F32), pltpu.SMEM((6,), jnp.int32)],
    )(bucket_owner, variant_weight.reshape(-1, WIDTH), variant_gene.reshape(-1, WIDTH), a[0])
    part = jax.ShapeDtypeStruct((CHUNK, WIDTH), F32)
    b = vmem_call(second_sum_kernel, [part] * 4, "second_sum", 5, any_in=1)(
        a[0], r[2], r[1], r[3], weights)
    q = {d: lax.ppermute(b[d], AXES, turns(d, False)) for d in (2, 1, 3)}
    routed = jax.ShapeDtypeStruct((ROUTED, WIDTH), F32)
    *e, moment = vmem_call(
        route_kernel, [routed] * 4 + [tile16], "route", 6, smem_in=2,
        scratch=[pltpu.VMEM((CHUNK, WIDTH), F32), pltpu.VMEM((4, ROUTED, WIDTH), F32)],
    )(turn, slot_at, b[0], q[2], q[1], q[3])
    w = {d: lax.ppermute(e[d], "g", [(i, (i + d) % 4) for i in range(4)]) for d in (2, 1, 3)}
    whiten, half = vmem_call(solve_kernel, [square] * 2, "solve", 1)(moment)
    (parts,) = vmem_call(
        scores_kernel, [jax.ShapeDtypeStruct((8, FINAL, WIDTH), F32)], "scores", 9, smem_in=2,
        scratch=[pltpu.VMEM((4, ROUTED, WIDTH), F32), pltpu.VMEM((64, WIDTH), F32)],
    )(source, rank, e[0], w[2], w[1], w[3], whiten, half, scale)
    parts = lax.all_to_all(parts, ("x", "k"), split_axis=0, concat_axis=0, tiled=True)
    tiles, rho, trace = vmem_call(
        finish_kernel,
        [jax.ShapeDtypeStruct((2, WIDTH, WIDTH), F32), jax.ShapeDtypeStruct((8, 8), F32),
         jax.ShapeDtypeStruct((1, 8), F32)], "finish", 3, smem_in=1,
    )(local_gene, parts, weights)
    return tiles[None], rho, trace.reshape(8)


def solution(mesh):
    grid = Mesh(mesh.devices.reshape(4, 2, 4, 4), AXES)
    rows = ("x", "k", "c")
    owners = ("g", "c")
    return jax.shard_map(
        shards,
        mesh=grid,
        in_specs=(P(rows, "g"), P(rows, None), P(rows), P(rows), P(), P(), P()),
        out_specs=(P(owners, ("x", "k"), None, None), P(None, owners), P(owners)),
        check_vma=False,
    )
```

time: 82.8 us -> 62.4 us (0.75)
  waiting for transfers between devices: 15 us -> 5.33 us
  Pallas kernels: 32.3 us -> 24.7 us
  local copies, waits for them, and re-layouts: 2.94 us -> 0.01 us
  starting transfers between devices: 17.4 us -> 19.2 us
  blocking collectives: 14 us -> 12.3 us
    ppermute x3, waiting for transfers between devices: 9.35 us -> 0.01 us  [shards(): r = {d: lax.ppermute(a[d], AXES, turns(d, True)) for d in (2, 1, 3)}]
    pallas_call x4 -> x5, Pallas kernels: 29.2 us -> 21.6 us  [the longest x1 9.16 us: products(): pl.pallas_call(products_kernel, out_shape=(out, out), in_specs=[pl.BlockS...]
    unnamed x11 -> x6, local copies, waits for them, and re-layouts: 2.25 us -> 0.01 us
    all_to_all x1, blocking collectives: 14 us -> 12.3 us  [shards(): lax.all_to_all(parts, ('x', 'k'), split_axis=0, concat_axis=0, tiled=True)]
  transfers between devices with their start and end apart: 10 -> 10, of which waited for: 5 -> 2; matrix products, arithmetic and copies ran while one was open for 0% -> 0% of each run, Pallas kernels for 13% -> 19%
where the time goes in v2:
time: 62.4 us; the launch traced here: 62.3 us
  Pallas kernels  24.7 us (40%)
  starting transfers between devices  19.2 us (31%)
  blocking collectives  12.3 us (20%)
  waiting for transfers between devices  5.33 us (9%)
  between operations  0.71 us (1%)
    all_to_all x1, blocking collectives, shards(): lax.all_to_all(parts, ('x', 'k'), split_axis=0, concat_axis=0, tiled=True)  12.3 us
    pallas_call x1, Pallas kernels, products(): pl.pallas_call(products_kernel, out_shape=(out, out), in_specs=[pl.BlockS...  9.16 us
    pallas_call x1, Pallas kernels, shards(): vmem_call(layout_kernel, [list16] * 5 + [tile16] * 2, 'layout', 4, smem_i...  8.78 us
    ppermute x3, starting transfers between devices, shards(): r = {d: lax.ppermute(a[d], AXES, turns(d, True)) for d in (2, 1, 3)}  6.43 us
    ppermute x3, starting transfers between devices, shards(): lax.ppermute(e[d], 'g', [(i, (i + d) % 4) for i in range(4)])  5.67 us
    ppermute x3, starting transfers between devices, shards(): q = {d: lax.ppermute(b[d], AXES, turns(d, False)) for d in (2, 1, 3)}  5.5 us
    ppermute x1, waiting for transfers between devices, shards(): recv = lax.ppermute(send, 'k', [(0, 1), (1, 0)])  3.22 us
    pallas_call x1, Pallas kernels, shards(): whiten, half = vmem_call(solve_kernel, [square] * 2, 'solve', 1)(moment)  2.82 us
  transfers between devices with their start and end apart: 10, of which 2 were waited for; matrix products, arithmetic and copies ran while one was open for 0% of the time, Pallas kernels for 19%

profile of v2, /device:TPU:1, one launch (start us, length us, event | category | flops | bytes accessed | tf_op | source)
XLA Modules:
  0.0 62.3 jit_solution(3055019715172378090)
XLA Ops:
  0.6 9.2 %products.1 = (f32[4,4,208,128]{3,2,1,0:T(8,128)S(1)}, f32[4,4,208,128]{3,2,1,0:T(8,128)S(1)}) custom-call(s32[256]{0:T(256)} %owner_ref.1, bf16[512,8192]{1,0:T(8,128)(2,1)} %dosage_ref.1, bf16[32,512]{1,0:T(8,128)(2,1)} %bitcast.9, bf16[4,128]{1,0:T(4,128)(2,1)} %bitcast.11, s32[1,512]{1,0:T(1,128)} %bitcast.10), custom_call_target="tpu_custom_call" | custom-call | tf_op jit(solution)/shard_map/products/pallas_call | solution.py:138
  9.8 1.6 %collective-permute-start = (f32[4,4,208,128]{3,2,1,0:T(8,128)S(1)}, f32[4,4,208,128]{3,2,1,0:T(8,128)S(1)}, u32[]{:S(2)}, u32[]{:S(2)}) collective-permute-start(f32[4,4,208,128]{3,2,1,0:T(8,128)S(1)} %get-tuple-element.31), channel_id=1, source_target_pairs={{0,16},{16,0},{1,17},{17,1},{2,18},{18,2},{3,19},{19,3},{4,20},{20... | collective-permute-start | bytes 5111816 | tf_op jit(solution)/shard_map/ppermute | solution.py:383
  11.4 3.2 %collective-permute-done.recv_ref = f32[4,4,208,128]{3,2,1,0:T(8,128)S(1)} collective-permute-done((f32[4,4,208,128]{3,2,1,0:T(8,128)S(1)}, f32[4,4,208,128]{3,2,1,0:T(8,128)S(1)}, u32[]{:S(2)}, u32[]{:S(2)}) %collective-permute-start) | collective-permute-done | bytes 1703968 | tf_op jit(solution)/shard_map/ppermute | solution.py:383
  14.6 0.2 first_sum.1
  14.8 3.8 %collective-permute-start.1 = (f32[4,208,128]{2,1,0:T(8,128)S(1)}, f32[4,208,128]{2,1,0:T(8,128)S(1)}, u32[]{:S(2)}, u32[]{:S(2)}) collective-permute-start(f32[4,208,128]{2,1,0:T(8,128)S(1)} %get-tuple-element.38), channel_id=1, source_target_pairs={{0,64},{1,65},{2,66},{3,67},{4,68},{5,69},{6,70},{7,71},{8,72},{9,... | collective-permute-start | bytes 1277960 | tf_op jit(solution)/shard_map/ppermute | solution.py:386
  18.5 0.7 %collective-permute-start.2 = (f32[4,208,128]{2,1,0:T(8,128)S(1)}, f32[4,208,128]{2,1,0:T(8,128)S(1)}, u32[]{:S(2)}, u32[]{:S(2)}) collective-permute-start(f32[4,208,128]{2,1,0:T(8,128)S(1)} %get-tuple-element.39), channel_id=1, source_target_pairs={{0,32},{1,33},{2,34},{3,35},{4,36},{5,37},{6,38},{7,39},{8,40},{9,... | collective-permute-start | bytes 1277960 | tf_op jit(solution)/shard_map/ppermute | solution.py:386
  19.3 1.9 %collective-permute-start.3 = (f32[4,208,128]{2,1,0:T(8,128)S(1)}, f32[4,208,128]{2,1,0:T(8,128)S(1)}, u32[]{:S(2)}, u32[]{:S(2)}) collective-permute-start(f32[4,208,128]{2,1,0:T(8,128)S(1)} %get-tuple-element.40), channel_id=1, source_target_pairs={{0,96},{1,97},{2,98},{3,99},{4,100},{5,101},{6,102},{7,103},{8,104... | collective-permute-start | bytes 1277960 | tf_op jit(solution)/shard_map/ppermute | solution.py:386
  21.2 0.0 copy-done
  21.2 0.0 copy-done.1
  21.2 0.0 copy-done.2
  21.2 8.8 %layout.1 = (s32[16]{0:T(128)S(1)}, s32[16]{0:T(128)S(1)}, s32[16]{0:T(128)S(1)}, s32[16]{0:T(128)S(1)}, s32[16]{0:T(128)S(1)}, /*index=5*/f32[16,128]{1,0:T(8,128)S(1)}, f32[16,128]{1,0:T(8,128)S(1)}) custom-call(s32[256]{0:T(256)S(1)} %copy-done.2, f32[256,128]{1,0:T(8,128)S(1)} %bitcast.7, s32[256,128]{1,0:T(8,128)S(1)} %bitcast.8, ...), custom_call_target="tpu_custom_call" | custom-call | tf_op jit(solution)/shard_map/layout/pallas_call | solution.py:390
  30.0 0.0 collective-permute-done.1.r2
  30.0 0.0 collective-permute-done.2.r1
  30.0 0.0 collective-permute-done.3.r3
  30.1 0.1 second_sum.1
  30.2 2.8 %collective-permute-start.4 = (f32[208,128]{1,0:T(8,128)S(1)}, f32[208,128]{1,0:T(8,128)S(1)}, u32[]{:S(2)}, u32[]{:S(2)}) collective-permute-start(f32[208,128]{1,0:T(8,128)S(1)} %get-tuple-element.43), channel_id=1, source_target_pairs={{0,2},{1,3},{2,0},{3,1},{4,6},{5,7},{6,4},{7,5},{8,10},{9,11},{10,... | collective-permute-start | bytes 319496 | tf_op jit(solution)/shard_map/ppermute | solution.py:398
  33.0 0.3 collective-permute-start.5
  33.3 2.4 %collective-permute-start.6 = (f32[208,128]{1,0:T(8,128)S(1)}, f32[208,128]{1,0:T(8,128)S(1)}, u32[]{:S(2)}, u32[]{:S(2)}) collective-permute-start(f32[208,128]{1,0:T(8,128)S(1)} %get-tuple-element.45), channel_id=1, source_target_pairs={{0,3},{1,0},{2,1},{3,2},{4,7},{5,4},{6,5},{7,6},{8,11},{9,8},{10,9... | collective-permute-start | bytes 319496 | tf_op jit(solution)/shard_map/ppermute | solution.py:398
  35.7 0.0 collective-permute-done.4.q2
  35.7 2.1 %collective-permute-done.5.q1 = f32[208,128]{1,0:T(8,128)S(1)} collective-permute-done((f32[208,128]{1,0:T(8,128)S(1)}, f32[208,128]{1,0:T(8,128)S(1)}, u32[]{:S(2)}, u32[]{:S(2)}) %collective-permute-start.5) | collective-permute-done | bytes 106528 | tf_op jit(solution)/shard_map/ppermute | solution.py:398
  37.8 0.0 collective-permute-done.6.q3
  37.8 0.7 %route.1 = (f32[112,128]{1,0:T(8,128)S(1)}, f32[112,128]{1,0:T(8,128)S(1)}, f32[112,128]{1,0:T(8,128)S(1)}, f32[112,128]{1,0:T(8,128)S(1)}, f32[16,128]{1,0:T(8,128)S(1)}) custom-call(s32[16]{0:T(128)S(1)} %get-tuple-element.36.turn_ref, s32[16]{0:T(128)S(1)} %get-tuple-element.37.slot_at_ref, f32[208,128]{1,0:T(8,128)S(1)} %get-tuple-element.42.b0, ...), custom_call_target="tpu_custom_call" | custom-call | tf_op jit(solution)/shard_map/route/pallas_call | solution.py:400
  38.5 3.0 %collective-permute-start.7 = (f32[112,128]{1,0:T(8,128)S(1)}, f32[112,128]{1,0:T(8,128)S(1)}, u32[]{:S(2)}, u32[]{:S(2)}) collective-permute-start(f32[112,128]{1,0:T(8,128)S(1)} %get-tuple-element.47), channel_id=1, source_target_pairs={{0,8},{4,12},{8,0},{12,4},{1,9},{5,13},{9,1},{13,5},{2,10},{6,14},... | collective-permute-start | bytes 172040 | tf_op jit(solution)/shard_map/ppermute | solution.py:404
  41.5 0.4 collective-permute-start.8
  41.9 2.3 %collective-permute-start.9 = (f32[112,128]{1,0:T(8,128)S(1)}, f32[112,128]{1,0:T(8,128)S(1)}, u32[]{:S(2)}, u32[]{:S(2)}) collective-permute-start(f32[112,128]{1,0:T(8,128)S(1)} %get-tuple-element.49), channel_id=1, source_target_pairs={{0,12},{4,0},{8,4},{12,8},{1,13},{5,1},{9,5},{13,9},{2,14},{6,2},{... | collective-permute-start | bytes 172040 | tf_op jit(solution)/shard_map/ppermute | solution.py:404
  44.2 2.8 %solve.1 = (f32[128,128]{1,0:T(8,128)S(1)}, f32[128,128]{1,0:T(8,128)S(1)}) custom-call(f32[16,128]{1,0:T(8,128)S(1)} %get-tuple-element.50.moment_ref), custom_call_target="tpu_custom_call" | custom-call | tf_op jit(solution)/shard_map/solve/pallas_call | solution.py:405
  47.0 0.0 collective-permute-done.7.w2
  47.0 0.0 collective-permute-done.8.w1
  47.0 0.0 collective-permute-done.9.w3
  47.0 1.3 %scores.1 = f32[8,48,128]{2,1,0:T(8,128)S(1)} custom-call(s32[16]{0:T(128)S(1)} %get-tuple-element.34.source_ref, s32[16]{0:T(128)S(1)} %get-tuple-element.35.rank_ref, f32[112,128]{1,0:T(8,128)S(1)} %get-tuple-element.46.w0, f32[112,128]{1,0:T(8,128)S(1)} %collective-permute-done.7.w2, f32[112,128]{1,0:T(8,128)S(1)} %collective-permute-done.8.w1, ...), custom_call_target="tpu_custom_call" | custom-call | tf_op jit(solution)/shard_map/scores/pallas_call | solution.py:406
  48.3 12.3 %all_to_all.5.parts_ref = f32[8,48,128]{2,1,0:T(8,128)S(1)} all-to-all(f32[8,48,128]{2,1,0:T(8,128)S(1)} %scores.1), channel_id=1, replica_groups=mesh['x'=4,'k'=2,'g'=4,'c'=4] {'x','k'}, dimensions={0} | all-to-all | bytes 393216 | tf_op jit(solution)/shard_map/all_to_all | solution.py:410
  60.6 1.6 %finish.1 = (f32[2,128,128]{2,1,0:T(8,128)}, f32[8,8]{1,0:T(8,128)}, f32[1,8]{1,0:T(1,128)}) custom-call(s32[16]{0:T(128)S(1)} %get-tuple-element.33.local_gene_ref, f32[8,48,128]{2,1,0:T(8,128)S(1)} %all_to_all.5.parts_ref, f32[16,128]{1,0:T(8,128)S(1)} %get-tuple-element.41._.weights_ref), custom_call_target="tpu_custom_call" | custom-call | tf_op jit(solution)/shard_map/finish/pallas_call | solution.py:411
  (3 shorter events, 0.0 us)
Async XLA Ops:
  9.8 4.8 %collective-permute-start = (f32[4,4,208,128]{3,2,1,0:T(8,128)S(1)}, f32[4,4,208,128]{3,2,1,0:T(8,128)S(1)}, u32[]{:S(2)}, u32[]{:S(2)}) collective-permute-start(f32[4,4,208,128]{3,2,1,0:T(8,128)S(1)} %get-tuple-element.31), channel_id=1, source_target_pairs={{0,16},{16,0},{1,17},{17,1},{2,18},{18,2},{3,19},{19,3},{4,20},{20... | collective-permute-start | bytes 5111816 | tf_op jit(solution)/shard_map/ppermute | solution.py:383
  14.6 6.6 %copy-start = (f32[32768]{0:T(1024)S(1)}, f32[32768]{0:T(1024)}, u32[]{:S(2)}) copy-start(f32[32768]{0:T(1024)} %param.11) | copy-start | bytes 393220
  14.6 6.6 %copy-start.1 = (s32[32768]{0:T(1024)S(1)}, s32[32768]{0:T(1024)}, u32[]{:S(2)}) copy-start(s32[32768]{0:T(1024)} %param.13) | copy-start | bytes 393220
  14.6 6.6 %copy-start.2 = (s32[256]{0:T(256)S(1)}, s32[256]{0:T(256)}, u32[]{:S(2)}) copy-start(s32[256]{0:T(256)} %owner_ref.1) | copy-start | bytes 3076
  14.8 15.2 %collective-permute-start.1 = (f32[4,208,128]{2,1,0:T(8,128)S(1)}, f32[4,208,128]{2,1,0:T(8,128)S(1)}, u32[]{:S(2)}, u32[]{:S(2)}) collective-permute-start(f32[4,208,128]{2,1,0:T(8,128)S(1)} %get-tuple-element.38), channel_id=1, source_target_pairs={{0,64},{1,65},{2,66},{3,67},{4,68},{5,69},{6,70},{7,71},{8,72},{9,... | collective-permute-start | bytes 1277960 | tf_op jit(solution)/shard_map/ppermute | solution.py:386
  18.5 11.5 %collective-permute-start.2 = (f32[4,208,128]{2,1,0:T(8,128)S(1)}, f32[4,208,128]{2,1,0:T(8,128)S(1)}, u32[]{:S(2)}, u32[]{:S(2)}) collective-permute-start(f32[4,208,128]{2,1,0:T(8,128)S(1)} %get-tuple-element.39), channel_id=1, source_target_pairs={{0,32},{1,33},{2,34},{3,35},{4,36},{5,37},{6,38},{7,39},{8,40},{9,... | collective-permute-start | bytes 1277960 | tf_op jit(solution)/shard_map/ppermute | solution.py:386
  19.3 10.8 %collective-permute-start.3 = (f32[4,208,128]{2,1,0:T(8,128)S(1)}, f32[4,208,128]{2,1,0:T(8,128)S(1)}, u32[]{:S(2)}, u32[]{:S(2)}) collective-permute-start(f32[4,208,128]{2,1,0:T(8,128)S(1)} %get-tuple-element.40), channel_id=1, source_target_pairs={{0,96},{1,97},{2,98},{3,99},{4,100},{5,101},{6,102},{7,103},{8,104... | collective-permute-start | bytes 1277960 | tf_op jit(solution)/shard_map/ppermute | solution.py:386
  30.2 5.5 %collective-permute-start.4 = (f32[208,128]{1,0:T(8,128)S(1)}, f32[208,128]{1,0:T(8,128)S(1)}, u32[]{:S(2)}, u32[]{:S(2)}) collective-permute-start(f32[208,128]{1,0:T(8,128)S(1)} %get-tuple-element.43), channel_id=1, source_target_pairs={{0,2},{1,3},{2,0},{3,1},{4,6},{5,7},{6,4},{7,5},{8,10},{9,11},{10,... | collective-permute-start | bytes 319496 | tf_op jit(solution)/shard_map/ppermute | solution.py:398
  33.0 4.8 %collective-permute-start.5 = (f32[208,128]{1,0:T(8,128)S(1)}, f32[208,128]{1,0:T(8,128)S(1)}, u32[]{:S(2)}, u32[]{:S(2)}) collective-permute-start(f32[208,128]{1,0:T(8,128)S(1)} %get-tuple-element.44), channel_id=1, source_target_pairs={{0,1},{1,2},{2,3},{3,0},{4,5},{5,6},{6,7},{7,4},{8,9},{9,10},{10,1... | collective-permute-start | bytes 319496 | tf_op jit(solution)/shard_map/ppermute | solution.py:398
  33.3 4.5 %collective-permute-start.6 = (f32[208,128]{1,0:T(8,128)S(1)}, f32[208,128]{1,0:T(8,128)S(1)}, u32[]{:S(2)}, u32[]{:S(2)}) collective-permute-start(f32[208,128]{1,0:T(8,128)S(1)} %get-tuple-element.45), channel_id=1, source_target_pairs={{0,3},{1,0},{2,1},{3,2},{4,7},{5,4},{6,5},{7,6},{8,11},{9,8},{10,9... | collective-permute-start | bytes 319496 | tf_op jit(solution)/shard_map/ppermute | solution.py:398
  38.5 8.5 %collective-permute-start.7 = (f32[112,128]{1,0:T(8,128)S(1)}, f32[112,128]{1,0:T(8,128)S(1)}, u32[]{:S(2)}, u32[]{:S(2)}) collective-permute-start(f32[112,128]{1,0:T(8,128)S(1)} %get-tuple-element.47), channel_id=1, source_target_pairs={{0,8},{4,12},{8,0},{12,4},{1,9},{5,13},{9,1},{13,5},{2,10},{6,14},... | collective-permute-start | bytes 172040 | tf_op jit(solution)/shard_map/ppermute | solution.py:404
  41.5 5.5 %collective-permute-start.8 = (f32[112,128]{1,0:T(8,128)S(1)}, f32[112,128]{1,0:T(8,128)S(1)}, u32[]{:S(2)}, u32[]{:S(2)}) collective-permute-start(f32[112,128]{1,0:T(8,128)S(1)} %get-tuple-element.48), channel_id=1, source_target_pairs={{0,4},{4,8},{8,12},{12,0},{1,5},{5,9},{9,13},{13,1},{2,6},{6,10},{... | collective-permute-start | bytes 172040 | tf_op jit(solution)/shard_map/ppermute | solution.py:404
  41.9 5.1 %collective-permute-start.9 = (f32[112,128]{1,0:T(8,128)S(1)}, f32[112,128]{1,0:T(8,128)S(1)}, u32[]{:S(2)}, u32[]{:S(2)}) collective-permute-start(f32[112,128]{1,0:T(8,128)S(1)} %get-tuple-element.49), channel_id=1, source_target_pairs={{0,12},{4,0},{8,4},{12,8},{1,13},{5,1},{9,5},{13,9},{2,14},{6,2},{... | collective-permute-start | bytes 172040 | tf_op jit(solution)/shard_map/ppermute | solution.py:404

commit v3 on v2

--- a/solution.py
+++ b/solution.py
@@ -13,7 +13,9 @@
 LOCAL = 64
 STEP = 16
 LOAD = 16
-CHUNK = 208
+GRAM = 128
+CROSS = 80
+CHUNK = GRAM + CROSS
 ROUTED = 112
 FINAL = 48
 F32 = jnp.float32
@@ -28,10 +30,15 @@
     return lax.broadcasted_iota(jnp.int32, shape, dim)
 
 
+def placed(core, xd, cd):
+    x, k, g, c = (lax.axis_index(a) for a in AXES)
+    first = core == 0
+    return jnp.where(first, (xd - x) & 3, (cd - c) & 3), jnp.where(first, cd, xd)
+
+
 def products_kernel(owner_hbm, dosage_ref, cov_hbm, pheno_hbm, mask_hbm, keep_ref, send_ref,
-                    owner_ref, cov_ref, pheno_ref, mask_ref,
-                    panel_ref, left_ref, packed_ref, cross_ref, rest_ref, moment_ref, count_ref,
-                    sems, small_sems):
+                    cross_ref, rest_ref, moment_ref, owner_ref, cov_ref, pheno_ref, mask_ref,
+                    panel_ref, left_ref, packed_ref, count_ref, sems, small_sems):
     x, k, g, c = (lax.axis_index(a) for a in AXES)
     samples = dosage_ref.shape[0]
 
@@ -47,12 +54,6 @@
         copy.start()
     for i in range(LOCAL // LOAD):
         fetch(i).start()
-
-    def place(core, xd, cd):
-        first = core == 0
-        d = jnp.where(first, (xd - x) & 3, (cd - c) & 3)
-        j = jnp.where(first, cd, xd)
-        return d, j
 
     rest_ref[...] = jnp.zeros_like(rest_ref)
     for i in range(4):
@@ -94,10 +95,10 @@
                 packed_ref[slot] = jnp.where(take_low, pltpu.roll(block[64:], 64, 1), block[:64])
                 rows = pl.ds(pl.multiple_of(pos * 8, 8), 8)
                 for xd in range(4):
-                    d, j = place(k, xd, cd)
+                    d, j = placed(k, xd, cd)
                     keep_ref[d, j, rows, :] = packed_ref[
                         slot, pl.ds(pl.multiple_of((2 * xd + k) * 8, 8), 8), :]
-                    d, j = place(1 - k, xd, cd)
+                    d, j = placed(1 - k, xd, cd)
                     send_ref[d, j, rows, :] = packed_ref[
                         slot, pl.ds(pl.multiple_of((2 * xd + 1 - k) * 8, 8), 8), :]
                 cross_ref[cd, pl.ds(pl.multiple_of(pos * COVS, 8), COVS), :] = out[
@@ -109,37 +110,33 @@
 
     lax.fori_loop(0, LOCAL // STEP, run, 0)
 
+
+def cross_kernel(cross_ref, rest_ref, moment_ref, keep_ref, send_ref, turned_ref):
+    k = lax.axis_index("k")
     for cd in range(4):
         for q in range(5):
+            slot = cd * 5 + q
             if q < 4:
-                turned = cross_ref[cd, q * WIDTH:(q + 1) * WIDTH, :].T
+                turned_ref[slot] = cross_ref[cd, q * WIDTH:(q + 1) * WIDTH, :].T
             else:
-                turned = rest_ref[cd].T
-            for t in range(8):
-                tile = turned[16 * t:16 * t + 16]
-                if q == 4:
-                    tile = tile + moment_ref[...]
-                rows = slice(128 + 16 * q, 144 + 16 * q)
-                d, j = place(t & 1, t >> 1, cd)
-
-                @pl.when(k == (t & 1))
-                def _():
-                    keep_ref[d, j, rows, :] = tile
-
-                @pl.when(k != (t & 1))
-                def _():
-                    send_ref[d, j, rows, :] = tile
+                moment = moment_ref[...]
+                turned_ref[slot] = rest_ref[cd].T + jnp.concatenate([moment] * 8, 0)
+            for xd in range(4):
+                for core, ref in ((k, keep_ref), (1 - k, send_ref)):
+                    d, j = placed(core, xd, cd)
+                    at = pl.ds(pl.multiple_of((2 * xd + core) * 16, 16), 16)
+                    ref[d, j, 16 * q:16 * q + 16, :] = turned_ref[slot, at, :]
 
 
 def products(owner, dosage, cov, pheno, mask):
     samples = dosage.shape[0]
-    out = jax.ShapeDtypeStruct((4, 4, CHUNK, WIDTH), F32)
     vmem = pl.BlockSpec(memory_space=pltpu.VMEM)
+    shapes = [(4, 4, GRAM, WIDTH)] * 2 + [(4, 16 * COVS, WIDTH), (4, WIDTH, WIDTH), (16, WIDTH)]
     return pl.pallas_call(
         products_kernel,
-        out_shape=(out, out),
+        out_shape=tuple(jax.ShapeDtypeStruct(shape, F32) for shape in shapes),
         in_specs=[pl.BlockSpec(memory_space=pltpu.HBM)] * 5,
-        out_specs=(vmem, vmem),
+        out_specs=(vmem,) * 5,
         scratch_shapes=[
             pltpu.SMEM(owner.shape, jnp.int32),
             pltpu.VMEM(cov.shape, jnp.bfloat16),
@@ -148,9 +145,6 @@
             pltpu.VMEM((LOCAL // LOAD, samples, LOAD * WIDTH), jnp.bfloat16),
             pltpu.VMEM((48, samples), jnp.bfloat16),
             pltpu.VMEM((STEP, 64, WIDTH), F32),
-            pltpu.VMEM((4, 16 * COVS, WIDTH), F32),
-            pltpu.VMEM((4, WIDTH, WIDTH), F32),
-            pltpu.VMEM((16, WIDTH), F32),
             pltpu.SMEM((4,), jnp.int32),
             pltpu.SemaphoreType.DMA((LOCAL // LOAD,)),
             pltpu.SemaphoreType.DMA((4,)),
@@ -166,12 +160,13 @@
         outs[d][...] = keep_ref[d] + recv_ref[d]
 
 
-def second_sum_kernel(a0, r2, r1, r3, _, *outs):
+def second_sum_kernel(a0, a2, a1, a3, c0, c2, c1, c3, _, *outs):
     x, k, g, c = (lax.axis_index(a) for a in AXES)
     base = jnp.where(k == 0, c, x)
     for d in range(4):
         j = (base + d) & 3
-        outs[d][...] = (a0[j] + r1[j]) + (r2[j] + r3[j])
+        outs[d][:GRAM] = (a0[j] + a1[j]) + (a2[j] + a3[j])
+        outs[d][GRAM:] = (c0[j] + c1[j]) + (c2[j] + c3[j])
 
 
 def vmem_call(kernel, shapes, name, n_in, scratch=(), smem_in=0, smem_out=(), any_in=0):
@@ -213,53 +208,45 @@
 
 
 def layout_kernel(owner_ref, weight_ref, gene_ref, _, turn_ref, slot_at_ref, source_ref, rank_ref,
-                  local_gene_ref, scale_ref, weights_ref, pad_ref, count_ref):
+                  genes_ref, scale_ref, weights_ref, pad_ref, label_ref, list_ref, count_ref):
     x, k, g, c = (lax.axis_index(a) for a in AXES)
     me = g * 4 + c
-    for i in range(6):
+    for i in range(4):
         count_ref[i] = 0
     pad_ref[...] = jnp.zeros_like(pad_ref)
 
-    def outgoing(i, _):
-        owner = owner_ref[g * LOCAL + i]
-
-        @pl.when((owner & 3) == c)
-        def _():
-            pos = count_ref[4]
-            count_ref[4] = pos + 1
-            gd = owner >> 2
-            pr = count_ref[gd]
-            count_ref[gd] = pr + 1
-            turn_ref[pos] = (gd - g) & 3
-            slot_at_ref[pos] = pr
-
-        return 0
-
-    lax.fori_loop(0, LOCAL, outgoing, 0)
-    count_ref[4] = 0
-
-    for source in range(4):
-        count_ref[5] = 0
-
-        def owned(i, _):
-            bucket = source * LOCAL + i
-
-            @pl.when(owner_ref[bucket] == me)
-            def _():
-                r = count_ref[4]
-                count_ref[4] = r + 1
-                pr = count_ref[5]
-                count_ref[5] = pr + 1
-                source_ref[r] = (g - source) & 3
-                rank_ref[r] = pr
-                genes = gene_ref[pl.ds(bucket, 1), :]
-                local_gene_ref[r] = jnp.max(genes) - me * 8
-                pad_ref[pl.ds(r, 1), :] = jnp.where(
-                    genes >= 0, weight_ref[pl.ds(bucket, 1), :], 0.0)
-
-            return 0
-
-        lax.fori_loop(0, LOCAL, owned, 0)
+    def scan(start, count, wanted, list_ref, value):
+        def body(i, end):
+            for u in range(8):
+                bucket = start + i * 8 + u
+                owner = owner_ref[bucket]
+                list_ref[end] = value(bucket, owner)
+                end = end + wanted(owner).astype(jnp.int32)
+            return end
+
+        lax.fori_loop(0, count // 8, body, 0)
+
+    scan(g * LOCAL, LOCAL, lambda owner: (owner & 3) == c, list_ref, lambda b, owner: owner >> 2)
+    for pos in range(16):
+        gd = list_ref[pos]
+        pr = count_ref[gd]
+        count_ref[gd] = pr + 1
+        turn_ref[pos] = (gd - g) & 3
+        slot_at_ref[pos] = pr
+    scan(0, 4 * LOCAL, lambda owner: owner == me, list_ref, lambda b, owner: b)
+    last, pr = -1, 0
+    for r in range(16):
+        bucket = list_ref[r]
+        source = bucket >> 6
+        pr = jnp.where(source == last, pr + 1, 0)
+        last = source
+        source_ref[r] = (g - source) & 3
+        rank_ref[r] = pr
+        genes = gene_ref[pl.ds(bucket, 1), :]
+        pad_ref[r:r + 1, :] = jnp.where(genes >= 0, weight_ref[pl.ds(bucket, 1), :], 0.0)
+        label_ref[r:r + 1, :] = genes
+    labels = jnp.max(label_ref[...], axis=1, keepdims=True)
+    genes_ref[...] = jnp.broadcast_to(labels - me * 8, genes_ref.shape)
 
     weights_ref[...] = pad_ref[:16, :]
     pad_ref[...] = pad_ref[...].T
@@ -274,13 +261,22 @@
     m = jnp.concatenate([pltpu.roll(m, WIDTH - 32, 1), pltpu.roll(m, WIDTH - 65, 1)], 0)
     row, lane = iota((COVS, WIDTH), 0), iota((COVS, WIDTH), 1)
     m = jnp.where(lane <= COVS, m, jnp.where(lane == row + 64, 1.0, 0.0))
-    scales = jnp.zeros((COVS, WIDTH), F32)
-    for i in range(COVS):
-        col = jnp.broadcast_to(m[:, i:i + 1], m.shape)
-        inv = 1.0 / col[i:i + 1, :]
-        scales = jnp.where(row == i, inv, scales)
-        m = m - jnp.where(row > i, col * inv, 0.0) * m[i:i + 1, :]
-    m = m * jnp.sqrt(scales)
+    first = jnp.zeros((COVS, WIDTH), F32)
+    mixed = jnp.zeros((COVS, WIDTH), F32)
+    second = jnp.ones((COVS, WIDTH), F32)
+    for i in range(0, COVS, 2):
+        col0 = jnp.broadcast_to(m[:, i:i + 1], m.shape)
+        col1 = jnp.broadcast_to(m[:, i + 1:i + 2], m.shape)
+        a, b, d = col0[i:i + 1, :], col0[i + 1:i + 2, :], col1[i + 1:i + 2, :]
+        inv = 1.0 / (a * d - b * b)
+        below = row > i + 1
+        first = jnp.where(row >= i, a, first)
+        mixed = jnp.where(row == i + 1, b, mixed)
+        second = jnp.where(row == i, a, jnp.where(row == i + 1, d, second))
+        m = (m - jnp.where(below, (col0 * d - col1 * b) * inv, 0.0) * m[i:i + 1, :]
+             - jnp.where(below, (col1 * a - col0 * b) * inv, 0.0) * m[i + 1:i + 2, :])
+    ratio = mixed / first
+    m = (m - ratio * pltpu.roll(m, 1, 0)) * lax.rsqrt(second - mixed * ratio)
     inverse = jnp.where(lane < COVS, pltpu.roll(m, 64, 1), 0.0)
     whiten_ref[...] = jnp.concatenate(
         [inverse] + [pltpu.roll(inverse, 32 * q, 1) for q in range(1, 4)], 0)
@@ -290,7 +286,8 @@
 
 
 def scores_kernel(source_ref, rank_ref, w0, w2, w1, w3, whiten_ref, half_ref, scale_ref,
-                  out_ref, slot_ref, cross_ref):
+                  mine_ref, other_ref, slot_ref, cross_ref):
+    x, k = lax.axis_index("x"), lax.axis_index("k")
     for d, ref in enumerate((w0, w1, w2, w3)):
         slot_ref[d] = ref[...]
     lane = iota((16, WIDTH), 1)
@@ -300,8 +297,6 @@
         for q in range(4):
             r = group * 4 + q
             d, pr = source_ref[r], rank_ref[r]
-            out_ref[r >> 1, 8 * (r & 1):8 * (r & 1) + 8, :] = slot_ref[
-                d, pl.ds(pl.multiple_of(pr * 8, 8), 8), :]
             part = slot_ref[d, pl.ds(pl.multiple_of(64 + 16 * (pr >> 2), 16), 16), :]
             part = pltpu.roll(part, (32 * (q - pr)) & 127, 1)
             tile = jnp.where((lane >> 5) == q, part, tile)
@@ -318,13 +313,30 @@
         rest = rest - pltpu.roll(taken[group * 16:group * 16 + 16], 4 * group, 1)
     scale = scale_ref[...]
     rest = jnp.where(lane < 32, rest * scale, jnp.where(lane < 48, scale, 0.0))
-    for t in range(8):
-        out_ref[t, 16:32, :] = whitened[(t >> 1) * 16:(t >> 1) * 16 + 16]
-        out_ref[t, 32:48, :] = rest
-
-
-def finish_kernel(local_gene_ref, parts_ref, weights_ref, tiles_ref, rho_ref, trace_ref):
+    cross_ref[...] = whitened
+    for d in range(4):
+        xd = (x + d) & 3
+        for core, ref in ((k, mine_ref), (1 - k, other_ref)):
+            for q in range(2):
+                r = 4 * xd + 2 * core + q
+                ref[d, 8 * q:8 * q + 8, :] = slot_ref[
+                    source_ref[r], pl.ds(pl.multiple_of(rank_ref[r] * 8, 8), 8), :]
+            ref[d, 16:32, :] = cross_ref[pl.ds(pl.multiple_of(16 * xd, 16), 16), :]
+            ref[d, 32:48, :] = rest
+
+
+def pair_kernel(mine_ref, got_ref, *outs):
+    k = lax.axis_index("k")
+    for d in range(4):
+        outs[d][k] = mine_ref[d]
+        outs[d][1 - k] = got_ref[d]
+
+
+def finish_kernel(genes_ref, p0, p2, p1, p3, weights_ref, tiles_ref, rho_ref, trace_ref, parts_ref):
     x, k, g, c = (lax.axis_index(a) for a in AXES)
+    for d, ref in enumerate((p0, p1, p2, p3)):
+        for core in range(2):
+            parts_ref[2 * ((x - d) & 3) + core] = ref[core]
     part = 2 * x + k
     row, lane = iota((WIDTH, WIDTH), 0), iota((WIDTH, WIDTH), 1)
     whitened = jnp.concatenate([parts_ref[t, 16:32, :] for t in range(8)], 0)
@@ -344,17 +356,17 @@
         tile = weight_col * weight_row * (gram - projected) * (1.0 / SAMPLES)
         tiles_ref[q] = jnp.where(row == lane, diag_col, tile)
 
-    row8, lane8 = iota((8, WIDTH), 0), iota((8, WIDTH), 1)
-    member = jnp.zeros((8, WIDTH), F32)
-    for r in range(16):
-        member = jnp.where((lane8 == r) & (row8 == local_gene_ref[r]), 1.0, member)
+    row8 = iota((8, WIDTH), 0)
+    member = jnp.where(genes_ref[...] == iota((16, WIDTH), 1), 1.0, 0.0)
+    none = jnp.zeros((16, WIDTH), F32)
+    rest_of = jnp.zeros((WIDTH - 32, WIDTH), F32)
     squares = jnp.sum(rest * rest, axis=0, keepdims=True)
     sums = jnp.sum(rest, axis=0, keepdims=True)
     table = jnp.where(row8 == 0, squares, sums)
-    nt = (((1,), (1,)), ((), ()))
-    by_gene = lax.dot_general(table, member, nt, precision=HIGHEST, preferred_element_type=F32)
-    traces = lax.dot_general(table, pltpu.roll(member, 16, 1), nt, precision=HIGHEST,
-                             preferred_element_type=F32)
+    by_gene = jnp.dot(table, jnp.concatenate([member, none, rest_of], 0), precision=HIGHEST,
+                      preferred_element_type=F32)[:, :8]
+    traces = jnp.dot(table, jnp.concatenate([none, member, rest_of], 0), precision=HIGHEST,
+                     preferred_element_type=F32)[:, :8]
     level = iota((8, 8), 0)
     rho = jnp.zeros((8, 8), F32)
     for i, value in enumerate(RHO_GRID):
@@ -378,23 +390,32 @@
 
 def shards(dosage, covariates, phenotype, sample_mask, variant_weight, bucket_owner, variant_gene):
     samples = dosage.shape[0]
-    keep, send = products(bucket_owner, dosage, covariates.T, phenotype.reshape(-1, WIDTH),
-                          sample_mask.reshape(1, samples))
-    recv = lax.ppermute(send, "k", [(0, 1), (1, 0)])
-    chunk = jax.ShapeDtypeStruct((4, CHUNK, WIDTH), F32)
-    a = vmem_call(first_sum_kernel, [chunk] * 4, "first_sum", 2)(keep, recv)
+    keep, send, *raw = products(bucket_owner, dosage, covariates.T, phenotype.reshape(-1, WIDTH),
+                                sample_mask.reshape(1, samples))
+    other = [(0, 1), (1, 0)]
+    recv = lax.ppermute(send, "k", other)
+    keep_cross, send_cross = vmem_call(
+        cross_kernel, [jax.ShapeDtypeStruct((4, 4, CROSS, WIDTH), F32)] * 2, "cross", 3,
+        scratch=[pltpu.VMEM((20, WIDTH, WIDTH), F32)])(*raw)
+    recv_cross = lax.ppermute(send_cross, "k", other)
+    first = [jax.ShapeDtypeStruct((4, GRAM, WIDTH), F32)] * 4
+    a = vmem_call(first_sum_kernel, first, "first_sum", 2)(keep, recv)
     r = {d: lax.ppermute(a[d], AXES, turns(d, True)) for d in (2, 1, 3)}
+    first = [jax.ShapeDtypeStruct((4, CROSS, WIDTH), F32)] * 4
+    ac = vmem_call(first_sum_kernel, first, "cross_sum", 2)(keep_cross, recv_cross)
+    rc = {d: lax.ppermute(ac[d], AXES, turns(d, True)) for d in (2, 1, 3)}
     list16 = jax.ShapeDtypeStruct((16,), jnp.int32)
     square = jax.ShapeDtypeStruct((WIDTH, WIDTH), F32)
     tile16 = jax.ShapeDtypeStruct((16, WIDTH), F32)
-    turn, slot_at, source, rank, local_gene, scale, weights = vmem_call(
-        layout_kernel, [list16] * 5 + [tile16] * 2, "layout", 4, smem_in=1,
-        smem_out=(0, 1, 2, 3, 4), any_in=1,
-        scratch=[pltpu.VMEM((WIDTH, WIDTH), F32), pltpu.SMEM((6,), jnp.int32)],
-    )(bucket_owner, variant_weight.reshape(-1, WIDTH), variant_gene.reshape(-1, WIDTH), a[0])
+    turn, slot_at, source, rank, genes, scale, weights = vmem_call(
+        layout_kernel, [list16] * 4 + [jax.ShapeDtypeStruct((16, WIDTH), jnp.int32)] + [tile16] * 2,
+        "layout", 4, smem_in=1, smem_out=(0, 1, 2, 3), any_in=1,
+        scratch=[pltpu.VMEM((WIDTH, WIDTH), F32), pltpu.VMEM((16, WIDTH), jnp.int32),
+                 pltpu.SMEM((17,), jnp.int32), pltpu.SMEM((4,), jnp.int32)],
+    )(bucket_owner, variant_weight.reshape(-1, WIDTH), variant_gene.reshape(-1, WIDTH), ac[0])
     part = jax.ShapeDtypeStruct((CHUNK, WIDTH), F32)
-    b = vmem_call(second_sum_kernel, [part] * 4, "second_sum", 5, any_in=1)(
-        a[0], r[2], r[1], r[3], weights)
+    b = vmem_call(second_sum_kernel, [part] * 4, "second_sum", 9, any_in=1)(
+        a[0], r[2], r[1], r[3], ac[0], rc[2], rc[1], rc[3], weights)
     q = {d: lax.ppermute(b[d], AXES, turns(d, False)) for d in (2, 1, 3)}
     routed = jax.ShapeDtypeStruct((ROUTED, WIDTH), F32)
     *e, moment = vmem_call(
@@ -403,16 +424,20 @@
     )(turn, slot_at, b[0], q[2], q[1], q[3])
     w = {d: lax.ppermute(e[d], "g", [(i, (i + d) % 4) for i in range(4)]) for d in (2, 1, 3)}
     whiten, half = vmem_call(solve_kernel, [square] * 2, "solve", 1)(moment)
-    (parts,) = vmem_call(
-        scores_kernel, [jax.ShapeDtypeStruct((8, FINAL, WIDTH), F32)], "scores", 9, smem_in=2,
+    mine, theirs = vmem_call(
+        scores_kernel, [jax.ShapeDtypeStruct((4, FINAL, WIDTH), F32)] * 2, "scores", 9, smem_in=2,
         scratch=[pltpu.VMEM((4, ROUTED, WIDTH), F32), pltpu.VMEM((64, WIDTH), F32)],
     )(source, rank, e[0], w[2], w[1], w[3], whiten, half, scale)
-    parts = lax.all_to_all(parts, ("x", "k"), split_axis=0, concat_axis=0, tiled=True)
+    got = lax.ppermute(theirs, "k", other)
+    p = vmem_call(pair_kernel, [jax.ShapeDtypeStruct((2, FINAL, WIDTH), F32)] * 4, "pair", 2)(
+        mine, got)
+    p = [p[0]] + [lax.ppermute(p[d], "x", [(i, (i + d) % 4) for i in range(4)]) for d in (2, 1, 3)]
     tiles, rho, trace = vmem_call(
         finish_kernel,
         [jax.ShapeDtypeStruct((2, WIDTH, WIDTH), F32), jax.ShapeDtypeStruct((8, 8), F32),
-         jax.ShapeDtypeStruct((1, 8), F32)], "finish", 3, smem_in=1,
-    )(local_gene, parts, weights)
+         jax.ShapeDtypeStruct((1, 8), F32)], "finish", 6,
+        scratch=[pltpu.VMEM((8, FINAL, WIDTH), F32)],
+    )(genes, *p, weights)
     return tiles[None], rho, trace.reshape(8)
 
 

time: 62.4 us -> 57.3 us (0.918)
  blocking collectives: 12.3 us -> 0 us
  starting transfers between devices: 19.2 us -> 30.4 us
  Pallas kernels: 24.7 us -> 14.6 us
  waiting for transfers between devices: 5.33 us -> 11 us
    ppermute x1 -> x9, starting transfers between devices: 1.59 us -> 16.4 us  [the longest x3 6.56 us: shards(): rc = {d: lax.ppermute(ac[d], AXES, turns(d, True)) for d in (2, 1, 3)}]
    all_to_all x1 -> x0, blocking collectives: 12.3 us -> none  [shards(): lax.all_to_all(parts, ('x', 'k'), split_axis=0, concat_axis=0, tiled=True)]
    pallas_call x5 -> x8, Pallas kernels: 19.5 us -> 10.7 us  [the longest x1 6.18 us: products(): pl.pallas_call(products_kernel, out_shape=tuple((jax.ShapeDtypeStruct(sha...]
    ppermute x1 -> x9, waiting for transfers between devices: 3.22 us -> 8.87 us  [the longest x3 3.51 us: shards(): rc = {d: lax.ppermute(ac[d], AXES, turns(d, True)) for d in (2, 1, 3)}]
    ppermute x3, starting transfers between devices: 6.43 us -> 3.21 us  [shards(): r = {d: lax.ppermute(a[d], AXES, turns(d, True)) for d in (2, 1, 3)}]
    pallas_call x1, Pallas kernels: 2.82 us -> 2.11 us  [shards(): whiten, half = vmem_call(solve_kernel, [square] * 2, 'solve', 1)(moment)]
  transfers between devices with their start and end apart: 10 -> 18, of which waited for: 2 -> 6; matrix products, arithmetic and copies ran while one was open for 0% -> 0% of each run, Pallas kernels for 19% -> 9%
where the time goes in v3:
time: 57.3 us; the launch traced here: 56.8 us
  starting transfers between devices  30.4 us (53%)
  Pallas kernels  14.6 us (25%)
  waiting for transfers between devices  11 us (19%)
  between operations  0.75 us (1%)
    ppermute x3, starting transfers between devices, shards(): rc = {d: lax.ppermute(ac[d], AXES, turns(d, True)) for d in (2, 1, 3)}  6.56 us
    pallas_call x1, Pallas kernels, products(): pl.pallas_call(products_kernel, out_shape=tuple((jax.ShapeDtypeStruct(sha...  6.18 us
    ppermute x3, starting transfers between devices, shards(): lax.ppermute(e[d], 'g', [(i, (i + d) % 4) for i in range(4)])  5.67 us
    ppermute x3, starting transfers between devices, shards(): q = {d: lax.ppermute(b[d], AXES, turns(d, False)) for d in (2, 1, 3)}  5.2 us
    ppermute x1, starting transfers between devices, shards(): got = lax.ppermute(theirs, 'k', other)  4.17 us
    ppermute x3, starting transfers between devices, shards(): lax.ppermute(p[d], 'x', [(i, (i + d) % 4) for i in range(4)])  4.04 us
    ppermute x3, waiting for transfers between devices, shards(): rc = {d: lax.ppermute(ac[d], AXES, turns(d, True)) for d in (2, 1, 3)}  3.51 us
    ppermute x3, starting transfers between devices, shards(): r = {d: lax.ppermute(a[d], AXES, turns(d, True)) for d in (2, 1, 3)}  3.21 us
  transfers between devices with their start and end apart: 18, of which 6 were waited for; matrix products, arithmetic and copies ran while one was open for 0% of the time, Pallas kernels for 9%

profile of v3, /device:TPU:1, one launch (start us, length us, event | category | flops | bytes accessed | tf_op | source)
XLA Modules:
  0.0 56.8 jit_solution(18440207076648029859)
XLA Ops:
  0.7 6.2 %products.1 = (f32[4,4,128,128]{3,2,1,0:T(8,128)S(1)}, f32[4,4,128,128]{3,2,1,0:T(8,128)S(1)}, f32[4,512,128]{2,1,0:T(8,128)S(1)}, f32[4,128,128]{2,1,0:T(8,128)S(1)}, f32[16,128]{1,0:T(8,128)S(1)}) custom-call(s32[256]{0:T(256)} %owner_ref.1, bf16[512,8192]{1,0:T(8,128)(2,1)} %dosage_ref.1, bf16[32,512]{1,0:T(8,128)(2,1)} %bitcast.9, ...), custom_call_target="tpu_custom_call" | custom-call | tf_op jit(solution)/shard_map/products/pallas_call | solution.py:135
  6.8 1.5 %collective-permute-start.1 = (f32[4,4,128,128]{3,2,1,0:T(8,128)S(1)}, f32[4,4,128,128]{3,2,1,0:T(8,128)S(1)}, u32[]{:S(2)}, u32[]{:S(2)}) collective-permute-start(f32[4,4,128,128]{3,2,1,0:T(8,128)S(1)} %get-tuple-element.57), channel_id=1, source_target_pairs={{0,16},{16,0},{1,17},{17,1},{2,18},{18,2},{3,19},{19,3},{4,20},{20... | collective-permute-start | bytes 3145736 | tf_op jit(solution)/shard_map/ppermute | solution.py:396
  8.4 0.7 %cross.1 = (f32[4,4,80,128]{3,2,1,0:T(8,128)S(1)}, f32[4,4,80,128]{3,2,1,0:T(8,128)S(1)}) custom-call(f32[4,512,128]{2,1,0:T(8,128)S(1)} %get-tuple-element.45.cross_ref, f32[4,128,128]{2,1,0:T(8,128)S(1)} %get-tuple-element.46.rest_ref, f32[16,128]{1,0:T(8,128)S(1)} %get-tuple-element.47.moment_ref), custom_call_target="tpu_custom_call" | custom-call | tf_op jit(solution)/shard_map/cross/pallas_call | solution.py:397
  9.1 0.1 collective-permute-start
  9.2 2.4 %collective-permute-done.recv_ref = f32[4,4,80,128]{3,2,1,0:T(8,128)S(1)} collective-permute-done((f32[4,4,80,128]{3,2,1,0:T(8,128)S(1)}, f32[4,4,80,128]{3,2,1,0:T(8,128)S(1)}, u32[]{:S(2)}, u32[]{:S(2)}) %collective-permute-start) | collective-permute-done | bytes 655392 | tf_op jit(solution)/shard_map/ppermute | solution.py:400
  11.6 3.8 %collective-permute-start.5 = (f32[4,80,128]{2,1,0:T(8,128)S(1)}, f32[4,80,128]{2,1,0:T(8,128)S(1)}, u32[]{:S(2)}, u32[]{:S(2)}) collective-permute-start(f32[4,80,128]{2,1,0:T(8,128)S(1)} %get-tuple-element.62), channel_id=1, source_target_pairs={{0,64},{1,65},{2,66},{3,67},{4,68},{5,69},{6,70},{7,71},{8,72},{9,... | collective-permute-start | bytes 491528 | tf_op jit(solution)/shard_map/ppermute | solution.py:406
  15.4 0.1 first_sum.1
  15.5 0.1 collective-permute-start.2
  15.6 1.0 %collective-permute-start.3 = (f32[4,128,128]{2,1,0:T(8,128)S(1)}, f32[4,128,128]{2,1,0:T(8,128)S(1)}, u32[]{:S(2)}, u32[]{:S(2)}) collective-permute-start(f32[4,128,128]{2,1,0:T(8,128)S(1)} %get-tuple-element.60), channel_id=1, source_target_pairs={{0,32},{1,33},{2,34},{3,35},{4,36},{5,37},{6,38},{7,39},{8,40},{9,... | collective-permute-start | bytes 786440 | tf_op jit(solution)/shard_map/ppermute | solution.py:403
  16.6 2.1 %collective-permute-start.4 = (f32[4,128,128]{2,1,0:T(8,128)S(1)}, f32[4,128,128]{2,1,0:T(8,128)S(1)}, u32[]{:S(2)}, u32[]{:S(2)}) collective-permute-start(f32[4,128,128]{2,1,0:T(8,128)S(1)} %get-tuple-element.61), channel_id=1, source_target_pairs={{0,96},{1,97},{2,98},{3,99},{4,100},{5,101},{6,102},{7,103},{8,104... | collective-permute-start | bytes 786440 | tf_op jit(solution)/shard_map/ppermute | solution.py:403
  18.7 2.8 %collective-permute-start.7 = (f32[4,80,128]{2,1,0:T(8,128)S(1)}, f32[4,80,128]{2,1,0:T(8,128)S(1)}, u32[]{:S(2)}, u32[]{:S(2)}) collective-permute-start(f32[4,80,128]{2,1,0:T(8,128)S(1)} %get-tuple-element.64), channel_id=1, source_target_pairs={{0,96},{1,97},{2,98},{3,99},{4,100},{5,101},{6,102},{7,103},{8,104... | collective-permute-start | bytes 491528 | tf_op jit(solution)/shard_map/ppermute | solution.py:406
  21.5 2.1 %layout.1 = (s32[16]{0:T(128)S(1)}, s32[16]{0:T(128)S(1)}, s32[16]{0:T(128)S(1)}, s32[16]{0:T(128)S(1)}, s32[16,128]{1,0:T(8,128)S(1)}, /*index=5*/f32[16,128]{1,0:T(8,128)S(1)}, f32[16,128]{1,0:T(8,128)S(1)}) custom-call(s32[256]{0:T(256)S(1)} %copy-done.2, f32[256,128]{1,0:T(8,128)S(1)} %bitcast.7, s32[256,128]{1,0:T(8,128)S(1)} %bitcast.8, ...), custom_call_target="tpu_custom_call" | custom-call | tf_op jit(solution)/shard_map/layout/pallas_call | solution.py:410
  23.7 3.5 %collective-permute-done.6.c1 = f32[4,80,128]{2,1,0:T(8,128)S(1)} collective-permute-done((f32[4,80,128]{2,1,0:T(8,128)S(1)}, f32[4,80,128]{2,1,0:T(8,128)S(1)}, u32[]{:S(2)}, u32[]{:S(2)}) %collective-permute-start.6) | collective-permute-done | bytes 163872 | tf_op jit(solution)/shard_map/ppermute | solution.py:406
  27.2 0.1 second_sum.1
  27.3 2.5 %collective-permute-start.8 = (f32[208,128]{1,0:T(8,128)S(1)}, f32[208,128]{1,0:T(8,128)S(1)}, u32[]{:S(2)}, u32[]{:S(2)}) collective-permute-start(f32[208,128]{1,0:T(8,128)S(1)} %get-tuple-element.67), channel_id=1, source_target_pairs={{0,2},{1,3},{2,0},{3,1},{4,6},{5,7},{6,4},{7,5},{8,10},{9,11},{10,... | collective-permute-start | bytes 319496 | tf_op jit(solution)/shard_map/ppermute | solution.py:419
  29.9 0.3 collective-permute-start.9
  30.2 2.4 %collective-permute-start.10 = (f32[208,128]{1,0:T(8,128)S(1)}, f32[208,128]{1,0:T(8,128)S(1)}, u32[]{:S(2)}, u32[]{:S(2)}) collective-permute-start(f32[208,128]{1,0:T(8,128)S(1)} %get-tuple-element.69), channel_id=1, source_target_pairs={{0,3},{1,0},{2,1},{3,2},{4,7},{5,4},{6,5},{7,6},{8,11},{9,8},{10,9... | collective-permute-start | bytes 319496 | tf_op jit(solution)/shard_map/ppermute | solution.py:419
  32.5 2.1 %collective-permute-done.9.q1 = f32[208,128]{1,0:T(8,128)S(1)} collective-permute-done((f32[208,128]{1,0:T(8,128)S(1)}, f32[208,128]{1,0:T(8,128)S(1)}, u32[]{:S(2)}, u32[]{:S(2)}) %collective-permute-start.9) | collective-permute-done | bytes 106528 | tf_op jit(solution)/shard_map/ppermute | solution.py:419
  34.6 0.7 %route.1 = (f32[112,128]{1,0:T(8,128)S(1)}, f32[112,128]{1,0:T(8,128)S(1)}, f32[112,128]{1,0:T(8,128)S(1)}, f32[112,128]{1,0:T(8,128)S(1)}, f32[16,128]{1,0:T(8,128)S(1)}) custom-call(s32[16]{0:T(128)S(1)} %get-tuple-element.54.turn_ref, s32[16]{0:T(128)S(1)} %get-tuple-element.55.slot_at_ref, f32[208,128]{1,0:T(8,128)S(1)} %get-tuple-element.66.b0, ...), custom_call_target="tpu_custom_call" | custom-call | tf_op jit(solution)/shard_map/route/pallas_call | solution.py:421
  35.4 3.0 %collective-permute-start.11 = (f32[112,128]{1,0:T(8,128)S(1)}, f32[112,128]{1,0:T(8,128)S(1)}, u32[]{:S(2)}, u32[]{:S(2)}) collective-permute-start(f32[112,128]{1,0:T(8,128)S(1)} %get-tuple-element.71), channel_id=1, source_target_pairs={{0,8},{4,12},{8,0},{12,4},{1,9},{5,13},{9,1},{13,5},{2,10},{6,14},... | collective-permute-start | bytes 172040 | tf_op jit(solution)/shard_map/ppermute | solution.py:425
  38.4 0.4 collective-permute-start.12
  38.8 2.3 %collective-permute-start.13 = (f32[112,128]{1,0:T(8,128)S(1)}, f32[112,128]{1,0:T(8,128)S(1)}, u32[]{:S(2)}, u32[]{:S(2)}) collective-permute-start(f32[112,128]{1,0:T(8,128)S(1)} %get-tuple-element.73), channel_id=1, source_target_pairs={{0,12},{4,0},{8,4},{12,8},{1,13},{5,1},{9,5},{13,9},{2,14},{6,2},{... | collective-permute-start | bytes 172040 | tf_op jit(solution)/shard_map/ppermute | solution.py:425
  41.1 2.1 %solve.1 = (f32[128,128]{1,0:T(8,128)S(1)}, f32[128,128]{1,0:T(8,128)S(1)}) custom-call(f32[16,128]{1,0:T(8,128)S(1)} %get-tuple-element.74.moment_ref), custom_call_target="tpu_custom_call" | custom-call | tf_op jit(solution)/shard_map/solve/pallas_call | solution.py:426
  43.2 1.3 %scores.1 = (f32[4,48,128]{2,1,0:T(8,128)S(1)}, f32[4,48,128]{2,1,0:T(8,128)S(1)}) custom-call(s32[16]{0:T(128)S(1)} %get-tuple-element.52.source_ref, s32[16]{0:T(128)S(1)} %get-tuple-element.53.rank_ref, f32[112,128]{1,0:T(8,128)S(1)} %get-tuple-element.70.w0, f32[112,128]{1,0:T(8,128)S(1)} %collective-permute-done.11.w2, ...), custom_call_target="tpu_custom_call" | custom-call | tf_op jit(solution)/shard_map/scores/pallas_call | solution.py:427
  44.5 4.2 %collective-permute-start.14 = (f32[4,48,128]{2,1,0:T(8,128)S(1)}, f32[4,48,128]{2,1,0:T(8,128)S(1)}, u32[]{:S(2)}, u32[]{:S(2)}) collective-permute-start(f32[4,48,128]{2,1,0:T(8,128)S(1)} %get-tuple-element.79), channel_id=1, source_target_pairs={{0,16},{16,0},{1,17},{17,1},{2,18},{18,2},{3,19},{19,3},{4,20},{20... | collective-permute-start | bytes 294920 | tf_op jit(solution)/shard_map/ppermute | solution.py:431
  48.7 0.9 %collective-permute-done.14.got_ref = f32[4,48,128]{2,1,0:T(8,128)S(1)} collective-permute-done((f32[4,48,128]{2,1,0:T(8,128)S(1)}, f32[4,48,128]{2,1,0:T(8,128)S(1)}, u32[]{:S(2)}, u32[]{:S(2)}) %collective-permute-start.14) | collective-permute-done | bytes 98336 | tf_op jit(solution)/shard_map/ppermute | solution.py:431
  49.7 1.4 %collective-permute-start.15 = (f32[2,48,128]{2,1,0:T(8,128)S(1)}, f32[2,48,128]{2,1,0:T(8,128)S(1)}, u32[]{:S(2)}, u32[]{:S(2)}) collective-permute-start(f32[2,48,128]{2,1,0:T(8,128)S(1)} %get-tuple-element.81), channel_id=1, source_target_pairs={{0,64},{32,96},{64,0},{96,32},{1,65},{33,97},{65,1},{97,33},{2,66}... | collective-permute-start | bytes 147464 | tf_op jit(solution)/shard_map/ppermute | solution.py:434
  51.0 0.3 collective-permute-start.16
  51.3 2.4 %collective-permute-start.17 = (f32[2,48,128]{2,1,0:T(8,128)S(1)}, f32[2,48,128]{2,1,0:T(8,128)S(1)}, u32[]{:S(2)}, u32[]{:S(2)}) collective-permute-start(f32[2,48,128]{2,1,0:T(8,128)S(1)} %get-tuple-element.83), channel_id=1, source_target_pairs={{0,96},{32,0},{64,32},{96,64},{1,97},{33,1},{65,33},{97,65},{2,98}... | collective-permute-start | bytes 147464 | tf_op jit(solution)/shard_map/ppermute | solution.py:434
  53.7 0.5 collective-permute-done.15.p2
  54.2 1.6 %collective-permute-done.16.p1 = f32[2,48,128]{2,1,0:T(8,128)S(1)} collective-permute-done((f32[2,48,128]{2,1,0:T(8,128)S(1)}, f32[2,48,128]{2,1,0:T(8,128)S(1)}, u32[]{:S(2)}, u32[]{:S(2)}) %collective-permute-start.16) | collective-permute-done | bytes 49184 | tf_op jit(solution)/shard_map/ppermute | solution.py:434
  55.7 1.1 %finish.1 = (f32[2,128,128]{2,1,0:T(8,128)}, f32[8,8]{1,0:T(8,128)}, f32[1,8]{1,0:T(1,128)}) custom-call(s32[16,128]{1,0:T(8,128)S(1)} %get-tuple-element.51.genes_ref, f32[2,48,128]{2,1,0:T(8,128)S(1)} %get-tuple-element.80.p0, f32[2,48,128]{2,1,0:T(8,128)S(1)} %collective-permute-done.15.p2, f32[2,48,128]{2,1,0:T(8,128)S(1)} %collective-permute-done.16.p1, ...), custom_call_target="tpu_custom_call" | custom-call | tf_op jit(solution)/shard_map/finish/pallas_call | solution.py:435
  (21 shorter events, 0.1 us)
Async XLA Ops:
  0.6 20.9 %copy-start.2 = (s32[256]{0:T(256)S(1)}, s32[256]{0:T(256)}, u32[]{:S(2)}) copy-start(s32[256]{0:T(256)} %owner_ref.1) | copy-start | bytes 3076
  0.6 20.9 %copy-start.1 = (s32[32768]{0:T(1024)S(1)}, s32[32768]{0:T(1024)}, u32[]{:S(2)}) copy-start(s32[32768]{0:T(1024)} %param.13) | copy-start | bytes 393220
  0.7 20.9 %copy-start = (f32[32768]{0:T(1024)S(1)}, f32[32768]{0:T(1024)}, u32[]{:S(2)}) copy-start(f32[32768]{0:T(1024)} %param.11) | copy-start | bytes 393220
  6.8 8.6 %collective-permute-start.1 = (f32[4,4,128,128]{3,2,1,0:T(8,128)S(1)}, f32[4,4,128,128]{3,2,1,0:T(8,128)S(1)}, u32[]{:S(2)}, u32[]{:S(2)}) collective-permute-start(f32[4,4,128,128]{3,2,1,0:T(8,128)S(1)} %get-tuple-element.57), channel_id=1, source_target_pairs={{0,16},{16,0},{1,17},{17,1},{2,18},{18,2},{3,19},{19,3},{4,20},{20... | collective-permute-start | bytes 3145736 | tf_op jit(solution)/shard_map/ppermute | solution.py:396
  9.1 2.5 %collective-permute-start = (f32[4,4,80,128]{3,2,1,0:T(8,128)S(1)}, f32[4,4,80,128]{3,2,1,0:T(8,128)S(1)}, u32[]{:S(2)}, u32[]{:S(2)}) collective-permute-start(f32[4,4,80,128]{3,2,1,0:T(8,128)S(1)} %get-tuple-element.49), channel_id=1, source_target_pairs={{0,16},{16,0},{1,17},{17,1},{2,18},{18,2},{3,19},{19,3},{4,20},{20... | collective-permute-start | bytes 1966088 | tf_op jit(solution)/shard_map/ppermute | solution.py:400
  11.6 7.1 %collective-permute-start.5 = (f32[4,80,128]{2,1,0:T(8,128)S(1)}, f32[4,80,128]{2,1,0:T(8,128)S(1)}, u32[]{:S(2)}, u32[]{:S(2)}) collective-permute-start(f32[4,80,128]{2,1,0:T(8,128)S(1)} %get-tuple-element.62), channel_id=1, source_target_pairs={{0,64},{1,65},{2,66},{3,67},{4,68},{5,69},{6,70},{7,71},{8,72},{9,... | collective-permute-start | bytes 491528 | tf_op jit(solution)/shard_map/ppermute | solution.py:406
  15.5 11.7 %collective-permute-start.2 = (f32[4,128,128]{2,1,0:T(8,128)S(1)}, f32[4,128,128]{2,1,0:T(8,128)S(1)}, u32[]{:S(2)}, u32[]{:S(2)}) collective-permute-start(f32[4,128,128]{2,1,0:T(8,128)S(1)} %get-tuple-element.59), channel_id=1, source_target_pairs={{0,64},{1,65},{2,66},{3,67},{4,68},{5,69},{6,70},{7,71},{8,72},{9,... | collective-permute-start | bytes 786440 | tf_op jit(solution)/shard_map/ppermute | solution.py:403
  15.6 11.6 %collective-permute-start.3 = (f32[4,128,128]{2,1,0:T(8,128)S(1)}, f32[4,128,128]{2,1,0:T(8,128)S(1)}, u32[]{:S(2)}, u32[]{:S(2)}) collective-permute-start(f32[4,128,128]{2,1,0:T(8,128)S(1)} %get-tuple-element.60), channel_id=1, source_target_pairs={{0,32},{1,33},{2,34},{3,35},{4,36},{5,37},{6,38},{7,39},{8,40},{9,... | collective-permute-start | bytes 786440 | tf_op jit(solution)/shard_map/ppermute | solution.py:403
  16.6 10.6 %collective-permute-start.4 = (f32[4,128,128]{2,1,0:T(8,128)S(1)}, f32[4,128,128]{2,1,0:T(8,128)S(1)}, u32[]{:S(2)}, u32[]{:S(2)}) collective-permute-start(f32[4,128,128]{2,1,0:T(8,128)S(1)} %get-tuple-element.61), channel_id=1, source_target_pairs={{0,96},{1,97},{2,98},{3,99},{4,100},{5,101},{6,102},{7,103},{8,104... | collective-permute-start | bytes 786440 | tf_op jit(solution)/shard_map/ppermute | solution.py:403
  18.7 8.5 %collective-permute-start.6 = (f32[4,80,128]{2,1,0:T(8,128)S(1)}, f32[4,80,128]{2,1,0:T(8,128)S(1)}, u32[]{:S(2)}, u32[]{:S(2)}) collective-permute-start(f32[4,80,128]{2,1,0:T(8,128)S(1)} %get-tuple-element.63), channel_id=1, source_target_pairs={{0,32},{1,33},{2,34},{3,35},{4,36},{5,37},{6,38},{7,39},{8,40},{9,... | collective-permute-start | bytes 491528 | tf_op jit(solution)/shard_map/ppermute | solution.py:406
  18.7 8.5 %collective-permute-start.7 = (f32[4,80,128]{2,1,0:T(8,128)S(1)}, f32[4,80,128]{2,1,0:T(8,128)S(1)}, u32[]{:S(2)}, u32[]{:S(2)}) collective-permute-start(f32[4,80,128]{2,1,0:T(8,128)S(1)} %get-tuple-element.64), channel_id=1, source_target_pairs={{0,96},{1,97},{2,98},{3,99},{4,100},{5,101},{6,102},{7,103},{8,104... | collective-permute-start | bytes 491528 | tf_op jit(solution)/shard_map/ppermute | solution.py:406
  27.3 5.2 %collective-permute-start.8 = (f32[208,128]{1,0:T(8,128)S(1)}, f32[208,128]{1,0:T(8,128)S(1)}, u32[]{:S(2)}, u32[]{:S(2)}) collective-permute-start(f32[208,128]{1,0:T(8,128)S(1)} %get-tuple-element.67), channel_id=1, source_target_pairs={{0,2},{1,3},{2,0},{3,1},{4,6},{5,7},{6,4},{7,5},{8,10},{9,11},{10,... | collective-permute-start | bytes 319496 | tf_op jit(solution)/shard_map/ppermute | solution.py:419
  29.9 4.8 %collective-permute-start.9 = (f32[208,128]{1,0:T(8,128)S(1)}, f32[208,128]{1,0:T(8,128)S(1)}, u32[]{:S(2)}, u32[]{:S(2)}) collective-permute-start(f32[208,128]{1,0:T(8,128)S(1)} %get-tuple-element.68), channel_id=1, source_target_pairs={{0,1},{1,2},{2,3},{3,0},{4,5},{5,6},{6,7},{7,4},{8,9},{9,10},{10,1... | collective-permute-start | bytes 319496 | tf_op jit(solution)/shard_map/ppermute | solution.py:419
  30.2 4.5 %collective-permute-start.10 = (f32[208,128]{1,0:T(8,128)S(1)}, f32[208,128]{1,0:T(8,128)S(1)}, u32[]{:S(2)}, u32[]{:S(2)}) collective-permute-start(f32[208,128]{1,0:T(8,128)S(1)} %get-tuple-element.69), channel_id=1, source_target_pairs={{0,3},{1,0},{2,1},{3,2},{4,7},{5,4},{6,5},{7,6},{8,11},{9,8},{10,9... | collective-permute-start | bytes 319496 | tf_op jit(solution)/shard_map/ppermute | solution.py:419
  35.4 7.8 %collective-permute-start.11 = (f32[112,128]{1,0:T(8,128)S(1)}, f32[112,128]{1,0:T(8,128)S(1)}, u32[]{:S(2)}, u32[]{:S(2)}) collective-permute-start(f32[112,128]{1,0:T(8,128)S(1)} %get-tuple-element.71), channel_id=1, source_target_pairs={{0,8},{4,12},{8,0},{12,4},{1,9},{5,13},{9,1},{13,5},{2,10},{6,14},... | collective-permute-start | bytes 172040 | tf_op jit(solution)/shard_map/ppermute | solution.py:425
  38.4 4.8 %collective-permute-start.12 = (f32[112,128]{1,0:T(8,128)S(1)}, f32[112,128]{1,0:T(8,128)S(1)}, u32[]{:S(2)}, u32[]{:S(2)}) collective-permute-start(f32[112,128]{1,0:T(8,128)S(1)} %get-tuple-element.72), channel_id=1, source_target_pairs={{0,4},{4,8},{8,12},{12,0},{1,5},{5,9},{9,13},{13,1},{2,6},{6,10},{... | collective-permute-start | bytes 172040 | tf_op jit(solution)/shard_map/ppermute | solution.py:425
  38.8 4.4 %collective-permute-start.13 = (f32[112,128]{1,0:T(8,128)S(1)}, f32[112,128]{1,0:T(8,128)S(1)}, u32[]{:S(2)}, u32[]{:S(2)}) collective-permute-start(f32[112,128]{1,0:T(8,128)S(1)} %get-tuple-element.73), channel_id=1, source_target_pairs={{0,12},{4,0},{8,4},{12,8},{1,13},{5,1},{9,5},{13,9},{2,14},{6,2},{... | collective-permute-start | bytes 172040 | tf_op jit(solution)/shard_map/ppermute | solution.py:425
  44.5 5.1 %collective-permute-start.14 = (f32[4,48,128]{2,1,0:T(8,128)S(1)}, f32[4,48,128]{2,1,0:T(8,128)S(1)}, u32[]{:S(2)}, u32[]{:S(2)}) collective-permute-start(f32[4,48,128]{2,1,0:T(8,128)S(1)} %get-tuple-element.79), channel_id=1, source_target_pairs={{0,16},{16,0},{1,17},{17,1},{2,18},{18,2},{3,19},{19,3},{4,20},{20... | collective-permute-start | bytes 294920 | tf_op jit(solution)/shard_map/ppermute | solution.py:431
  49.7 4.5 %collective-permute-start.15 = (f32[2,48,128]{2,1,0:T(8,128)S(1)}, f32[2,48,128]{2,1,0:T(8,128)S(1)}, u32[]{:S(2)}, u32[]{:S(2)}) collective-permute-start(f32[2,48,128]{2,1,0:T(8,128)S(1)} %get-tuple-element.81), channel_id=1, source_target_pairs={{0,64},{32,96},{64,0},{96,32},{1,65},{33,97},{65,1},{97,33},{2,66}... | collective-permute-start | bytes 147464 | tf_op jit(solution)/shard_map/ppermute | solution.py:434
  51.0 4.7 %collective-permute-start.16 = (f32[2,48,128]{2,1,0:T(8,128)S(1)}, f32[2,48,128]{2,1,0:T(8,128)S(1)}, u32[]{:S(2)}, u32[]{:S(2)}) collective-permute-start(f32[2,48,128]{2,1,0:T(8,128)S(1)} %get-tuple-element.82), channel_id=1, source_target_pairs={{0,32},{32,64},{64,96},{96,0},{1,33},{33,65},{65,97},{97,1},{2,34}... | collective-permute-start | bytes 147464 | tf_op jit(solution)/shard_map/ppermute | solution.py:434
  51.3 4.4 %collective-permute-start.17 = (f32[2,48,128]{2,1,0:T(8,128)S(1)}, f32[2,48,128]{2,1,0:T(8,128)S(1)}, u32[]{:S(2)}, u32[]{:S(2)}) collective-permute-start(f32[2,48,128]{2,1,0:T(8,128)S(1)} %get-tuple-element.83), channel_id=1, source_target_pairs={{0,96},{32,0},{64,32},{96,64},{1,97},{33,1},{65,33},{97,65},{2,98}... | collective-permute-start | bytes 147464 | tf_op jit(solution)/shard_map/ppermute | solution.py:434

commit v4 on v3

--- a/solution.py
+++ b/solution.py
@@ -13,6 +13,7 @@
 LOCAL = 64
 STEP = 16
 LOAD = 16
+AHEAD = 2
 GRAM = 128
 CROSS = 80
 CHUNK = GRAM + CROSS
@@ -52,7 +53,7 @@
                                         (mask_hbm, mask_ref), (owner_hbm, owner_ref)])]
     for copy in small:
         copy.start()
-    for i in range(LOCAL // LOAD):
+    for i in range(AHEAD):
         fetch(i).start()
 
     rest_ref[...] = jnp.zeros_like(rest_ref)
@@ -80,6 +81,11 @@
             load = step * (STEP // LOAD) + pair * 2 // LOAD
             if pair * 2 % LOAD == 0:
                 fetch(load).wait()
+
+                @pl.when(load + AHEAD < LOCAL // LOAD)
+                def _():
+                    fetch(load + AHEAD).start()
+
             lo = pair * 256 % (LOAD * WIDTH)
             panel = panel_ref[load, :, lo:lo + 256]
             left = jnp.concatenate([panel.T * keep_row, left_ref[...]], 0)
@@ -155,18 +161,24 @@
         for a in (owner, dosage, cov, pheno, mask)])
 
 
-def first_sum_kernel(keep_ref, recv_ref, *outs):
-    for d in range(4):
-        outs[d][...] = keep_ref[d] + recv_ref[d]
-
-
-def second_sum_kernel(a0, a2, a1, a3, c0, c2, c1, c3, _, *outs):
+def far_sum_kernel(keep_ref, recv_ref, out):
+    out[...] = keep_ref[2] + recv_ref[2]
+
+
+def near_sum_kernel(keep_ref, recv_ref, keep_cross_ref, recv_cross_ref, _, a0, a1, a3, c2):
+    for d, out in ((0, a0), (1, a1), (3, a3)):
+        out[:, :GRAM, :] = keep_ref[d] + recv_ref[d]
+        out[:, GRAM:, :] = keep_cross_ref[d] + recv_cross_ref[d]
+    c2[...] = keep_cross_ref[2] + recv_cross_ref[2]
+
+
+def second_sum_kernel(a0, a2, c2, a1, a3, _, *outs):
     x, k, g, c = (lax.axis_index(a) for a in AXES)
     base = jnp.where(k == 0, c, x)
     for d in range(4):
         j = (base + d) & 3
-        outs[d][:GRAM] = (a0[j] + a1[j]) + (a2[j] + a3[j])
-        outs[d][GRAM:] = (c0[j] + c1[j]) + (c2[j] + c3[j])
+        outs[d][:GRAM] = (a0[j, :GRAM] + a1[j, :GRAM]) + (a2[j] + a3[j, :GRAM])
+        outs[d][GRAM:] = (a0[j, GRAM:] + a1[j, GRAM:]) + (c2[j] + a3[j, GRAM:])
 
 
 def vmem_call(kernel, shapes, name, n_in, scratch=(), smem_in=0, smem_out=(), any_in=0):
@@ -285,7 +297,7 @@
     half_ref[...] = jnp.where(lane == (row >> 5), half, 0.0)
 
 
-def scores_kernel(source_ref, rank_ref, w0, w2, w1, w3, whiten_ref, half_ref, scale_ref,
+def scores_kernel(source_ref, rank_ref, w0, w3, w2, w1, whiten_ref, half_ref, scale_ref,
                   mine_ref, other_ref, slot_ref, cross_ref):
     x, k = lax.axis_index("x"), lax.axis_index("k")
     for d, ref in enumerate((w0, w1, w2, w3)):
@@ -398,12 +410,16 @@
         cross_kernel, [jax.ShapeDtypeStruct((4, 4, CROSS, WIDTH), F32)] * 2, "cross", 3,
         scratch=[pltpu.VMEM((20, WIDTH, WIDTH), F32)])(*raw)
     recv_cross = lax.ppermute(send_cross, "k", other)
-    first = [jax.ShapeDtypeStruct((4, GRAM, WIDTH), F32)] * 4
-    a = vmem_call(first_sum_kernel, first, "first_sum", 2)(keep, recv)
-    r = {d: lax.ppermute(a[d], AXES, turns(d, True)) for d in (2, 1, 3)}
-    first = [jax.ShapeDtypeStruct((4, CROSS, WIDTH), F32)] * 4
-    ac = vmem_call(first_sum_kernel, first, "cross_sum", 2)(keep_cross, recv_cross)
-    rc = {d: lax.ppermute(ac[d], AXES, turns(d, True)) for d in (2, 1, 3)}
+    gram = jax.ShapeDtypeStruct((4, GRAM, WIDTH), F32)
+    (far,) = vmem_call(far_sum_kernel, [gram], "far_sum", 2)(keep, recv)
+    a2 = lax.ppermute(far, AXES, turns(2, True))
+    chunk = jax.ShapeDtypeStruct((4, CHUNK, WIDTH), F32)
+    rest = jax.ShapeDtypeStruct((4, CROSS, WIDTH), F32)
+    a0, a1, a3, far_cross = vmem_call(near_sum_kernel, [chunk] * 3 + [rest], "near_sum", 5, any_in=1)(
+        keep, recv, keep_cross, recv_cross, far)
+    a1 = lax.ppermute(a1, AXES, turns(1, True))
+    a3 = lax.ppermute(a3, AXES, turns(3, True))
+    c2 = lax.ppermute(far_cross, AXES, turns(2, True))
     list16 = jax.ShapeDtypeStruct((16,), jnp.int32)
     square = jax.ShapeDtypeStruct((WIDTH, WIDTH), F32)
     tile16 = jax.ShapeDtypeStruct((16, WIDTH), F32)
@@ -412,10 +428,10 @@
         "layout", 4, smem_in=1, smem_out=(0, 1, 2, 3), any_in=1,
         scratch=[pltpu.VMEM((WIDTH, WIDTH), F32), pltpu.VMEM((16, WIDTH), jnp.int32),
                  pltpu.SMEM((17,), jnp.int32), pltpu.SMEM((4,), jnp.int32)],
-    )(bucket_owner, variant_weight.reshape(-1, WIDTH), variant_gene.reshape(-1, WIDTH), ac[0])
+    )(bucket_owner, variant_weight.reshape(-1, WIDTH), variant_gene.reshape(-1, WIDTH), a0)
     part = jax.ShapeDtypeStruct((CHUNK, WIDTH), F32)
-    b = vmem_call(second_sum_kernel, [part] * 4, "second_sum", 9, any_in=1)(
-        a[0], r[2], r[1], r[3], ac[0], rc[2], rc[1], rc[3], weights)
+    b = vmem_call(second_sum_kernel, [part] * 4, "second_sum", 6, any_in=1)(
+        a0, a2, c2, a1, a3, weights)
     q = {d: lax.ppermute(b[d], AXES, turns(d, False)) for d in (2, 1, 3)}
     routed = jax.ShapeDtypeStruct((ROUTED, WIDTH), F32)
     *e, moment = vmem_call(
@@ -427,7 +443,7 @@
     mine, theirs = vmem_call(
         scores_kernel, [jax.ShapeDtypeStruct((4, FINAL, WIDTH), F32)] * 2, "scores", 9, smem_in=2,
         scratch=[pltpu.VMEM((4, ROUTED, WIDTH), F32), pltpu.VMEM((64, WIDTH), F32)],
-    )(source, rank, e[0], w[2], w[1], w[3], whiten, half, scale)
+    )(source, rank, e[0], w[3], w[2], w[1], whiten, half, scale)
     got = lax.ppermute(theirs, "k", other)
     p = vmem_call(pair_kernel, [jax.ShapeDtypeStruct((2, FINAL, WIDTH), F32)] * 4, "pair", 2)(
         mine, got)

time: 57.3 us -> 56.4 us (0.984)
  starting transfers between devices: 30.4 us -> 26.7 us
  waiting for transfers between devices: 11 us -> 14.1 us
    ppermute x6 -> x4, starting transfers between devices: 9.77 us -> 6.97 us  [the longest x1 2.2 us: shards(): a3 = lax.ppermute(a3, AXES, turns(3, True))]
    ppermute x6 -> x4, waiting for transfers between devices: 3.51 us -> 6.06 us  [the longest x1 6.05 us: shards(): c2 = lax.ppermute(far_cross, AXES, turns(2, True))]
    ppermute x1, waiting for transfers between devices: 2.38 us -> 0.91 us  [shards(): recv_cross = lax.ppermute(send_cross, 'k', other)]
    ppermute x1, waiting for transfers between devices: 0.01 us -> 1.44 us  [shards(): recv = lax.ppermute(send, 'k', other)]
    ppermute x1, starting transfers between devices: 4.17 us -> 3.38 us  [shards(): got = lax.ppermute(theirs, 'k', other)]
  transfers between devices with their start and end apart: 18 -> 16, of which waited for: 6 -> 8; matrix products, arithmetic and copies ran while one was open for 0% -> 0% of each run, Pallas kernels for 9% -> 9%
where the time goes in v4:
time: 56.4 us; the launch traced here: 56.1 us
  starting transfers between devices  26.7 us (47%)
  Pallas kernels  14.6 us (26%)
  waiting for transfers between devices  14.1 us (25%)
  between operations  0.73 us (1%)
    pallas_call x1, Pallas kernels, products(): pl.pallas_call(products_kernel, out_shape=tuple((jax.ShapeDtypeStruct(sha...  6.12 us
    ppermute x1, waiting for transfers between devices, shards(): c2 = lax.ppermute(far_cross, AXES, turns(2, True))  6.05 us
    ppermute x3, starting transfers between devices, shards(): lax.ppermute(e[d], 'g', [(i, (i + d) % 4) for i in range(4)])  5.67 us
    ppermute x3, starting transfers between devices, shards(): q = {d: lax.ppermute(b[d], AXES, turns(d, False)) for d in (2, 1, 3)}  5.5 us
    ppermute x3, starting transfers between devices, shards(): lax.ppermute(p[d], 'x', [(i, (i + d) % 4) for i in range(4)])  3.62 us
    ppermute x1, starting transfers between devices, shards(): got = lax.ppermute(theirs, 'k', other)  3.38 us
    ppermute x3, waiting for transfers between devices, shards(): lax.ppermute(p[d], 'x', [(i, (i + d) % 4) for i in range(4)])  2.5 us
    ppermute x1, starting transfers between devices, shards(): a3 = lax.ppermute(a3, AXES, turns(3, True))  2.2 us
  transfers between devices with their start and end apart: 16, of which 8 were waited for; matrix products, arithmetic and copies ran while one was open for 0% of the time, Pallas kernels for 9%

profile of v4, /device:TPU:1, one launch (start us, length us, event | category | flops | bytes accessed | tf_op | source)
XLA Modules:
  0.0 56.1 jit_solution(11827247334972494701)
XLA Ops:
  0.7 6.1 %products.1 = (f32[4,4,128,128]{3,2,1,0:T(8,128)S(1)}, f32[4,4,128,128]{3,2,1,0:T(8,128)S(1)}, f32[4,512,128]{2,1,0:T(8,128)S(1)}, f32[4,128,128]{2,1,0:T(8,128)S(1)}, f32[16,128]{1,0:T(8,128)S(1)}) custom-call(s32[256]{0:T(256)} %owner_ref.1, bf16[512,8192]{1,0:T(8,128)(2,1)} %dosage_ref.1, bf16[32,512]{1,0:T(8,128)(2,1)} %bitcast.9, ...), custom_call_target="tpu_custom_call" | custom-call | tf_op jit(solution)/shard_map/products/pallas_call | solution.py:141
  6.8 1.5 %collective-permute-start = (f32[4,4,128,128]{3,2,1,0:T(8,128)S(1)}, f32[4,4,128,128]{3,2,1,0:T(8,128)S(1)}, u32[]{:S(2)}, u32[]{:S(2)}) collective-permute-start(f32[4,4,128,128]{3,2,1,0:T(8,128)S(1)} %get-tuple-element.42), channel_id=1, source_target_pairs={{0,16},{16,0},{1,17},{17,1},{2,18},{18,2},{3,19},{19,3},{4,20},{20... | collective-permute-start | bytes 3145736 | tf_op jit(solution)/shard_map/ppermute | solution.py:408
  8.3 0.7 %cross.1 = (f32[4,4,80,128]{3,2,1,0:T(8,128)S(1)}, f32[4,4,80,128]{3,2,1,0:T(8,128)S(1)}) custom-call(f32[4,512,128]{2,1,0:T(8,128)S(1)} %get-tuple-element.43.cross_ref, f32[4,128,128]{2,1,0:T(8,128)S(1)} %get-tuple-element.44.rest_ref, f32[16,128]{1,0:T(8,128)S(1)} %get-tuple-element.45.moment_ref), custom_call_target="tpu_custom_call" | custom-call | tf_op jit(solution)/shard_map/cross/pallas_call | solution.py:409
  9.1 1.4 %collective-permute-done.recv_ref = f32[4,4,128,128]{3,2,1,0:T(8,128)S(1)} collective-permute-done((f32[4,4,128,128]{3,2,1,0:T(8,128)S(1)}, f32[4,4,128,128]{3,2,1,0:T(8,128)S(1)}, u32[]{:S(2)}, u32[]{:S(2)}) %collective-permute-start) | collective-permute-done | bytes 1048608 | tf_op jit(solution)/shard_map/ppermute | solution.py:408
  10.6 0.9 %collective-permute-done.1.recv_cross_ref = f32[4,4,80,128]{3,2,1,0:T(8,128)S(1)} collective-permute-done((f32[4,4,80,128]{3,2,1,0:T(8,128)S(1)}, f32[4,4,80,128]{3,2,1,0:T(8,128)S(1)}, u32[]{:S(2)}, u32[]{:S(2)}) %collective-permute-start.1) | collective-permute-done | bytes 655392 | tf_op jit(solution)/shard_map/ppermute | solution.py:412
  11.5 0.2 near_sum.1
  11.7 1.8 %collective-permute-start.4 = (f32[4,208,128]{2,1,0:T(8,128)S(1)}, f32[4,208,128]{2,1,0:T(8,128)S(1)}, u32[]{:S(2)}, u32[]{:S(2)}) collective-permute-start(f32[4,208,128]{2,1,0:T(8,128)S(1)} %get-tuple-element.55), channel_id=1, source_target_pairs={{0,32},{1,33},{2,34},{3,35},{4,36},{5,37},{6,38},{7,39},{8,40},{9,... | collective-permute-start | bytes 1277960 | tf_op jit(solution)/shard_map/ppermute | solution.py:420
  13.5 2.2 %collective-permute-start.5 = (f32[4,208,128]{2,1,0:T(8,128)S(1)}, f32[4,208,128]{2,1,0:T(8,128)S(1)}, u32[]{:S(2)}, u32[]{:S(2)}) collective-permute-start(f32[4,208,128]{2,1,0:T(8,128)S(1)} %get-tuple-element.56), channel_id=1, source_target_pairs={{0,96},{1,97},{2,98},{3,99},{4,100},{5,101},{6,102},{7,103},{8,104... | collective-permute-start | bytes 1277960 | tf_op jit(solution)/shard_map/ppermute | solution.py:421
  15.7 1.2 %collective-permute-start.2 = (f32[4,128,128]{2,1,0:T(8,128)S(1)}, f32[4,128,128]{2,1,0:T(8,128)S(1)}, u32[]{:S(2)}, u32[]{:S(2)}) collective-permute-start(f32[4,128,128]{2,1,0:T(8,128)S(1)} %far_sum.1._), channel_id=1, source_target_pairs={{0,64},{1,65},{2,66},{3,67},{4,68},{5,69},{6,70},{7,71},{8,72},{9,... | collective-permute-start | bytes 786440 | tf_op jit(solution)/shard_map/ppermute | solution.py:415
  16.9 1.7 %collective-permute-start.3 = (f32[4,80,128]{2,1,0:T(8,128)S(1)}, f32[4,80,128]{2,1,0:T(8,128)S(1)}, u32[]{:S(2)}, u32[]{:S(2)}) collective-permute-start(f32[4,80,128]{2,1,0:T(8,128)S(1)} %get-tuple-element.54), channel_id=1, source_target_pairs={{0,64},{1,65},{2,66},{3,67},{4,68},{5,69},{6,70},{7,71},{8,72},{9,... | collective-permute-start | bytes 491528 | tf_op jit(solution)/shard_map/ppermute | solution.py:422
  18.7 2.1 %layout.1 = (s32[16]{0:T(128)S(1)}, s32[16]{0:T(128)S(1)}, s32[16]{0:T(128)S(1)}, s32[16]{0:T(128)S(1)}, s32[16,128]{1,0:T(8,128)S(1)}, /*index=5*/f32[16,128]{1,0:T(8,128)S(1)}, f32[16,128]{1,0:T(8,128)S(1)}) custom-call(s32[256]{0:T(256)S(1)} %copy-done.2, f32[256,128]{1,0:T(8,128)S(1)} %bitcast.7, s32[256,128]{1,0:T(8,128)S(1)} %bitcast.8, ...), custom_call_target="tpu_custom_call" | custom-call | tf_op jit(solution)/shard_map/layout/pallas_call | solution.py:426
  20.8 6.1 %collective-permute-done.3.c2 = f32[4,80,128]{2,1,0:T(8,128)S(1)} collective-permute-done((f32[4,80,128]{2,1,0:T(8,128)S(1)}, f32[4,80,128]{2,1,0:T(8,128)S(1)}, u32[]{:S(2)}, u32[]{:S(2)}) %collective-permute-start.3) | collective-permute-done | bytes 163872 | tf_op jit(solution)/shard_map/ppermute | solution.py:422
  26.9 0.1 second_sum.1
  27.0 2.8 %collective-permute-start.6 = (f32[208,128]{1,0:T(8,128)S(1)}, f32[208,128]{1,0:T(8,128)S(1)}, u32[]{:S(2)}, u32[]{:S(2)}) collective-permute-start(f32[208,128]{1,0:T(8,128)S(1)} %get-tuple-element.59), channel_id=1, source_target_pairs={{0,2},{1,3},{2,0},{3,1},{4,6},{5,7},{6,4},{7,5},{8,10},{9,11},{10,... | collective-permute-start | bytes 319496 | tf_op jit(solution)/shard_map/ppermute | solution.py:435
  29.8 0.3 collective-permute-start.7
  30.1 2.4 %collective-permute-start.8 = (f32[208,128]{1,0:T(8,128)S(1)}, f32[208,128]{1,0:T(8,128)S(1)}, u32[]{:S(2)}, u32[]{:S(2)}) collective-permute-start(f32[208,128]{1,0:T(8,128)S(1)} %get-tuple-element.61), channel_id=1, source_target_pairs={{0,3},{1,0},{2,1},{3,2},{4,7},{5,4},{6,5},{7,6},{8,11},{9,8},{10,9... | collective-permute-start | bytes 319496 | tf_op jit(solution)/shard_map/ppermute | solution.py:435
  32.5 2.1 %collective-permute-done.7.q1 = f32[208,128]{1,0:T(8,128)S(1)} collective-permute-done((f32[208,128]{1,0:T(8,128)S(1)}, f32[208,128]{1,0:T(8,128)S(1)}, u32[]{:S(2)}, u32[]{:S(2)}) %collective-permute-start.7) | collective-permute-done | bytes 106528 | tf_op jit(solution)/shard_map/ppermute | solution.py:435
  34.6 0.7 %route.1 = (f32[112,128]{1,0:T(8,128)S(1)}, f32[112,128]{1,0:T(8,128)S(1)}, f32[112,128]{1,0:T(8,128)S(1)}, f32[112,128]{1,0:T(8,128)S(1)}, f32[16,128]{1,0:T(8,128)S(1)}) custom-call(s32[16]{0:T(128)S(1)} %get-tuple-element.52.turn_ref, s32[16]{0:T(128)S(1)} %get-tuple-element.53.slot_at_ref, f32[208,128]{1,0:T(8,128)S(1)} %get-tuple-element.58.b0, ...), custom_call_target="tpu_custom_call" | custom-call | tf_op jit(solution)/shard_map/route/pallas_call | solution.py:437
  35.3 3.0 %collective-permute-start.10 = (f32[112,128]{1,0:T(8,128)S(1)}, f32[112,128]{1,0:T(8,128)S(1)}, u32[]{:S(2)}, u32[]{:S(2)}) collective-permute-start(f32[112,128]{1,0:T(8,128)S(1)} %get-tuple-element.64), channel_id=1, source_target_pairs={{0,8},{4,12},{8,0},{12,4},{1,9},{5,13},{9,1},{13,5},{2,10},{6,14},... | collective-permute-start | bytes 172040 | tf_op jit(solution)/shard_map/ppermute | solution.py:441
  38.3 0.4 collective-permute-start.11
  38.7 2.3 %collective-permute-start.9 = (f32[112,128]{1,0:T(8,128)S(1)}, f32[112,128]{1,0:T(8,128)S(1)}, u32[]{:S(2)}, u32[]{:S(2)}) collective-permute-start(f32[112,128]{1,0:T(8,128)S(1)} %get-tuple-element.63), channel_id=1, source_target_pairs={{0,12},{4,0},{8,4},{12,8},{1,13},{5,1},{9,5},{13,9},{2,14},{6,2},{... | collective-permute-start | bytes 172040 | tf_op jit(solution)/shard_map/ppermute | solution.py:441
  41.0 2.1 %solve.1 = (f32[128,128]{1,0:T(8,128)S(1)}, f32[128,128]{1,0:T(8,128)S(1)}) custom-call(f32[16,128]{1,0:T(8,128)S(1)} %get-tuple-element.66.moment_ref), custom_call_target="tpu_custom_call" | custom-call | tf_op jit(solution)/shard_map/solve/pallas_call | solution.py:442
  43.1 0.1 collective-permute-done.11.w1
  43.2 1.3 %scores.1 = (f32[4,48,128]{2,1,0:T(8,128)S(1)}, f32[4,48,128]{2,1,0:T(8,128)S(1)}) custom-call(s32[16]{0:T(128)S(1)} %get-tuple-element.50.source_ref, s32[16]{0:T(128)S(1)} %get-tuple-element.51.rank_ref, f32[112,128]{1,0:T(8,128)S(1)} %get-tuple-element.62.w0, f32[112,128]{1,0:T(8,128)S(1)} %collective-permute-done.9.w3, ...), custom_call_target="tpu_custom_call" | custom-call | tf_op jit(solution)/shard_map/scores/pallas_call | solution.py:443
  44.5 3.4 %collective-permute-start.12 = (f32[4,48,128]{2,1,0:T(8,128)S(1)}, f32[4,48,128]{2,1,0:T(8,128)S(1)}, u32[]{:S(2)}, u32[]{:S(2)}) collective-permute-start(f32[4,48,128]{2,1,0:T(8,128)S(1)} %get-tuple-element.71), channel_id=1, source_target_pairs={{0,16},{16,0},{1,17},{17,1},{2,18},{18,2},{3,19},{19,3},{4,20},{20... | collective-permute-start | bytes 294920 | tf_op jit(solution)/shard_map/ppermute | solution.py:447
  47.9 0.9 %collective-permute-done.12.got_ref = f32[4,48,128]{2,1,0:T(8,128)S(1)} collective-permute-done((f32[4,48,128]{2,1,0:T(8,128)S(1)}, f32[4,48,128]{2,1,0:T(8,128)S(1)}, u32[]{:S(2)}, u32[]{:S(2)}) %collective-permute-start.12) | collective-permute-done | bytes 98336 | tf_op jit(solution)/shard_map/ppermute | solution.py:447
  48.9 0.6 %collective-permute-start.13 = (f32[2,48,128]{2,1,0:T(8,128)S(1)}, f32[2,48,128]{2,1,0:T(8,128)S(1)}, u32[]{:S(2)}, u32[]{:S(2)}) collective-permute-start(f32[2,48,128]{2,1,0:T(8,128)S(1)} %get-tuple-element.73), channel_id=1, source_target_pairs={{0,64},{32,96},{64,0},{96,32},{1,65},{33,97},{65,1},{97,33},{2,66}... | collective-permute-start | bytes 147464 | tf_op jit(solution)/shard_map/ppermute | solution.py:450
  49.5 2.0 %collective-permute-start.14 = (f32[2,48,128]{2,1,0:T(8,128)S(1)}, f32[2,48,128]{2,1,0:T(8,128)S(1)}, u32[]{:S(2)}, u32[]{:S(2)}) collective-permute-start(f32[2,48,128]{2,1,0:T(8,128)S(1)} %get-tuple-element.74), channel_id=1, source_target_pairs={{0,32},{32,64},{64,96},{96,0},{1,33},{33,65},{65,97},{97,1},{2,34}... | collective-permute-start | bytes 147464 | tf_op jit(solution)/shard_map/ppermute | solution.py:450
  51.5 1.0 %collective-permute-start.15 = (f32[2,48,128]{2,1,0:T(8,128)S(1)}, f32[2,48,128]{2,1,0:T(8,128)S(1)}, u32[]{:S(2)}, u32[]{:S(2)}) collective-permute-start(f32[2,48,128]{2,1,0:T(8,128)S(1)} %get-tuple-element.75), channel_id=1, source_target_pairs={{0,96},{32,0},{64,32},{96,64},{1,97},{33,1},{65,33},{97,65},{2,98}... | collective-permute-start | bytes 147464 | tf_op jit(solution)/shard_map/ppermute | solution.py:450
  52.5 0.9 %collective-permute-done.13.p2 = f32[2,48,128]{2,1,0:T(8,128)S(1)} collective-permute-done((f32[2,48,128]{2,1,0:T(8,128)S(1)}, f32[2,48,128]{2,1,0:T(8,128)S(1)}, u32[]{:S(2)}, u32[]{:S(2)}) %collective-permute-start.13) | collective-permute-done | bytes 49184 | tf_op jit(solution)/shard_map/ppermute | solution.py:450
  53.4 1.6 %collective-permute-done.14.p1 = f32[2,48,128]{2,1,0:T(8,128)S(1)} collective-permute-done((f32[2,48,128]{2,1,0:T(8,128)S(1)}, f32[2,48,128]{2,1,0:T(8,128)S(1)}, u32[]{:S(2)}, u32[]{:S(2)}) %collective-permute-start.14) | collective-permute-done | bytes 49184 | tf_op jit(solution)/shard_map/ppermute | solution.py:450
  55.0 1.1 %finish.1 = (f32[2,128,128]{2,1,0:T(8,128)}, f32[8,8]{1,0:T(8,128)}, f32[1,8]{1,0:T(1,128)}) custom-call(s32[16,128]{1,0:T(8,128)S(1)} %get-tuple-element.49.genes_ref, f32[2,48,128]{2,1,0:T(8,128)S(1)} %get-tuple-element.72.p0, f32[2,48,128]{2,1,0:T(8,128)S(1)} %collective-permute-done.13.p2, f32[2,48,128]{2,1,0:T(8,128)S(1)} %collective-permute-done.14.p1, ...), custom_call_target="tpu_custom_call" | custom-call | tf_op jit(solution)/shard_map/finish/pallas_call | solution.py:451
  (17 shorter events, 0.2 us)
Async XLA Ops:
  0.6 18.0 %copy-start.2 = (s32[256]{0:T(256)S(1)}, s32[256]{0:T(256)}, u32[]{:S(2)}) copy-start(s32[256]{0:T(256)} %owner_ref.1) | copy-start | bytes 3076
  0.6 18.0 %copy-start = (f32[32768]{0:T(1024)S(1)}, f32[32768]{0:T(1024)}, u32[]{:S(2)}) copy-start(f32[32768]{0:T(1024)} %param.11) | copy-start | bytes 393220
  0.7 18.0 %copy-start.1 = (s32[32768]{0:T(1024)S(1)}, s32[32768]{0:T(1024)}, u32[]{:S(2)}) copy-start(s32[32768]{0:T(1024)} %param.13) | copy-start | bytes 393220
  6.8 3.8 %collective-permute-start = (f32[4,4,128,128]{3,2,1,0:T(8,128)S(1)}, f32[4,4,128,128]{3,2,1,0:T(8,128)S(1)}, u32[]{:S(2)}, u32[]{:S(2)}) collective-permute-start(f32[4,4,128,128]{3,2,1,0:T(8,128)S(1)} %get-tuple-element.42), channel_id=1, source_target_pairs={{0,16},{16,0},{1,17},{17,1},{2,18},{18,2},{3,19},{19,3},{4,20},{20... | collective-permute-start | bytes 3145736 | tf_op jit(solution)/shard_map/ppermute | solution.py:408
  9.0 2.5 %collective-permute-start.1 = (f32[4,4,80,128]{3,2,1,0:T(8,128)S(1)}, f32[4,4,80,128]{3,2,1,0:T(8,128)S(1)}, u32[]{:S(2)}, u32[]{:S(2)}) collective-permute-start(f32[4,4,80,128]{3,2,1,0:T(8,128)S(1)} %get-tuple-element.47), channel_id=1, source_target_pairs={{0,16},{16,0},{1,17},{17,1},{2,18},{18,2},{3,19},{19,3},{4,20},{20... | collective-permute-start | bytes 1966088 | tf_op jit(solution)/shard_map/ppermute | solution.py:412
  11.7 15.2 %collective-permute-start.4 = (f32[4,208,128]{2,1,0:T(8,128)S(1)}, f32[4,208,128]{2,1,0:T(8,128)S(1)}, u32[]{:S(2)}, u32[]{:S(2)}) collective-permute-start(f32[4,208,128]{2,1,0:T(8,128)S(1)} %get-tuple-element.55), channel_id=1, source_target_pairs={{0,32},{1,33},{2,34},{3,35},{4,36},{5,37},{6,38},{7,39},{8,40},{9,... | collective-permute-start | bytes 1277960 | tf_op jit(solution)/shard_map/ppermute | solution.py:420
  13.5 13.4 %collective-permute-start.5 = (f32[4,208,128]{2,1,0:T(8,128)S(1)}, f32[4,208,128]{2,1,0:T(8,128)S(1)}, u32[]{:S(2)}, u32[]{:S(2)}) collective-permute-start(f32[4,208,128]{2,1,0:T(8,128)S(1)} %get-tuple-element.56), channel_id=1, source_target_pairs={{0,96},{1,97},{2,98},{3,99},{4,100},{5,101},{6,102},{7,103},{8,104... | collective-permute-start | bytes 1277960 | tf_op jit(solution)/shard_map/ppermute | solution.py:421
  15.7 11.2 %collective-permute-start.2 = (f32[4,128,128]{2,1,0:T(8,128)S(1)}, f32[4,128,128]{2,1,0:T(8,128)S(1)}, u32[]{:S(2)}, u32[]{:S(2)}) collective-permute-start(f32[4,128,128]{2,1,0:T(8,128)S(1)} %far_sum.1._), channel_id=1, source_target_pairs={{0,64},{1,65},{2,66},{3,67},{4,68},{5,69},{6,70},{7,71},{8,72},{9,... | collective-permute-start | bytes 786440 | tf_op jit(solution)/shard_map/ppermute | solution.py:415
  16.9 10.0 %collective-permute-start.3 = (f32[4,80,128]{2,1,0:T(8,128)S(1)}, f32[4,80,128]{2,1,0:T(8,128)S(1)}, u32[]{:S(2)}, u32[]{:S(2)}) collective-permute-start(f32[4,80,128]{2,1,0:T(8,128)S(1)} %get-tuple-element.54), channel_id=1, source_target_pairs={{0,64},{1,65},{2,66},{3,67},{4,68},{5,69},{6,70},{7,71},{8,72},{9,... | collective-permute-start | bytes 491528 | tf_op jit(solution)/shard_map/ppermute | solution.py:422
  27.0 5.5 %collective-permute-start.6 = (f32[208,128]{1,0:T(8,128)S(1)}, f32[208,128]{1,0:T(8,128)S(1)}, u32[]{:S(2)}, u32[]{:S(2)}) collective-permute-start(f32[208,128]{1,0:T(8,128)S(1)} %get-tuple-element.59), channel_id=1, source_target_pairs={{0,2},{1,3},{2,0},{3,1},{4,6},{5,7},{6,4},{7,5},{8,10},{9,11},{10,... | collective-permute-start | bytes 319496 | tf_op jit(solution)/shard_map/ppermute | solution.py:435
  29.8 4.8 %collective-permute-start.7 = (f32[208,128]{1,0:T(8,128)S(1)}, f32[208,128]{1,0:T(8,128)S(1)}, u32[]{:S(2)}, u32[]{:S(2)}) collective-permute-start(f32[208,128]{1,0:T(8,128)S(1)} %get-tuple-element.60), channel_id=1, source_target_pairs={{0,1},{1,2},{2,3},{3,0},{4,5},{5,6},{6,7},{7,4},{8,9},{9,10},{10,1... | collective-permute-start | bytes 319496 | tf_op jit(solution)/shard_map/ppermute | solution.py:435
  30.1 4.5 %collective-permute-start.8 = (f32[208,128]{1,0:T(8,128)S(1)}, f32[208,128]{1,0:T(8,128)S(1)}, u32[]{:S(2)}, u32[]{:S(2)}) collective-permute-start(f32[208,128]{1,0:T(8,128)S(1)} %get-tuple-element.61), channel_id=1, source_target_pairs={{0,3},{1,0},{2,1},{3,2},{4,7},{5,4},{6,5},{7,6},{8,11},{9,8},{10,9... | collective-permute-start | bytes 319496 | tf_op jit(solution)/shard_map/ppermute | solution.py:435
  35.3 7.8 %collective-permute-start.10 = (f32[112,128]{1,0:T(8,128)S(1)}, f32[112,128]{1,0:T(8,128)S(1)}, u32[]{:S(2)}, u32[]{:S(2)}) collective-permute-start(f32[112,128]{1,0:T(8,128)S(1)} %get-tuple-element.64), channel_id=1, source_target_pairs={{0,8},{4,12},{8,0},{12,4},{1,9},{5,13},{9,1},{13,5},{2,10},{6,14},... | collective-permute-start | bytes 172040 | tf_op jit(solution)/shard_map/ppermute | solution.py:441
  38.3 4.9 %collective-permute-start.11 = (f32[112,128]{1,0:T(8,128)S(1)}, f32[112,128]{1,0:T(8,128)S(1)}, u32[]{:S(2)}, u32[]{:S(2)}) collective-permute-start(f32[112,128]{1,0:T(8,128)S(1)} %get-tuple-element.65), channel_id=1, source_target_pairs={{0,4},{4,8},{8,12},{12,0},{1,5},{5,9},{9,13},{13,1},{2,6},{6,10},{... | collective-permute-start | bytes 172040 | tf_op jit(solution)/shard_map/ppermute | solution.py:441
  38.7 4.5 %collective-permute-start.9 = (f32[112,128]{1,0:T(8,128)S(1)}, f32[112,128]{1,0:T(8,128)S(1)}, u32[]{:S(2)}, u32[]{:S(2)}) collective-permute-start(f32[112,128]{1,0:T(8,128)S(1)} %get-tuple-element.63), channel_id=1, source_target_pairs={{0,12},{4,0},{8,4},{12,8},{1,13},{5,1},{9,5},{13,9},{2,14},{6,2},{... | collective-permute-start | bytes 172040 | tf_op jit(solution)/shard_map/ppermute | solution.py:441
  44.5 4.3 %collective-permute-start.12 = (f32[4,48,128]{2,1,0:T(8,128)S(1)}, f32[4,48,128]{2,1,0:T(8,128)S(1)}, u32[]{:S(2)}, u32[]{:S(2)}) collective-permute-start(f32[4,48,128]{2,1,0:T(8,128)S(1)} %get-tuple-element.71), channel_id=1, source_target_pairs={{0,16},{16,0},{1,17},{17,1},{2,18},{18,2},{3,19},{19,3},{4,20},{20... | collective-permute-start | bytes 294920 | tf_op jit(solution)/shard_map/ppermute | solution.py:447
  48.9 4.5 %collective-permute-start.13 = (f32[2,48,128]{2,1,0:T(8,128)S(1)}, f32[2,48,128]{2,1,0:T(8,128)S(1)}, u32[]{:S(2)}, u32[]{:S(2)}) collective-permute-start(f32[2,48,128]{2,1,0:T(8,128)S(1)} %get-tuple-element.73), channel_id=1, source_target_pairs={{0,64},{32,96},{64,0},{96,32},{1,65},{33,97},{65,1},{97,33},{2,66}... | collective-permute-start | bytes 147464 | tf_op jit(solution)/shard_map/ppermute | solution.py:450
  49.5 5.5 %collective-permute-start.14 = (f32[2,48,128]{2,1,0:T(8,128)S(1)}, f32[2,48,128]{2,1,0:T(8,128)S(1)}, u32[]{:S(2)}, u32[]{:S(2)}) collective-permute-start(f32[2,48,128]{2,1,0:T(8,128)S(1)} %get-tuple-element.74), channel_id=1, source_target_pairs={{0,32},{32,64},{64,96},{96,0},{1,33},{33,65},{65,97},{97,1},{2,34}... | collective-permute-start | bytes 147464 | tf_op jit(solution)/shard_map/ppermute | solution.py:450
  51.5 3.5 %collective-permute-start.15 = (f32[2,48,128]{2,1,0:T(8,128)S(1)}, f32[2,48,128]{2,1,0:T(8,128)S(1)}, u32[]{:S(2)}, u32[]{:S(2)}) collective-permute-start(f32[2,48,128]{2,1,0:T(8,128)S(1)} %get-tuple-element.75), channel_id=1, source_target_pairs={{0,96},{32,0},{64,32},{96,64},{1,97},{33,1},{65,33},{97,65},{2,98}... | collective-permute-start | bytes 147464 | tf_op jit(solution)/shard_map/ppermute | solution.py:450

commit v5 on v4

--- a/solution.py
+++ b/solution.py
@@ -319,8 +319,9 @@
                                precision=HIGHEST, preferred_element_type=F32)
     row, col = iota((WIDTH, WIDTH), 0), iota((WIDTH, WIDTH), 1)
     ones = jnp.where(col == (row >> 5) + 16, 1.0, 0.0)
-    taken = (jnp.dot(whitened, half_ref[...], precision=HIGHEST, preferred_element_type=F32)
-             + jnp.dot(whitened * whitened, ones, precision=HIGHEST, preferred_element_type=F32))
+    taken = jnp.dot(jnp.concatenate([whitened, whitened * whitened], 1),
+                    jnp.concatenate([half_ref[...], ones], 0), precision=HIGHEST,
+                    preferred_element_type=F32)
     for group in range(4):
         rest = rest - pltpu.roll(taken[group * 16:group * 16 + 16], 4 * group, 1)
     scale = scale_ref[...]
@@ -370,15 +371,13 @@
 
     row8 = iota((8, WIDTH), 0)
     member = jnp.where(genes_ref[...] == iota((16, WIDTH), 1), 1.0, 0.0)
-    none = jnp.zeros((16, WIDTH), F32)
-    rest_of = jnp.zeros((WIDTH - 32, WIDTH), F32)
+    member = jnp.concatenate(
+        [member, pltpu.roll(member, 8, 1), jnp.zeros((WIDTH - 32, WIDTH), F32)], 0)
     squares = jnp.sum(rest * rest, axis=0, keepdims=True)
     sums = jnp.sum(rest, axis=0, keepdims=True)
     table = jnp.where(row8 == 0, squares, sums)
-    by_gene = jnp.dot(table, jnp.concatenate([member, none, rest_of], 0), precision=HIGHEST,
-                      preferred_element_type=F32)[:, :8]
-    traces = jnp.dot(table, jnp.concatenate([none, member, rest_of], 0), precision=HIGHEST,
-                     preferred_element_type=F32)[:, :8]
+    totals = jnp.dot(table, member, precision=HIGHEST, preferred_element_type=F32)
+    by_gene, traces = totals[:, :8], totals[:, 8:16]
     level = iota((8, 8), 0)
     rho = jnp.zeros((8, 8), F32)
     for i, value in enumerate(RHO_GRID):

time: 56.4 us -> 56.3 us (level)
  no operation moved by 1% of the time
where the time goes in v5:
time: 56.3 us; the launch traced here: 56 us
  starting transfers between devices  26.7 us (47%)
  Pallas kernels  14.5 us (26%)
  waiting for transfers between devices  14.1 us (25%)
  between operations  0.73 us (1%)
    pallas_call x1, Pallas kernels, products(): pl.pallas_call(products_kernel, out_shape=tuple((jax.ShapeDtypeStruct(sha...  6.12 us
    ppermute x1, waiting for transfers between devices, shards(): c2 = lax.ppermute(far_cross, AXES, turns(2, True))  6.05 us
    ppermute x3, starting transfers between devices, shards(): lax.ppermute(e[d], 'g', [(i, (i + d) % 4) for i in range(4)])  5.67 us
    ppermute x3, starting transfers between devices, shards(): q = {d: lax.ppermute(b[d], AXES, turns(d, False)) for d in (2, 1, 3)}  5.5 us
    ppermute x3, starting transfers between devices, shards(): lax.ppermute(p[d], 'x', [(i, (i + d) % 4) for i in range(4)])  3.62 us
    ppermute x1, starting transfers between devices, shards(): got = lax.ppermute(theirs, 'k', other)  3.38 us
    ppermute x3, waiting for transfers between devices, shards(): lax.ppermute(p[d], 'x', [(i, (i + d) % 4) for i in range(4)])  2.5 us
    ppermute x1, starting transfers between devices, shards(): a3 = lax.ppermute(a3, AXES, turns(3, True))  2.2 us
  transfers between devices with their start and end apart: 16, of which 8 were waited for; matrix products, arithmetic and copies ran while one was open for 0% of the time, Pallas kernels for 9%

profile of v5, /device:TPU:1, one launch (start us, length us, event | category | flops | bytes accessed | tf_op | source)
XLA Modules:
  0.0 56.0 jit_solution(6658457536333858976)
XLA Ops:
  0.7 6.1 %products.1 = (f32[4,4,128,128]{3,2,1,0:T(8,128)S(1)}, f32[4,4,128,128]{3,2,1,0:T(8,128)S(1)}, f32[4,512,128]{2,1,0:T(8,128)S(1)}, f32[4,128,128]{2,1,0:T(8,128)S(1)}, f32[16,128]{1,0:T(8,128)S(1)}) custom-call(s32[256]{0:T(256)} %owner_ref.1, bf16[512,8192]{1,0:T(8,128)(2,1)} %dosage_ref.1, bf16[32,512]{1,0:T(8,128)(2,1)} %bitcast.9, ...), custom_call_target="tpu_custom_call" | custom-call | tf_op jit(solution)/shard_map/products/pallas_call | solution.py:141
  6.8 1.5 %collective-permute-start = (f32[4,4,128,128]{3,2,1,0:T(8,128)S(1)}, f32[4,4,128,128]{3,2,1,0:T(8,128)S(1)}, u32[]{:S(2)}, u32[]{:S(2)}) collective-permute-start(f32[4,4,128,128]{3,2,1,0:T(8,128)S(1)} %get-tuple-element.42), channel_id=1, source_target_pairs={{0,16},{16,0},{1,17},{17,1},{2,18},{18,2},{3,19},{19,3},{4,20},{20... | collective-permute-start | bytes 3145736 | tf_op jit(solution)/shard_map/ppermute | solution.py:407
  8.3 0.7 %cross.1 = (f32[4,4,80,128]{3,2,1,0:T(8,128)S(1)}, f32[4,4,80,128]{3,2,1,0:T(8,128)S(1)}) custom-call(f32[4,512,128]{2,1,0:T(8,128)S(1)} %get-tuple-element.43.cross_ref, f32[4,128,128]{2,1,0:T(8,128)S(1)} %get-tuple-element.44.rest_ref, f32[16,128]{1,0:T(8,128)S(1)} %get-tuple-element.45.moment_ref), custom_call_target="tpu_custom_call" | custom-call | tf_op jit(solution)/shard_map/cross/pallas_call | solution.py:408
  9.1 1.4 %collective-permute-done.recv_ref = f32[4,4,128,128]{3,2,1,0:T(8,128)S(1)} collective-permute-done((f32[4,4,128,128]{3,2,1,0:T(8,128)S(1)}, f32[4,4,128,128]{3,2,1,0:T(8,128)S(1)}, u32[]{:S(2)}, u32[]{:S(2)}) %collective-permute-start) | collective-permute-done | bytes 1048608 | tf_op jit(solution)/shard_map/ppermute | solution.py:407
  10.6 0.9 %collective-permute-done.1.recv_cross_ref = f32[4,4,80,128]{3,2,1,0:T(8,128)S(1)} collective-permute-done((f32[4,4,80,128]{3,2,1,0:T(8,128)S(1)}, f32[4,4,80,128]{3,2,1,0:T(8,128)S(1)}, u32[]{:S(2)}, u32[]{:S(2)}) %collective-permute-start.1) | collective-permute-done | bytes 655392 | tf_op jit(solution)/shard_map/ppermute | solution.py:411
  11.5 0.2 near_sum.1
  11.7 1.8 %collective-permute-start.4 = (f32[4,208,128]{2,1,0:T(8,128)S(1)}, f32[4,208,128]{2,1,0:T(8,128)S(1)}, u32[]{:S(2)}, u32[]{:S(2)}) collective-permute-start(f32[4,208,128]{2,1,0:T(8,128)S(1)} %get-tuple-element.55), channel_id=1, source_target_pairs={{0,32},{1,33},{2,34},{3,35},{4,36},{5,37},{6,38},{7,39},{8,40},{9,... | collective-permute-start | bytes 1277960 | tf_op jit(solution)/shard_map/ppermute | solution.py:419
  13.5 2.2 %collective-permute-start.5 = (f32[4,208,128]{2,1,0:T(8,128)S(1)}, f32[4,208,128]{2,1,0:T(8,128)S(1)}, u32[]{:S(2)}, u32[]{:S(2)}) collective-permute-start(f32[4,208,128]{2,1,0:T(8,128)S(1)} %get-tuple-element.56), channel_id=1, source_target_pairs={{0,96},{1,97},{2,98},{3,99},{4,100},{5,101},{6,102},{7,103},{8,104... | collective-permute-start | bytes 1277960 | tf_op jit(solution)/shard_map/ppermute | solution.py:420
  15.7 1.2 %collective-permute-start.2 = (f32[4,128,128]{2,1,0:T(8,128)S(1)}, f32[4,128,128]{2,1,0:T(8,128)S(1)}, u32[]{:S(2)}, u32[]{:S(2)}) collective-permute-start(f32[4,128,128]{2,1,0:T(8,128)S(1)} %far_sum.1._), channel_id=1, source_target_pairs={{0,64},{1,65},{2,66},{3,67},{4,68},{5,69},{6,70},{7,71},{8,72},{9,... | collective-permute-start | bytes 786440 | tf_op jit(solution)/shard_map/ppermute | solution.py:414
  16.9 1.7 %collective-permute-start.3 = (f32[4,80,128]{2,1,0:T(8,128)S(1)}, f32[4,80,128]{2,1,0:T(8,128)S(1)}, u32[]{:S(2)}, u32[]{:S(2)}) collective-permute-start(f32[4,80,128]{2,1,0:T(8,128)S(1)} %get-tuple-element.54), channel_id=1, source_target_pairs={{0,64},{1,65},{2,66},{3,67},{4,68},{5,69},{6,70},{7,71},{8,72},{9,... | collective-permute-start | bytes 491528 | tf_op jit(solution)/shard_map/ppermute | solution.py:421
  18.7 2.1 %layout.1 = (s32[16]{0:T(128)S(1)}, s32[16]{0:T(128)S(1)}, s32[16]{0:T(128)S(1)}, s32[16]{0:T(128)S(1)}, s32[16,128]{1,0:T(8,128)S(1)}, /*index=5*/f32[16,128]{1,0:T(8,128)S(1)}, f32[16,128]{1,0:T(8,128)S(1)}) custom-call(s32[256]{0:T(256)S(1)} %copy-done.2, f32[256,128]{1,0:T(8,128)S(1)} %bitcast.7, s32[256,128]{1,0:T(8,128)S(1)} %bitcast.8, ...), custom_call_target="tpu_custom_call" | custom-call | tf_op jit(solution)/shard_map/layout/pallas_call | solution.py:425
  20.8 6.1 %collective-permute-done.3.c2 = f32[4,80,128]{2,1,0:T(8,128)S(1)} collective-permute-done((f32[4,80,128]{2,1,0:T(8,128)S(1)}, f32[4,80,128]{2,1,0:T(8,128)S(1)}, u32[]{:S(2)}, u32[]{:S(2)}) %collective-permute-start.3) | collective-permute-done | bytes 163872 | tf_op jit(solution)/shard_map/ppermute | solution.py:421
  26.9 0.1 second_sum.1
  27.0 2.8 %collective-permute-start.6 = (f32[208,128]{1,0:T(8,128)S(1)}, f32[208,128]{1,0:T(8,128)S(1)}, u32[]{:S(2)}, u32[]{:S(2)}) collective-permute-start(f32[208,128]{1,0:T(8,128)S(1)} %get-tuple-element.59), channel_id=1, source_target_pairs={{0,2},{1,3},{2,0},{3,1},{4,6},{5,7},{6,4},{7,5},{8,10},{9,11},{10,... | collective-permute-start | bytes 319496 | tf_op jit(solution)/shard_map/ppermute | solution.py:434
  29.8 0.3 collective-permute-start.7
  30.1 2.4 %collective-permute-start.8 = (f32[208,128]{1,0:T(8,128)S(1)}, f32[208,128]{1,0:T(8,128)S(1)}, u32[]{:S(2)}, u32[]{:S(2)}) collective-permute-start(f32[208,128]{1,0:T(8,128)S(1)} %get-tuple-element.61), channel_id=1, source_target_pairs={{0,3},{1,0},{2,1},{3,2},{4,7},{5,4},{6,5},{7,6},{8,11},{9,8},{10,9... | collective-permute-start | bytes 319496 | tf_op jit(solution)/shard_map/ppermute | solution.py:434
  32.5 2.1 %collective-permute-done.7.q1 = f32[208,128]{1,0:T(8,128)S(1)} collective-permute-done((f32[208,128]{1,0:T(8,128)S(1)}, f32[208,128]{1,0:T(8,128)S(1)}, u32[]{:S(2)}, u32[]{:S(2)}) %collective-permute-start.7) | collective-permute-done | bytes 106528 | tf_op jit(solution)/shard_map/ppermute | solution.py:434
  34.6 0.7 %route.1 = (f32[112,128]{1,0:T(8,128)S(1)}, f32[112,128]{1,0:T(8,128)S(1)}, f32[112,128]{1,0:T(8,128)S(1)}, f32[112,128]{1,0:T(8,128)S(1)}, f32[16,128]{1,0:T(8,128)S(1)}) custom-call(s32[16]{0:T(128)S(1)} %get-tuple-element.52.turn_ref, s32[16]{0:T(128)S(1)} %get-tuple-element.53.slot_at_ref, f32[208,128]{1,0:T(8,128)S(1)} %get-tuple-element.58.b0, ...), custom_call_target="tpu_custom_call" | custom-call | tf_op jit(solution)/shard_map/route/pallas_call | solution.py:436
  35.3 3.0 %collective-permute-start.10 = (f32[112,128]{1,0:T(8,128)S(1)}, f32[112,128]{1,0:T(8,128)S(1)}, u32[]{:S(2)}, u32[]{:S(2)}) collective-permute-start(f32[112,128]{1,0:T(8,128)S(1)} %get-tuple-element.64), channel_id=1, source_target_pairs={{0,8},{4,12},{8,0},{12,4},{1,9},{5,13},{9,1},{13,5},{2,10},{6,14},... | collective-permute-start | bytes 172040 | tf_op jit(solution)/shard_map/ppermute | solution.py:440
  38.3 0.4 collective-permute-start.11
  38.7 2.3 %collective-permute-start.9 = (f32[112,128]{1,0:T(8,128)S(1)}, f32[112,128]{1,0:T(8,128)S(1)}, u32[]{:S(2)}, u32[]{:S(2)}) collective-permute-start(f32[112,128]{1,0:T(8,128)S(1)} %get-tuple-element.63), channel_id=1, source_target_pairs={{0,12},{4,0},{8,4},{12,8},{1,13},{5,1},{9,5},{13,9},{2,14},{6,2},{... | collective-permute-start | bytes 172040 | tf_op jit(solution)/shard_map/ppermute | solution.py:440
  41.0 2.1 %solve.1 = (f32[128,128]{1,0:T(8,128)S(1)}, f32[128,128]{1,0:T(8,128)S(1)}) custom-call(f32[16,128]{1,0:T(8,128)S(1)} %get-tuple-element.66.moment_ref), custom_call_target="tpu_custom_call" | custom-call | tf_op jit(solution)/shard_map/solve/pallas_call | solution.py:441
  43.1 0.1 collective-permute-done.11.w1
  43.2 1.2 %scores.1 = (f32[4,48,128]{2,1,0:T(8,128)S(1)}, f32[4,48,128]{2,1,0:T(8,128)S(1)}) custom-call(s32[16]{0:T(128)S(1)} %get-tuple-element.50.source_ref, s32[16]{0:T(128)S(1)} %get-tuple-element.51.rank_ref, f32[112,128]{1,0:T(8,128)S(1)} %get-tuple-element.62.w0, f32[112,128]{1,0:T(8,128)S(1)} %collective-permute-done.9.w3, ...), custom_call_target="tpu_custom_call" | custom-call | tf_op jit(solution)/shard_map/scores/pallas_call | solution.py:442
  44.4 3.4 %collective-permute-start.12 = (f32[4,48,128]{2,1,0:T(8,128)S(1)}, f32[4,48,128]{2,1,0:T(8,128)S(1)}, u32[]{:S(2)}, u32[]{:S(2)}) collective-permute-start(f32[4,48,128]{2,1,0:T(8,128)S(1)} %get-tuple-element.71), channel_id=1, source_target_pairs={{0,16},{16,0},{1,17},{17,1},{2,18},{18,2},{3,19},{19,3},{4,20},{20... | collective-permute-start | bytes 294920 | tf_op jit(solution)/shard_map/ppermute | solution.py:446
  47.8 0.9 %collective-permute-done.12.got_ref = f32[4,48,128]{2,1,0:T(8,128)S(1)} collective-permute-done((f32[4,48,128]{2,1,0:T(8,128)S(1)}, f32[4,48,128]{2,1,0:T(8,128)S(1)}, u32[]{:S(2)}, u32[]{:S(2)}) %collective-permute-start.12) | collective-permute-done | bytes 98336 | tf_op jit(solution)/shard_map/ppermute | solution.py:446
  48.8 0.6 %collective-permute-start.13 = (f32[2,48,128]{2,1,0:T(8,128)S(1)}, f32[2,48,128]{2,1,0:T(8,128)S(1)}, u32[]{:S(2)}, u32[]{:S(2)}) collective-permute-start(f32[2,48,128]{2,1,0:T(8,128)S(1)} %get-tuple-element.73), channel_id=1, source_target_pairs={{0,64},{32,96},{64,0},{96,32},{1,65},{33,97},{65,1},{97,33},{2,66}... | collective-permute-start | bytes 147464 | tf_op jit(solution)/shard_map/ppermute | solution.py:449
  49.4 2.0 %collective-permute-start.14 = (f32[2,48,128]{2,1,0:T(8,128)S(1)}, f32[2,48,128]{2,1,0:T(8,128)S(1)}, u32[]{:S(2)}, u32[]{:S(2)}) collective-permute-start(f32[2,48,128]{2,1,0:T(8,128)S(1)} %get-tuple-element.74), channel_id=1, source_target_pairs={{0,32},{32,64},{64,96},{96,0},{1,33},{33,65},{65,97},{97,1},{2,34}... | collective-permute-start | bytes 147464 | tf_op jit(solution)/shard_map/ppermute | solution.py:449
  51.4 1.0 %collective-permute-start.15 = (f32[2,48,128]{2,1,0:T(8,128)S(1)}, f32[2,48,128]{2,1,0:T(8,128)S(1)}, u32[]{:S(2)}, u32[]{:S(2)}) collective-permute-start(f32[2,48,128]{2,1,0:T(8,128)S(1)} %get-tuple-element.75), channel_id=1, source_target_pairs={{0,96},{32,0},{64,32},{96,64},{1,97},{33,1},{65,33},{97,65},{2,98}... | collective-permute-start | bytes 147464 | tf_op jit(solution)/shard_map/ppermute | solution.py:449
  52.4 0.9 %collective-permute-done.13.p2 = f32[2,48,128]{2,1,0:T(8,128)S(1)} collective-permute-done((f32[2,48,128]{2,1,0:T(8,128)S(1)}, f32[2,48,128]{2,1,0:T(8,128)S(1)}, u32[]{:S(2)}, u32[]{:S(2)}) %collective-permute-start.13) | collective-permute-done | bytes 49184 | tf_op jit(solution)/shard_map/ppermute | solution.py:449
  53.3 1.6 %collective-permute-done.14.p1 = f32[2,48,128]{2,1,0:T(8,128)S(1)} collective-permute-done((f32[2,48,128]{2,1,0:T(8,128)S(1)}, f32[2,48,128]{2,1,0:T(8,128)S(1)}, u32[]{:S(2)}, u32[]{:S(2)}) %collective-permute-start.14) | collective-permute-done | bytes 49184 | tf_op jit(solution)/shard_map/ppermute | solution.py:449
  54.9 1.1 %finish.1 = (f32[2,128,128]{2,1,0:T(8,128)}, f32[8,8]{1,0:T(8,128)}, f32[1,8]{1,0:T(1,128)}) custom-call(s32[16,128]{1,0:T(8,128)S(1)} %get-tuple-element.49.genes_ref, f32[2,48,128]{2,1,0:T(8,128)S(1)} %get-tuple-element.72.p0, f32[2,48,128]{2,1,0:T(8,128)S(1)} %collective-permute-done.13.p2, f32[2,48,128]{2,1,0:T(8,128)S(1)} %collective-permute-done.14.p1, ...), custom_call_target="tpu_custom_call" | custom-call | tf_op jit(solution)/shard_map/finish/pallas_call | solution.py:450
  (17 shorter events, 0.2 us)
Async XLA Ops:
  0.6 18.0 %copy-start.2 = (s32[256]{0:T(256)S(1)}, s32[256]{0:T(256)}, u32[]{:S(2)}) copy-start(s32[256]{0:T(256)} %owner_ref.1) | copy-start | bytes 3076
  0.6 18.0 %copy-start = (f32[32768]{0:T(1024)S(1)}, f32[32768]{0:T(1024)}, u32[]{:S(2)}) copy-start(f32[32768]{0:T(1024)} %param.11) | copy-start | bytes 393220
  0.7 18.0 %copy-start.1 = (s32[32768]{0:T(1024)S(1)}, s32[32768]{0:T(1024)}, u32[]{:S(2)}) copy-start(s32[32768]{0:T(1024)} %param.13) | copy-start | bytes 393220
  6.8 3.8 %collective-permute-start = (f32[4,4,128,128]{3,2,1,0:T(8,128)S(1)}, f32[4,4,128,128]{3,2,1,0:T(8,128)S(1)}, u32[]{:S(2)}, u32[]{:S(2)}) collective-permute-start(f32[4,4,128,128]{3,2,1,0:T(8,128)S(1)} %get-tuple-element.42), channel_id=1, source_target_pairs={{0,16},{16,0},{1,17},{17,1},{2,18},{18,2},{3,19},{19,3},{4,20},{20... | collective-permute-start | bytes 3145736 | tf_op jit(solution)/shard_map/ppermute | solution.py:407
  9.0 2.5 %collective-permute-start.1 = (f32[4,4,80,128]{3,2,1,0:T(8,128)S(1)}, f32[4,4,80,128]{3,2,1,0:T(8,128)S(1)}, u32[]{:S(2)}, u32[]{:S(2)}) collective-permute-start(f32[4,4,80,128]{3,2,1,0:T(8,128)S(1)} %get-tuple-element.47), channel_id=1, source_target_pairs={{0,16},{16,0},{1,17},{17,1},{2,18},{18,2},{3,19},{19,3},{4,20},{20... | collective-permute-start | bytes 1966088 | tf_op jit(solution)/shard_map/ppermute | solution.py:411
  11.7 15.2 %collective-permute-start.4 = (f32[4,208,128]{2,1,0:T(8,128)S(1)}, f32[4,208,128]{2,1,0:T(8,128)S(1)}, u32[]{:S(2)}, u32[]{:S(2)}) collective-permute-start(f32[4,208,128]{2,1,0:T(8,128)S(1)} %get-tuple-element.55), channel_id=1, source_target_pairs={{0,32},{1,33},{2,34},{3,35},{4,36},{5,37},{6,38},{7,39},{8,40},{9,... | collective-permute-start | bytes 1277960 | tf_op jit(solution)/shard_map/ppermute | solution.py:419
  13.5 13.4 %collective-permute-start.5 = (f32[4,208,128]{2,1,0:T(8,128)S(1)}, f32[4,208,128]{2,1,0:T(8,128)S(1)}, u32[]{:S(2)}, u32[]{:S(2)}) collective-permute-start(f32[4,208,128]{2,1,0:T(8,128)S(1)} %get-tuple-element.56), channel_id=1, source_target_pairs={{0,96},{1,97},{2,98},{3,99},{4,100},{5,101},{6,102},{7,103},{8,104... | collective-permute-start | bytes 1277960 | tf_op jit(solution)/shard_map/ppermute | solution.py:420
  15.7 11.2 %collective-permute-start.2 = (f32[4,128,128]{2,1,0:T(8,128)S(1)}, f32[4,128,128]{2,1,0:T(8,128)S(1)}, u32[]{:S(2)}, u32[]{:S(2)}) collective-permute-start(f32[4,128,128]{2,1,0:T(8,128)S(1)} %far_sum.1._), channel_id=1, source_target_pairs={{0,64},{1,65},{2,66},{3,67},{4,68},{5,69},{6,70},{7,71},{8,72},{9,... | collective-permute-start | bytes 786440 | tf_op jit(solution)/shard_map/ppermute | solution.py:414
  16.9 10.0 %collective-permute-start.3 = (f32[4,80,128]{2,1,0:T(8,128)S(1)}, f32[4,80,128]{2,1,0:T(8,128)S(1)}, u32[]{:S(2)}, u32[]{:S(2)}) collective-permute-start(f32[4,80,128]{2,1,0:T(8,128)S(1)} %get-tuple-element.54), channel_id=1, source_target_pairs={{0,64},{1,65},{2,66},{3,67},{4,68},{5,69},{6,70},{7,71},{8,72},{9,... | collective-permute-start | bytes 491528 | tf_op jit(solution)/shard_map/ppermute | solution.py:421
  27.0 5.5 %collective-permute-start.6 = (f32[208,128]{1,0:T(8,128)S(1)}, f32[208,128]{1,0:T(8,128)S(1)}, u32[]{:S(2)}, u32[]{:S(2)}) collective-permute-start(f32[208,128]{1,0:T(8,128)S(1)} %get-tuple-element.59), channel_id=1, source_target_pairs={{0,2},{1,3},{2,0},{3,1},{4,6},{5,7},{6,4},{7,5},{8,10},{9,11},{10,... | collective-permute-start | bytes 319496 | tf_op jit(solution)/shard_map/ppermute | solution.py:434
  29.8 4.8 %collective-permute-start.7 = (f32[208,128]{1,0:T(8,128)S(1)}, f32[208,128]{1,0:T(8,128)S(1)}, u32[]{:S(2)}, u32[]{:S(2)}) collective-permute-start(f32[208,128]{1,0:T(8,128)S(1)} %get-tuple-element.60), channel_id=1, source_target_pairs={{0,1},{1,2},{2,3},{3,0},{4,5},{5,6},{6,7},{7,4},{8,9},{9,10},{10,1... | collective-permute-start | bytes 319496 | tf_op jit(solution)/shard_map/ppermute | solution.py:434
  30.1 4.5 %collective-permute-start.8 = (f32[208,128]{1,0:T(8,128)S(1)}, f32[208,128]{1,0:T(8,128)S(1)}, u32[]{:S(2)}, u32[]{:S(2)}) collective-permute-start(f32[208,128]{1,0:T(8,128)S(1)} %get-tuple-element.61), channel_id=1, source_target_pairs={{0,3},{1,0},{2,1},{3,2},{4,7},{5,4},{6,5},{7,6},{8,11},{9,8},{10,9... | collective-permute-start | bytes 319496 | tf_op jit(solution)/shard_map/ppermute | solution.py:434
  35.3 7.8 %collective-permute-start.10 = (f32[112,128]{1,0:T(8,128)S(1)}, f32[112,128]{1,0:T(8,128)S(1)}, u32[]{:S(2)}, u32[]{:S(2)}) collective-permute-start(f32[112,128]{1,0:T(8,128)S(1)} %get-tuple-element.64), channel_id=1, source_target_pairs={{0,8},{4,12},{8,0},{12,4},{1,9},{5,13},{9,1},{13,5},{2,10},{6,14},... | collective-permute-start | bytes 172040 | tf_op jit(solution)/shard_map/ppermute | solution.py:440
  38.3 4.9 %collective-permute-start.11 = (f32[112,128]{1,0:T(8,128)S(1)}, f32[112,128]{1,0:T(8,128)S(1)}, u32[]{:S(2)}, u32[]{:S(2)}) collective-permute-start(f32[112,128]{1,0:T(8,128)S(1)} %get-tuple-element.65), channel_id=1, source_target_pairs={{0,4},{4,8},{8,12},{12,0},{1,5},{5,9},{9,13},{13,1},{2,6},{6,10},{... | collective-permute-start | bytes 172040 | tf_op jit(solution)/shard_map/ppermute | solution.py:440
  38.7 4.5 %collective-permute-start.9 = (f32[112,128]{1,0:T(8,128)S(1)}, f32[112,128]{1,0:T(8,128)S(1)}, u32[]{:S(2)}, u32[]{:S(2)}) collective-permute-start(f32[112,128]{1,0:T(8,128)S(1)} %get-tuple-element.63), channel_id=1, source_target_pairs={{0,12},{4,0},{8,4},{12,8},{1,13},{5,1},{9,5},{13,9},{2,14},{6,2},{... | collective-permute-start | bytes 172040 | tf_op jit(solution)/shard_map/ppermute | solution.py:440
  44.4 4.3 %collective-permute-start.12 = (f32[4,48,128]{2,1,0:T(8,128)S(1)}, f32[4,48,128]{2,1,0:T(8,128)S(1)}, u32[]{:S(2)}, u32[]{:S(2)}) collective-permute-start(f32[4,48,128]{2,1,0:T(8,128)S(1)} %get-tuple-element.71), channel_id=1, source_target_pairs={{0,16},{16,0},{1,17},{17,1},{2,18},{18,2},{3,19},{19,3},{4,20},{20... | collective-permute-start | bytes 294920 | tf_op jit(solution)/shard_map/ppermute | solution.py:446
  48.8 4.5 %collective-permute-start.13 = (f32[2,48,128]{2,1,0:T(8,128)S(1)}, f32[2,48,128]{2,1,0:T(8,128)S(1)}, u32[]{:S(2)}, u32[]{:S(2)}) collective-permute-start(f32[2,48,128]{2,1,0:T(8,128)S(1)} %get-tuple-element.73), channel_id=1, source_target_pairs={{0,64},{32,96},{64,0},{96,32},{1,65},{33,97},{65,1},{97,33},{2,66}... | collective-permute-start | bytes 147464 | tf_op jit(solution)/shard_map/ppermute | solution.py:449
  49.4 5.5 %collective-permute-start.14 = (f32[2,48,128]{2,1,0:T(8,128)S(1)}, f32[2,48,128]{2,1,0:T(8,128)S(1)}, u32[]{:S(2)}, u32[]{:S(2)}) collective-permute-start(f32[2,48,128]{2,1,0:T(8,128)S(1)} %get-tuple-element.74), channel_id=1, source_target_pairs={{0,32},{32,64},{64,96},{96,0},{1,33},{33,65},{65,97},{97,1},{2,34}... | collective-permute-start | bytes 147464 | tf_op jit(solution)/shard_map/ppermute | solution.py:449
  51.4 3.5 %collective-permute-start.15 = (f32[2,48,128]{2,1,0:T(8,128)S(1)}, f32[2,48,128]{2,1,0:T(8,128)S(1)}, u32[]{:S(2)}, u32[]{:S(2)}) collective-permute-start(f32[2,48,128]{2,1,0:T(8,128)S(1)} %get-tuple-element.75), channel_id=1, source_target_pairs={{0,96},{32,0},{64,32},{96,64},{1,97},{33,1},{65,33},{97,65},{2,98}... | collective-permute-start | bytes 147464 | tf_op jit(solution)/shard_map/ppermute | solution.py:449
